TPU v7x, 256 devices: a whole 4x4x8 slice. The times are simulated.
256 devices in a mesh: dp: 64 (over z, y, core), section: 4 (over x).
Axes of the slice: x: 4, y: 4, z: 8, core: 2. Of those that a mesh axis runs over, the one named last changes fastest.
Arguments:
- hidden_in: bfloat16 [4, 2, 64, 4096], P('section', None, 'dp'), may hold values from -48 to 48
- grad_out: bfloat16 [2, 64, 4096], P(None, 'dp'), may hold values from -6 to 6
- weight_gate: bfloat16 [4, 14336, 4096], P('section', 'dp'), may hold values from -0.09375 to 0.09375
- weight_up: bfloat16 [4, 14336, 4096], P('section', 'dp'), may hold values from -0.09375 to 0.09375
- weight_down: bfloat16 [4, 14336, 4096], P('section', 'dp'), may hold values from -0.046875 to 0.046875
- gain: float32 [4, 4096], P('section'), may hold values from 0.5 to 1.5
- counts: int32 [2], replicated, may hold values from 1 to 64, 85 in all
Outputs:
- grad_inputs: bfloat16 [4, 2, 64, 4096], P('section', None, 'dp')
- gate_grads: bfloat16 [4, 14336, 4096], P('section', 'dp')
- up_grads: bfloat16 [4, 14336, 4096], P('section', 'dp')
- down_grads: bfloat16 [4, 14336, 4096], P('section', 'dp')
- gain_grads: float32 [4, 4096], P('section')
Inputs may be any that keep to these rules, and one draw needn't show every extreme that they name: The 2 counts sum to 85.
All inputs are finite; a program needn't handle non-finite values.
Results may differ from a plain program's by a relative error of at most 0.012.
Values may be sent and summed in bfloat16 or wider, within the bound.
No kernel may reach another device: no remote copies, remote signals or barrier semaphores. Data moves between devices by JAX's collectives and lax.ppermute only.
A program may use at most 128 MiB of HBM per device.

v0:
```python
import jax
import jax.numpy as jnp
from jax import lax
from jax.sharding import PartitionSpec as P


def from_behind(x, axis, by):
    size = lax.axis_size(axis)
    pairs = [(i, i + by) for i in range(size) if 0 <= i + by < size]
    return lax.ppermute(x, axis, pairs)


def norm_rows(layer_rows, gain_row):
    row_values = layer_rows.astype(jnp.float32)
    inv_rms = lax.rsqrt(jnp.mean(row_values * row_values, axis=-1, keepdims=True) + 1e-05)
    normed_rows = (row_values * inv_rms * gain_row).astype(jnp.bfloat16)
    return (inv_rms, normed_rows)


def unit_grads(upstream, gate_pre, up_pre, down_mat):
    sigmoid_pre = jax.nn.sigmoid(gate_pre)
    silu_pre = gate_pre * sigmoid_pre
    activation = (silu_pre * up_pre).astype(jnp.bfloat16)
    grad_act = lax.dot_general(
        upstream, down_mat, (((1,), (1,)), ((), ())), preferred_element_type=jnp.float32
    )
    grad_gate = (grad_act * up_pre * sigmoid_pre * (1.0 + gate_pre * (1.0 - sigmoid_pre))).astype(
        jnp.bfloat16
    )
    grad_up = (grad_act * silu_pre).astype(jnp.bfloat16)
    return (activation, grad_gate, grad_up)


def norm_back(layer_rows, inv_rms, upstream, grad_normed, gain_row):
    row_values = layer_rows.astype(jnp.float32)
    gained_grad = gain_row * grad_normed
    inner_sum = jnp.sum(gained_grad * row_values, axis=-1, keepdims=True)
    feature_count = row_values.shape[-1]
    grad_rows = (
        upstream.astype(jnp.float32)
        + inv_rms * gained_grad
        - row_values * inv_rms**3 * inner_sum / feature_count
    )
    return grad_rows.astype(jnp.bfloat16)


def transposed_product(left_rows, right_rows):
    return lax.dot_general(
        left_rows, right_rows, (((0,), (0,)), ((), ())), preferred_element_type=jnp.float32
    )


def pick_block(stacked, index_value):
    return lax.dynamic_index_in_dim(stacked, index_value, 0, keepdims=False)


def on_device(hidden_in, grad_out, weight_gate, weight_up, weight_down, gain, counts):
    section_count = lax.axis_size("section")
    section_pos = lax.axis_index("section")
    dp_pos = lax.axis_index("dp")
    layer_rows = hidden_in[0]
    gate_mat = weight_gate[0]
    up_mat = weight_up[0]
    down_mat = weight_down[0]
    gain_row = gain[0]
    batch_count, slot_local, feature_count = layer_rows.shape
    unit_count = gate_mat.shape[0]
    full_slots = slot_local * lax.axis_size("dp")
    slot_ids = dp_pos * slot_local + jnp.arange(slot_local)
    live_slots = slot_ids[None, :] < counts[:, None]
    top_local = jnp.where(live_slots[:, :, None], grad_out, jnp.zeros((), jnp.bfloat16))
    is_last = section_pos == section_count - 1
    top_whole = lax.all_gather(top_local, "dp", axis=1, tiled=True)
    received = jnp.zeros((full_slots, feature_count), jnp.bfloat16)
    gathered_all = lax.all_gather(layer_rows, "dp", axis=1, tiled=True)
    all_inv, all_normed = norm_rows(gathered_all, gain_row)
    all_gate = jnp.einsum("mpd,fd->mpf", all_normed, gate_mat, preferred_element_type=jnp.float32)
    all_up = jnp.einsum("mpd,fd->mpf", all_normed, up_mat, preferred_element_type=jnp.float32)
    grad_store = jnp.zeros_like(layer_rows)
    gate_total = jnp.zeros((unit_count, feature_count), jnp.float32)
    up_total = jnp.zeros((unit_count, feature_count), jnp.float32)
    down_total = jnp.zeros((unit_count, feature_count), jnp.float32)
    gain_total = jnp.zeros((feature_count,), jnp.float32)
    last_step = batch_count + section_count - 2
    for step_index in range(batch_count + section_count - 1):
        micro_index = step_index - (section_count - 1 - section_pos)
        is_valid = (micro_index >= 0) & (micro_index < batch_count)
        clamped = jnp.clip(micro_index, 0, batch_count - 1)
        gathered = pick_block(gathered_all, clamped)
        gate_pre = pick_block(all_gate, clamped)
        up_pre = pick_block(all_up, clamped)
        full_inv = pick_block(all_inv, clamped)
        full_normed = pick_block(all_normed, clamped)
        full_up = jnp.where(is_last, pick_block(top_whole, clamped), received)
        full_up = jnp.where(is_valid, full_up, jnp.zeros((), jnp.bfloat16))
        activation, grad_gate, grad_up = unit_grads(full_up, gate_pre, up_pre, down_mat)
        gate_total = gate_total + transposed_product(grad_gate, full_normed)
        up_total = up_total + transposed_product(grad_up, full_normed)
        down_total = down_total + transposed_product(activation, full_up)
        partial_sum = jnp.dot(grad_gate, gate_mat, preferred_element_type=jnp.float32) + jnp.dot(
            grad_up, up_mat, preferred_element_type=jnp.float32
        )
        grad_normed = lax.psum(partial_sum, "dp")
        grad_full = norm_back(gathered, full_inv, full_up, grad_normed, gain_row)
        gain_total = gain_total + jnp.sum(
            grad_normed * gathered.astype(jnp.float32) * full_inv, axis=0
        )
        grad_own = lax.dynamic_slice_in_dim(grad_full, dp_pos * slot_local, slot_local, 0)
        old_rows = pick_block(grad_store, clamped)
        grad_store = lax.dynamic_update_index_in_dim(
            grad_store, jnp.where(is_valid, grad_own, old_rows), clamped, 0
        )
        if step_index < last_step:
            received = from_behind(grad_full, "section", -1)
    return (
        grad_store[None],
        gate_total.astype(jnp.bfloat16)[None],
        up_total.astype(jnp.bfloat16)[None],
        down_total.astype(jnp.bfloat16)[None],
        gain_total[None],
    )


def solution(mesh):
    return jax.shard_map(
        on_device,
        mesh=mesh,
        in_specs=(
            P("section", None, "dp", None),
            P(None, "dp", None),
            P("section", "dp", None),
            P("section", "dp", None),
            P("section", "dp", None),
            P("section", None),
            P(),
        ),
        out_specs=(
            P("section", None, "dp", None),
            P("section", "dp", None),
            P("section", "dp", None),
            P("section", "dp", None),
            P("section", None),
        ),
        check_vma=False,
    )
```

profile of v0, /device:TPU:1, one launch (start us, length us, event | category | flops | bytes accessed | tf_op | source)
XLA Modules:
  0.0 1218.8 jit_solution(14955202066246153748)
XLA Ops:
  8.6 1.4 broadcast_select_fusion
  10.1 81.6 %all-gather.6.cloned.1.call-done = bf16[1,2,64,4096]{3,1,0,2:T(2,128)(2,1)} async-done(((bf16[1,2,1,4096]{3,1,0,2:T(2,128)(2,1)}), bf16[1,2,64,4096]{3,1,0,2:T(2,128)(2,1)}) %all-gather.6.cloned.1.call-update) | async-done | bytes 1048592 | tf_op jit(solution)/shard_map/all_gather | solution.py:75
  91.8 2.4 fusion.8
  94.2 2.0 fusion.10
  98.6 71.2 %all-gather.4.cloned.1.call-done = bf16[2,64,4096]{2,0,1:T(2,128)(2,1)} async-done(((bf16[2,1,4096]{2,0,1:T(2,128)(2,1)}), bf16[2,64,4096]{2,0,1:T(2,128)(2,1)}) %all-gather.4.cloned.1.call-update) | async-done | bytes 1048592 | tf_op jit(solution)/shard_map/all_gather | solution.py:73
  169.7 9.9 constant_dynamic-slice_fusion.1
  181.1 1.0 copy-done.2
  182.1 1.4 convolution_add_fusion.14
  183.6 2.5 fusion.86
  186.0 1.6 copy.28
  188.2 2.8 fusion.147
  191.1 175.2 %all-reduce.6.cloned.1.call-done = f32[64,4096]{1,0:T(8,128)} async-done(((f32[64,4096]{1,0:T(8,128)}), f32[64,4096]{1,0:T(8,128)}) %all-reduce.6.cloned.1.call-update) | async-done | bytes 1048592 | tf_op jit(solution)/shard_map/psum | solution.py:103
  366.3 2.3 fusion.46
  368.6 2.6 fusion.43
  371.2 1.5 collective-permute-start
  372.7 2.6 fusion.88
  376.4 1.1 bitcast_convert_fusion
  377.5 6.1 collective-permute-done
  386.5 1.5 convolution_add_fusion.13
  388.1 1.5 fusion.149
  390.2 1.4 dynamic_update_slice.17
  391.6 4.5 convolution_add_fusion.5
  396.1 178.3 %all-reduce.8.cloned.1.call-done = f32[64,4096]{1,0:T(8,128)} async-done(((f32[64,4096]{1,0:T(8,128)}), f32[64,4096]{1,0:T(8,128)}) %all-reduce.8.cloned.1.call-update) | async-done | bytes 1048592 | tf_op jit(solution)/shard_map/psum | solution.py:103
  574.4 2.3 fusion.53
  576.7 1.6 fusion.50
  578.4 1.4 collective-permute-start.1
  579.8 4.8 convolution_add_fusion.9
  584.6 2.5 convolution_add_fusion.1
  587.1 3.8 collective-permute-done.1
  593.8 1.4 convolution_add_fusion.12
  595.3 1.5 fusion.150
  596.8 1.4 dynamic_update_slice.18
  598.2 4.5 convolution_add_fusion.4
  602.7 178.9 %all-reduce.10.cloned.1.call-done = f32[64,4096]{1,0:T(8,128)} async-done(((f32[64,4096]{1,0:T(8,128)}), f32[64,4096]{1,0:T(8,128)}) %all-reduce.10.cloned.1.call-update) | async-done | bytes 1048592 | tf_op jit(solution)/shard_map/psum | solution.py:103
  781.6 2.3 fusion.60
  784.0 2.4 fusion.57
  786.4 1.4 collective-permute-start.2
  787.8 4.6 convolution_add_fusion.8
  792.4 1.5 fusion.151
  793.9 1.4 dynamic_update_slice.19
  795.3 3.8 collective-permute-done.2
  799.9 2.0 fusion.71
  801.9 1.6 multiply_convert_fusion.2
  805.0 1.4 convolution_add_fusion.11
  806.8 4.7 convolution_add_fusion.3
  811.4 2.6 convolution_add_fusion.7
  814.0 178.8 %all-reduce.12.cloned.1.call-done = f32[64,4096]{1,0:T(8,128)} async-done(((f32[64,4096]{1,0:T(8,128)}), f32[64,4096]{1,0:T(8,128)}) %all-reduce.12.cloned.1.call-update) | async-done | bytes 1048592 | tf_op jit(solution)/shard_map/psum | solution.py:103
  992.8 2.3 fusion.67
  995.2 2.4 fusion.64
  997.6 1.4 collective-permute-start.3
  999.0 2.5 fusion.143
  1002.4 1.4 dynamic_update_slice.20
  1003.8 6.6 collective-permute-done.3
  1010.4 2.0 fusion.69
  1012.5 1.6 multiply_convert_fusion.1
  1014.1 2.6 fusion.145
  1017.1 1.0 copy-done.6
  1018.1 1.5 convolution_add_fusion.10
  1019.7 4.1 fusion.6
  1023.8 2.8 fusion.7
  1026.6 4.1 fusion.5
  1030.7 175.5 %all-reduce.14.cloned.1.call-done = f32[64,4096]{1,0:T(8,128)} async-done(((f32[64,4096]{1,0:T(8,128)}), f32[64,4096]{1,0:T(8,128)}) %all-reduce.14.cloned.1.call-update) | async-done | bytes 1048592 | tf_op jit(solution)/shard_map/psum | solution.py:103
  1206.2 1.6 multiply_reduce_fusion
  1208.4 2.8 fusion.153
  (152 shorter events, 18.8 us)
Async XLA Ops:
  7.2 89.1 %copy-start = (bf16[1,224,4096]{2,1,0:T(8,128)(2,1)S(1)}, bf16[1,224,4096]{2,1,0:T(8,128)(2,1)}, u32[]{:S(2)}) copy-start(bf16[1,224,4096]{2,1,0:T(8,128)(2,1)} %param.9) | copy-start | bytes 5505028
  7.2 84.6 %all-gather.6.cloned.1.call-start = ((), (), s32[]{:S(2)}) async-start(), calls=%async_computation.6 | async-start | bytes 1064960 | tf_op jit(solution)/shard_map/all_gather | solution.py:75
  7.9 161.8 %all-gather.4.cloned.1.call-start = ((), (), s32[]{:S(2)}) async-start(), calls=%async_computation | async-start | bytes 1064960 | tf_op jit(solution)/shard_map/all_gather | solution.py:73
  10.1 356.2 %all-reduce.6.cloned.1.call-start = ((), (), s32[]{:S(2)}) async-start(), calls=%async_computation.1 | async-start | bytes 2097152 | tf_op jit(solution)/shard_map/psum | solution.py:103
  96.2 1.5 copy-start.1
  98.5 89.7 %copy-start.29 = (f32[2,64,224]{2,1,0:T(8,128)}, f32[2,64,224]{2,1,0:T(8,128)S(1)}, u32[]{:S(2)}) copy-start(f32[2,64,224]{2,1,0:T(8,128)S(1)} %fusion.23) | copy-start | bytes 344068
  169.7 10.0 copy-start.12
  179.7 1.4 copy-start.25
  180.6 1.5 copy-start.2
  183.5 390.9 %all-reduce.8.cloned.1.call-start = ((), (), s32[]{:S(2)}) async-start(), calls=%async_computation.2 | async-start | bytes 2097152 | tf_op jit(solution)/shard_map/psum | solution.py:103
  183.6 2.5 copy-start.22
  186.0 2.2 copy-start.26
  188.2 187.1 %copy-start.58 = (f32[64]{0:T(128)}, f32[64]{0:T(128)S(1)}, u32[]{:S(2)}) copy-start(f32[64]{0:T(128)S(1)} %get-tuple-element.16) | copy-start | bytes 772
  188.2 178.1 %copy-start.35 = (f32[1,4096]{1,0:T(1,128)S(1)}, f32[1,4096]{1,0:T(1,128)}, u32[]{:S(2)}) copy-start(f32[1,4096]{1,0:T(1,128)} %param.12) | copy-start | bytes 49156
  366.3 2.3 copy-start.7
  371.2 4.1 copy-start.36
  371.2 12.4 %collective-permute-start = (bf16[64,4096]{1,0:T(8,128)(2,1)S(1)}, bf16[64,4096]{1,0:T(8,128)(2,1)S(1)}, u32[]{:S(2)}, u32[]{:S(2)}) collective-permute-start(bf16[64,4096]{1,0:T(8,128)(2,1)S(1)} %fusion.43), channel_id=1, source_target_pairs={{1,0},{2,1},{3,2},{5,4},{6,5},{7,6},{9,8},{10,9},{11,10},{13,12},{... | collective-permute-start | bytes 1572872 | tf_op jit(solution)/shard_map/ppermute | solution.py:10
  375.3 8.3 copy-start.28
  376.4 7.8 copy-start.13
  376.4 7.8 copy-start.30
  385.0 1.1 copy-start.47
  385.0 1.5 copy-start.3
  388.0 393.6 %all-reduce.10.cloned.1.call-start = ((), (), s32[]{:S(2)}) async-start(), calls=%async_computation.3 | async-start | bytes 2097152 | tf_op jit(solution)/shard_map/psum | solution.py:103
  574.4 2.3 copy-start.8
  574.4 5.4 copy-start.44
  578.4 6.2 copy-start.37
  578.4 6.2 copy-start.31
  578.4 12.5 %collective-permute-start.1 = (bf16[64,4096]{1,0:T(8,128)(2,1)S(1)}, bf16[64,4096]{1,0:T(8,128)(2,1)S(1)}, u32[]{:S(2)}, u32[]{:S(2)}) collective-permute-start(bf16[64,4096]{1,0:T(8,128)(2,1)S(1)} %fusion.50), channel_id=1, source_target_pairs={{1,0},{2,1},{3,2},{5,4},{6,5},{7,6},{9,8},{10,9},{11,10},{13,12},{... | collective-permute-start | bytes 1572872 | tf_op jit(solution)/shard_map/ppermute | solution.py:10
  579.8 4.8 copy-start.17
  584.6 6.3 copy-start.27
  587.1 4.4 copy-start.14
  591.5 192.4 %copy-start.23 = (bf16[64,4096]{1,0:T(8,128)(2,1)}, bf16[64,4096]{1,0:T(8,128)(2,1)S(1)}, u32[]{:S(2)}) copy-start(bf16[64,4096]{1,0:T(8,128)(2,1)S(1)} %fusion.73) | copy-start | bytes 1572868
  592.3 1.1 copy-start.48
  592.3 1.5 copy-start.4
  595.3 397.6 %all-reduce.12.cloned.1.call-start = ((), (), s32[]{:S(2)}) async-start(), calls=%async_computation.4 | async-start | bytes 2097152 | tf_op jit(solution)/shard_map/psum | solution.py:103
  781.6 2.3 copy-start.9
  781.6 6.2 copy-start.46
  786.4 6.1 copy-start.39
  786.4 12.7 %collective-permute-start.2 = (bf16[64,4096]{1,0:T(8,128)(2,1)}, bf16[64,4096]{1,0:T(8,128)(2,1)S(1)}, u32[]{:S(2)}, u32[]{:S(2)}) collective-permute-start(bf16[64,4096]{1,0:T(8,128)(2,1)} %fusion.57), channel_id=1, source_target_pairs={{1,0},{2,1},{3,2},{5,4},{6,5},{7,6},{9,8},{10,9},{11,10},{13,12},{... | collective-permute-start | bytes 1572872 | tf_op jit(solution)/shard_map/ppermute | solution.py:10
  795.3 6.6 copy-start.15
  803.5 1.5 copy-start.5
  806.5 399.7 %all-reduce.14.cloned.1.call-start = ((), (), s32[]{:S(2)}) async-start(), calls=%async_computation.5 | async-start | bytes 2097152 | tf_op jit(solution)/shard_map/psum | solution.py:103
  806.7 4.7 copy-start.19
  806.7 4.7 copy-start.50
  992.8 2.3 copy-start.10
  992.8 6.2 copy-start.32
  997.6 3.9 copy-start.40
  997.6 12.8 %collective-permute-start.3 = (bf16[64,4096]{1,0:T(8,128)(2,1)}, bf16[64,4096]{1,0:T(8,128)(2,1)}, u32[]{:S(2)}, u32[]{:S(2)}) collective-permute-start(bf16[64,4096]{1,0:T(8,128)(2,1)} %fusion.64), channel_id=1, source_target_pairs={{1,0},{2,1},{3,2},{5,4},{6,5},{7,6},{9,8},{10,9},{11,10},{13,12},{... | collective-permute-start | bytes 1572872 | tf_op jit(solution)/shard_map/ppermute | solution.py:10
  1003.8 8.7 copy-start.16
  1010.4 3.6 copy-start.33
  1014.0 2.6 copy-start.51
  1014.0 3.1 copy-start.53
  1016.6 1.5 copy-start.6
  1019.6 4.1 copy-start.18
  1019.6 6.9 copy-start.21
  1023.8 2.8 copy-start.20
  1023.8 2.8 copy-start.24
  1023.8 2.8 copy-start.34
  1026.6 179.6 %copy-start.11 = (bf16[1,2,64,4096]{3,2,1,0:T(8,128)(2,1)S(1)}, bf16[1,2,64,4096]{3,2,1,0:T(8,128)(2,1)}, u32[]{:S(2)}) copy-start(bf16[1,2,64,4096]{3,2,1,0:T(8,128)(2,1)} %copy.28) | copy-start | bytes 3145732
  1030.7 177.7 %copy-start.41 = (bf16[2,1,4096]{2,0,1:T(2,128)(2,1)S(1)}, bf16[2,1,4096]{2,0,1:T(2,128)(2,1)}, u32[]{:S(2)}) copy-start(bf16[2,1,4096]{2,0,1:T(2,128)(2,1)} %dynamic_update_slice.20) | copy-start | bytes 49156
  1030.7 180.6 %copy-start.54 = (f32[4096]{0:T(1024)S(1)}, f32[4096]{0:T(1024)}, u32[]{:S(2)}) copy-start(f32[4096]{0:T(1024)} %get-tuple-element.7) | copy-start | bytes 49156
  1030.7 180.6 %copy-start.55 = (f32[4096]{0:T(1024)S(1)}, f32[4096]{0:T(1024)}, u32[]{:S(2)}) copy-start(f32[4096]{0:T(1024)} %get-tuple-element.5) | copy-start | bytes 49156
  1030.7 180.6 %copy-start.56 = (f32[4096]{0:T(1024)S(1)}, f32[4096]{0:T(1024)}, u32[]{:S(2)}) copy-start(f32[4096]{0:T(1024)} %get-tuple-element.9) | copy-start | bytes 49156
  1030.7 180.6 %copy-start.57 = (f32[4096]{0:T(1024)S(1)}, f32[4096]{0:T(1024)}, u32[]{:S(2)}) copy-start(f32[4096]{0:T(1024)} %get-tuple-element.11) | copy-start | bytes 49156
  (6 other events, 4.4 us)
Sparse Core Ops, SparseCore 0:
  10.8 80.9 all-gather.5
  95.1 74.5 all-gather.3
  183.6 182.5 all-reduce.5
  388.2 186.2 all-reduce.7
  595.4 186.2 all-reduce.9
  806.6 186.2 all-reduce.11
  1019.8 186.3 all-reduce.13
where the time goes:
time: 1220 us
  waiting for transfers between devices  1060 us (87%)
  matrix products  68.6 us (6%)
  other arithmetic  42.1 us (3%)
  local copies, waits for them, and re-layouts  26.6 us (2%)
  between operations  14.8 us (1%)
    psum x5, waiting for transfers between devices, on_device(): grad_normed = lax.psum(partial_sum, 'dp')  887 us
    all_gather x1, waiting for transfers between devices, on_device(): gathered_all = lax.all_gather(layer_rows, 'dp', axis=1, tiled=True)  81.6 us
    all_gather x1, waiting for transfers between devices, on_device(): top_whole = lax.all_gather(top_local, 'dp', axis=1, tiled=True)  71.2 us
    dot_general x15, matrix products, transposed_product(): lax.dot_general(left_rows, right_rows, (((0,), (0,)), ((), ())), preferre...  52.1 us
  transfers between devices with their start and end apart: 11, of which 11 were waited for; matrix products, arithmetic and copies ran while one was open for 6% of the time, Pallas kernels for 0%

commit v1 on v0

v1 whole, which is shorter than its diff:
```python
import jax
import jax.numpy as jnp
from jax import lax
from jax.sharding import Mesh
from jax.sharding import PartitionSpec as P

NZ, NY, NC, NS = 8, 4, 2, 4
DP = ("z", "y", "core")
PLANE = ("z", "y")
LIVE = 85
GROUP = 24
USED = 22
ROWS = NY * GROUP
BF = jnp.bfloat16
F32 = jnp.float32


def dot_nt(a, b):
    return lax.dot_general(a, b, (((1,), (1,)), ((), ())), preferred_element_type=F32)


def dot_nn(a, b):
    return lax.dot_general(a, b, (((1,), (0,)), ((), ())), preferred_element_type=F32)


def dot_tn(a, b):
    return lax.dot_general(a, b, (((0,), (0,)), ((), ())), preferred_element_type=F32)


def row_of(micro, slot):
    position = jnp.where(micro == 0, slot, LIVE - 1 - slot)
    return GROUP * (position // USED) + position % USED


def swap_core(x):
    return lax.ppermute(x, "core", [(0, 1), (1, 0)])


def exchange(x):
    return lax.all_to_all(x, PLANE, 0, 0, tiled=True)


def gather_rows(hidden, top, counts, core):
    width = hidden.shape[-1]
    half = width // 2
    own = jnp.concatenate([hidden, top], axis=0).reshape(8, half)
    mine = exchange(jnp.broadcast_to(own[None], (NZ * NY, 8, half)))
    other = swap_core(mine)
    mine = mine.reshape(NZ * NY * 8, half)
    other = other.reshape(NZ * NY * 8, half)
    cols = lax.broadcasted_iota(jnp.int32, (ROWS, NZ * NY * 8), 1)
    rows = lax.broadcasted_iota(jnp.int32, (ROWS, NZ * NY * 8), 0)
    place, piece = cols // 8, cols % 8
    micro, part = (piece // 2) % 2, piece % 2
    limit = jnp.where(micro == 0, counts[0], counts[1])

    def pick(kind, of_core, at_half):
        slot = place * NC + of_core
        hit = (row_of(micro, slot) == rows) & (slot < limit) & (piece // 4 == kind) & (part == at_half)
        return hit.astype(BF)

    def build(kind):
        halves = []
        for at_half in range(2):
            total = dot_nn(pick(kind, core, at_half), mine) + dot_nn(pick(kind, 1 - core, at_half), other)
            halves.append(total.astype(BF))
        return jnp.concatenate(halves, axis=1)

    return build(0), build(1)


def on_device(hidden_in, grad_out, weight_gate, weight_up, weight_down, gain, counts):
    gate_mat, up_mat, down_mat = weight_gate[0], weight_up[0], weight_down[0]
    gain_row = gain[0]
    width = gate_mat.shape[1]
    half = width // 2
    lanes = width // (NC * NZ)
    z, y, core = lax.axis_index("z"), lax.axis_index("y"), lax.axis_index("core")
    section = lax.axis_index("section")

    hidden, upstream = gather_rows(hidden_in[0, :, 0], grad_out[:, 0], counts, core)
    values = hidden.astype(F32)
    inv_rms = lax.rsqrt(jnp.mean(values * values, axis=-1, keepdims=True) + 1e-05)
    normed = (values * inv_rms * gain_row).astype(BF)
    gate_pre = dot_nt(normed, gate_mat)
    up_pre = dot_nt(normed, up_mat)
    sig = jax.nn.sigmoid(gate_pre)
    silu = gate_pre * sig
    activation = (silu * up_pre).astype(BF)
    gate_factor = up_pre * sig * (1.0 + gate_pre * (1.0 - sig))

    def tile_of(x):
        rows = lax.dynamic_slice_in_dim(x, y * GROUP, GROUP, 0)
        return lax.dynamic_slice_in_dim(rows, core * half + z * lanes, lanes, 1)

    hidden_tile = tile_of(hidden).astype(F32)
    inv_tile = lax.dynamic_slice_in_dim(inv_rms, y * GROUP, GROUP, 0)
    gain_tile = lax.dynamic_slice_in_dim(gain_row, core * half + z * lanes, lanes, 0)
    in_group = lax.broadcasted_iota(jnp.int32, (NY, GROUP, 1), 1)
    tile_row = lax.broadcasted_iota(jnp.int32, (GROUP, 1), 0)

    for step in range(NS):
        last = step == NS - 1
        grad_act = dot_nt(upstream, down_mat)
        grad_gate = (grad_act * gate_factor).astype(BF)
        grad_up = (grad_act * silu).astype(BF)
        partial = dot_nn(grad_gate, gate_mat) + dot_nn(grad_up, up_mat)
        inner = jnp.sum(grad_gate.astype(F32) * gate_pre + grad_up.astype(F32) * up_pre, axis=1)
        inner = jnp.pad(inner.reshape(NY, GROUP), ((0, 0), (0, lanes - GROUP)))
        inner = jnp.tile(inner, (1, NC * NZ))
        packed = jnp.where(in_group == USED, inner[:, None, :], partial.reshape(NY, GROUP, width))
        if last:
            gain_part = jnp.sum(partial * (values * inv_rms), axis=0)
            packed = jnp.where(in_group == USED + 1, gain_part, packed)
        packed = packed.astype(BF).reshape(ROWS, width)
        away = lax.dynamic_slice_in_dim(packed, (1 - core) * half, half, 1)
        kept = lax.dynamic_slice_in_dim(packed, core * half, half, 1)
        summed = (kept.astype(F32) + swap_core(away).astype(F32)).astype(BF)
        pieces = summed.reshape(NY, GROUP, NZ, lanes).transpose(2, 0, 1, 3).reshape(NZ * NY, GROUP, lanes)
        total = jnp.sum(exchange(pieces).astype(F32), axis=0)
        up_tile = tile_of(upstream)
        row_sum = total[USED, :GROUP][:, None]
        grad_tile = (
            up_tile.astype(F32)
            + inv_tile * (gain_tile * total)
            - hidden_tile * inv_tile * inv_tile * row_sum / width
        )
        grad_tile = jnp.where(tile_row < USED, grad_tile, 0.0).astype(BF)
        if last:
            gain_sum = total[USED + 1]
            high = gain_sum.astype(BF)
            low = (gain_sum - high.astype(F32)).astype(BF)
            grad_tile = jnp.where(tile_row == USED, high, grad_tile)
            grad_tile = jnp.where(tile_row == USED + 1, low, grad_tile)
        else:
            moved = lax.ppermute(grad_tile, "section", [(NS - 1 - step, NS - 2 - step)])
            grad_tile = jnp.where(section == NS - 2 - step, moved, up_tile)
        spread = exchange(jnp.broadcast_to(grad_tile[None], (NZ * NY, GROUP, lanes)))
        mine = spread.reshape(NZ, NY, GROUP, lanes).transpose(1, 2, 0, 3).reshape(ROWS, half)
        other = swap_core(mine)
        gathered = jnp.concatenate(
            [jnp.where(core == 0, mine, other), jnp.where(core == 0, other, mine)], axis=1
        )
        if not last:
            upstream = gathered

    gate_grads = dot_tn(grad_gate, normed).astype(BF)
    up_grads = dot_tn(grad_up, normed).astype(BF)
    down_grads = dot_tn(activation, upstream).astype(BF)
    slot = z * NY * NC + y * NC + core
    micro = lax.broadcasted_iota(jnp.int32, (2, ROWS), 0)
    rows = lax.broadcasted_iota(jnp.int32, (2, ROWS), 1)
    limit = jnp.where(micro == 0, counts[0], counts[1])
    own_rows = ((row_of(micro, slot) == rows) & (slot < limit)).astype(BF)
    grad_rows = dot_nn(own_rows, gathered).astype(BF)
    gain_grads = gathered[USED].astype(F32) + gathered[USED + 1].astype(F32)
    return (
        grad_rows[None, :, None],
        gate_grads[None],
        up_grads[None],
        down_grads[None],
        gain_grads[None],
    )


def solution(mesh):
    grid = Mesh(mesh.devices.reshape(NZ, NY, NC, NS), ("z", "y", "core", "section"))
    return jax.shard_map(
        on_device,
        mesh=grid,
        in_specs=(
            P("section", None, DP, None),
            P(None, DP, None),
            P("section", DP, None),
            P("section", DP, None),
            P("section", DP, None),
            P("section", None),
            P(),
        ),
        out_specs=(
            P("section", None, DP, None),
            P("section", DP, None),
            P("section", DP, None),
            P("section", DP, None),
            P("section", None),
        ),
        check_vma=False,
    )
```

time: 1220 us -> 287 us (0.24)
  waiting for transfers between devices: 1060 us -> 69.7 us
  blocking collectives: 0 us -> 104 us
  starting transfers between devices: 6.23 us -> 44.3 us
  other arithmetic: 42.1 us -> 10.3 us
  matrix products: 68.6 us -> 45.6 us
  local copies, waits for them, and re-layouts: 26.6 us -> 10.2 us
  between operations: 14.8 us -> 1.62 us
    psum x5 -> x0, waiting for transfers between devices: 887 us -> none  [on_device(): grad_normed = lax.psum(partial_sum, 'dp')]
    all_gather x2 -> x0, waiting for transfers between devices: 153 us -> none  [the longest x1 81.6 us: on_device(): gathered_all = lax.all_gather(layer_rows, 'dp', axis=1, tiled=True)]
    all_to_all x0 -> x6, blocking collectives: none -> 104 us  [exchange(): return lax.all_to_all(x, PLANE, 0, 0, tiled=True)]
    all_to_all x0 -> x3, waiting for transfers between devices: none -> 50.1 us  [exchange(): return lax.all_to_all(x, PLANE, 0, 0, tiled=True)]
    dot_general x32 -> x26, matrix products: 68.6 us -> 45.6 us  [the longest x17 28.7 us: dot_nn(): lax.dot_general(a, b, (((1,), (0,)), ((), ())), preferred_element_type=F32)]
    all_to_all x0 -> x3, starting transfers between devices: none -> 22.5 us  [exchange(): return lax.all_to_all(x, PLANE, 0, 0, tiled=True)]
    ppermute x4 -> x12, starting transfers between devices: 5.72 us -> 21.7 us  [the longest x9 19.1 us: swap_core(): return lax.ppermute(x, 'core', [(0, 1), (1, 0)])]
    reduce_sum x6 -> x5, other arithmetic: 13.3 us -> 0.53 us  [the longest x4 0.28 us: on_device(): total = jnp.sum(exchange(pieces).astype(F32), axis=0)]
  transfers between devices with their start and end apart: 11 -> 15, of which waited for: 11 -> 11; matrix products, arithmetic and copies ran while one was open for 6% -> 7% of each run, Pallas kernels for 0% -> 0%
where the time goes in v1:
time: 287 us; the launch traced here: 286 us
  blocking collectives  104 us (36%)
  waiting for transfers between devices  69.7 us (24%)
  matrix products  45.6 us (16%)
  starting transfers between devices  44.3 us (15%)
  other arithmetic  10.3 us (4%)
  local copies, waits for them, and re-layouts  10.2 us (4%)
    all_to_all x6, blocking collectives, exchange(): return lax.all_to_all(x, PLANE, 0, 0, tiled=True)  104 us
    all_to_all x3, waiting for transfers between devices, exchange(): return lax.all_to_all(x, PLANE, 0, 0, tiled=True)  50.1 us
    dot_general x17, matrix products, dot_nn(): lax.dot_general(a, b, (((1,), (0,)), ((), ())), preferred_element_type=F32)  28.7 us
    all_to_all x3, starting transfers between devices, exchange(): return lax.all_to_all(x, PLANE, 0, 0, tiled=True)  22.5 us
    ppermute x9, starting transfers between devices, swap_core(): return lax.ppermute(x, 'core', [(0, 1), (1, 0)])  19.1 us
    dot_general x6, matrix products, dot_nt(): lax.dot_general(a, b, (((1,), (1,)), ((), ())), preferred_element_type=F32)  11.1 us
    ppermute x9, waiting for transfers between devices, swap_core(): return lax.ppermute(x, 'core', [(0, 1), (1, 0)])  10.3 us
    ppermute x3, waiting for transfers between devices, on_device(): moved = lax.ppermute(grad_tile, 'section', [(NS - 1 - step, NS - 2 - step)])  9.32 us
  transfers between devices with their start and end apart: 15, of which 11 were waited for; matrix products, arithmetic and copies ran while one was open for 7% of the time, Pallas kernels for 0%

profile of v1, /device:TPU:1, one launch (start us, length us, event | category | flops | bytes accessed | tf_op | source)
XLA Modules:
  0.0 286.2 jit_solution(15111960333575407188)
XLA Ops:
  0.6 0.9 pad_maximum_fusion.10
  1.6 1.1 broadcast_in_dim.219
  2.7 12.2 %all-to-all-start = ((bf16[32,8,2048]{2,1,0:T(8,128)(2,1)}), bf16[32,8,2048]{2,1,0:T(8,128)(2,1)}, u32[]{:S(2)}, u32[]{:S(2)}) async-start(bf16[32,8,2048]{2,1,0:T(8,128)(2,1)} %broadcast_in_dim.219), calls=%async_computation | async-start | bytes 2097152 | tf_op jit(solution)/shard_map/all_to_all | solution.py:40
  15.6 25.4 %all-to-all-done = bf16[32,8,2048]{2,1,0:T(8,128)(2,1)} async-done(((bf16[32,8,2048]{2,1,0:T(8,128)(2,1)}), bf16[32,8,2048]{2,1,0:T(8,128)(2,1)}, u32[]{:S(2)}, u32[]{:S(2)}) %all-to-all-start) | async-done | bytes 1048608 | tf_op jit(solution)/shard_map/all_to_all | solution.py:40
  41.0 2.8 collective-permute-start
  43.8 2.8 fusion.53
  46.6 2.8 fusion.51
  49.4 2.8 fusion.49
  52.2 2.8 fusion.55
  55.0 1.6 fusion.12
  56.6 1.7 fusion.13
  58.6 0.7 fusion.24
  59.4 1.6 fusion.11
  61.0 1.7 fusion.10
  62.7 0.7 copy-done.6
  63.4 0.7 fusion.38
  64.2 1.5 add_reduce_fusion.3
  65.9 2.0 fusion.22
  68.4 0.8 constant_dynamic-slice_fusion.3
  69.2 2.1 collective-permute-done.1
  71.3 1.1 add_convert_fusion.3
  72.5 0.8 copy.12
  73.3 5.3 %all-to-all-start.1 = ((bf16[32,24,256]{2,1,0:T(8,128)(2,1)}), bf16[32,24,256]{2,1,0:T(8,128)(2,1)S(1)}, u32[]{:S(2)}, u32[]{:S(2)}) async-start(bf16[32,24,256]{2,1,0:T(8,128)(2,1)} %bitcast.13), calls=%async_computation.1 | async-start | bytes 786432 | tf_op jit(solution)/shard_map/all_to_all | solution.py:40
  79.3 13.7 %all-to-all-done.1 = bf16[32,24,256]{2,1,0:T(8,128)(2,1)S(1)} async-done(((bf16[32,24,256]{2,1,0:T(8,128)(2,1)}), bf16[32,24,256]{2,1,0:T(8,128)(2,1)S(1)}, u32[]{:S(2)}, u32[]{:S(2)}) %all-to-all-start.1) | async-done | bytes 393248 | tf_op jit(solution)/shard_map/all_to_all | solution.py:40
  93.1 0.7 select_convert_fusion.3
  93.8 0.7 collective-permute-start.2
  94.6 17.1 %all_to_all.45 = bf16[32,24,256]{2,1,0:T(8,128)(2,1)S(1)} all-to-all(bf16[32,24,256]{2,1,0:T(8,128)(2,1)S(1)} %broadcast_in_dim.226), channel_id=1, replica_groups=mesh['z'=8,'y'=4,'core'=2,'section'=4] {'z','y'}, dimensions={0} | all-to-all | bytes 786432 | tf_op jit(solution)/shard_map/all_to_all | solution.py:40
  112.0 3.5 %collective-permute-start.3 = (bf16[96,2048]{1,0:T(8,128)(2,1)S(1)}, bf16[96,2048]{1,0:T(8,128)(2,1)}, u32[]{:S(2)}, u32[]{:S(2)}) collective-permute-start(bf16[96,2048]{1,0:T(8,128)(2,1)S(1)} %bitcast.179), channel_id=1, source_target_pairs={{0,4},{4,0},{1,5},{5,1},{2,6},{6,2},{3,7},{7,3},{8,12},{12,8},{9,1... | collective-permute-start | bytes 1179656 | tf_op jit(solution)/shard_map/ppermute | solution.py:36
  115.5 1.5 collective-permute-done.3
  117.0 1.2 broadcast_select_fusion.7
  118.1 3.0 %add_reduce_fusion.2 = (bf16[96]{0:T(256)(128)(2,1)S(1)}, bf16[96,224]{1,0:T(8,128)(2,1)}, f32[96,224]{1,0:T(8,128)}) fusion(f32[96,224]{1,0:T(8,128)} %get-tuple-element.41, f32[96,224]{1,0:T(8,128)S(1)} %fusion.24, f32[96,224]{1,0:T(8,128)} %get-tuple-element.26, bf16[1,224,4096]{2,1,0:T(8,128)(2,1)} %param.11, ...), kind=kOutput, calls=%fused_computation.149 | convolution fusion | flops 178034592 | bytes 3008704 | tf_op jit(solution)/shard_map/dot_general | solution.py:19
  121.3 2.0 fusion.20
  124.4 1.4 collective-permute-done.4
  126.1 17.7 %all_to_all.46 = bf16[32,24,256]{2,1,0:T(8,128)(2,1)S(1)} all-to-all(bf16[32,24,256]{2,1,0:T(8,128)(2,1)S(1)} %bitcast.165), channel_id=1, replica_groups=mesh['z'=8,'y'=4,'core'=2,'section'=4] {'z','y'}, dimensions={0} | all-to-all | bytes 786432 | tf_op jit(solution)/shard_map/all_to_all | solution.py:40
  143.9 0.7 select_convert_fusion.2
  145.3 17.6 %all_to_all.47 = bf16[32,24,256]{2,1,0:T(8,128)(2,1)S(1)} all-to-all(bf16[32,24,256]{2,1,0:T(8,128)(2,1)S(1)} %broadcast_in_dim.229), channel_id=1, replica_groups=mesh['z'=8,'y'=4,'core'=2,'section'=4] {'z','y'}, dimensions={0} | all-to-all | bytes 786432 | tf_op jit(solution)/shard_map/all_to_all | solution.py:40
  163.3 3.6 %collective-permute-start.6 = (bf16[96,2048]{1,0:T(8,128)(2,1)S(1)}, bf16[96,2048]{1,0:T(8,128)(2,1)S(1)}, u32[]{:S(2)}, u32[]{:S(2)}) collective-permute-start(bf16[96,2048]{1,0:T(8,128)(2,1)S(1)} %bitcast.181), channel_id=1, source_target_pairs={{0,4},{4,0},{1,5},{5,1},{2,6},{6,2},{3,7},{7,3},{8,12},{12,8},{9,1... | collective-permute-start | bytes 1179656 | tf_op jit(solution)/shard_map/ppermute | solution.py:36
  166.9 1.3 collective-permute-done.6
  168.3 1.5 add_reduce_fusion.1
  170.0 2.0 fusion.18
  173.1 1.3 collective-permute-done.7
  174.7 17.6 %all_to_all.48 = bf16[32,24,256]{2,1,0:T(8,128)(2,1)S(1)} all-to-all(bf16[32,24,256]{2,1,0:T(8,128)(2,1)S(1)} %bitcast.169), channel_id=1, replica_groups=mesh['z'=8,'y'=4,'core'=2,'section'=4] {'z','y'}, dimensions={0} | all-to-all | bytes 786432 | tf_op jit(solution)/shard_map/all_to_all | solution.py:40
  192.4 0.7 select_convert_fusion.1
  193.1 1.3 collective-permute-start.8
  194.4 9.3 %collective-permute-done.8 = bf16[24,256]{1,0:T(8,128)(2,1)S(1)} collective-permute-done((bf16[24,256]{1,0:T(8,128)(2,1)}, bf16[24,256]{1,0:T(8,128)(2,1)S(1)}, u32[]{:S(2)}, u32[]{:S(2)}) %collective-permute-start.8) | collective-permute-done | bytes 12320 | tf_op jit(solution)/shard_map/ppermute | solution.py:136
  203.8 16.7 %all_to_all.49 = bf16[32,24,256]{2,1,0:T(8,128)(2,1)S(1)} all-to-all(bf16[32,24,256]{2,1,0:T(8,128)(2,1)S(1)} %broadcast_in_dim.232), channel_id=1, replica_groups=mesh['z'=8,'y'=4,'core'=2,'section'=4] {'z','y'}, dimensions={0} | all-to-all | bytes 786432 | tf_op jit(solution)/shard_map/all_to_all | solution.py:40
  220.8 4.4 %collective-permute-start.9 = (bf16[96,2048]{1,0:T(8,128)(2,1)S(1)}, bf16[96,2048]{1,0:T(8,128)(2,1)}, u32[]{:S(2)}, u32[]{:S(2)}) collective-permute-start(bf16[96,2048]{1,0:T(8,128)(2,1)S(1)} %bitcast.177), channel_id=1, source_target_pairs={{0,4},{4,0},{1,5},{5,1},{2,6},{6,2},{3,7},{7,3},{8,12},{12,8},{9,1... | collective-permute-start | bytes 1179656 | tf_op jit(solution)/shard_map/ppermute | solution.py:36
  225.3 1.4 collective-permute-done.9
  226.7 1.2 broadcast_select_fusion.3
  227.9 3.5 %add_reduce_fusion = (bf16[96]{0:T(256)(128)(2,1)}, bf16[96,224]{1,0:T(8,128)(2,1)}, bf16[96,224]{1,0:T(8,128)(2,1)}) fusion(f32[96,224]{1,0:T(8,128)} %get-tuple-element.41, f32[96,224]{1,0:T(8,128)S(1)} %fusion.24, f32[96,224]{1,0:T(8,128)} %get-tuple-element.26, bf16[1,224,4096]{2,1,0:T(8,128)(2,1)} %param.11, ...), kind=kOutput, calls=%fused_computation.143 | convolution fusion | flops 178034592 | bytes 2965696 | tf_op jit(solution)/shard_map/dot_general | solution.py:19
  231.4 0.7 reshape.183
  232.2 2.0 fusion.16
  235.6 1.4 collective-permute-done.10
  237.2 17.7 %all_to_all.50 = bf16[32,24,256]{2,1,0:T(8,128)(2,1)S(1)} all-to-all(bf16[32,24,256]{2,1,0:T(8,128)(2,1)S(1)} %bitcast.173), channel_id=1, replica_groups=mesh['z'=8,'y'=4,'core'=2,'section'=4] {'z','y'}, dimensions={0} | all-to-all | bytes 786432 | tf_op jit(solution)/shard_map/all_to_all | solution.py:40
  255.2 0.8 broadcast_in_dim.239
  256.0 5.1 %all-to-all-start.8 = ((bf16[32,24,256]{2,1,0:T(8,128)(2,1)}), bf16[32,24,256]{2,1,0:T(8,128)(2,1)}, u32[]{:S(2)}, u32[]{:S(2)}) async-start(bf16[32,24,256]{2,1,0:T(8,128)(2,1)} %broadcast_in_dim.239), calls=%async_computation.8 | async-start | bytes 786432 | tf_op jit(solution)/shard_map/all_to_all | solution.py:40
  261.1 1.2 fusion.121
  262.9 11.0 %all-to-all-done.8 = bf16[32,24,256]{2,1,0:T(8,128)(2,1)} async-done(((bf16[32,24,256]{2,1,0:T(8,128)(2,1)}), bf16[32,24,256]{2,1,0:T(8,128)(2,1)}, u32[]{:S(2)}, u32[]{:S(2)}) %all-to-all-start.8) | async-done | bytes 393248 | tf_op jit(solution)/shard_map/all_to_all | solution.py:40
  273.9 1.3 copy.19
  275.3 3.5 %collective-permute-start.11 = (bf16[96,2048]{1,0:T(8,128)(2,1)S(1)}, bf16[96,2048]{1,0:T(8,128)(2,1)S(1)}, u32[]{:S(2)}, u32[]{:S(2)}) collective-permute-start(bf16[96,2048]{1,0:T(8,128)(2,1)S(1)} %bitcast.175), channel_id=1, source_target_pairs={{0,4},{4,0},{1,5},{5,1},{2,6},{6,2},{3,7},{7,3},{8,12},{12,8},{9,1... | collective-permute-start | bytes 1179656 | tf_op jit(solution)/shard_map/ppermute | solution.py:36
  278.7 1.9 fusion.2
  280.7 1.9 fusion.1
  282.6 1.9 fusion
  285.3 0.9 fusion.9
  (160 shorter events, 10.7 us)
Async XLA Ops:
  0.6 63.5 %copy-start = (bf16[1,224,4096]{2,1,0:T(8,128)(2,1)S(1)}, bf16[1,224,4096]{2,1,0:T(8,128)(2,1)}, u32[]{:S(2)}) copy-start(bf16[1,224,4096]{2,1,0:T(8,128)(2,1)} %param.10) | copy-start | bytes 5505028
  1.6 13.4 %copy-start.26 = (s32[2]{0:T(128)S(1)}, s32[2]{0:T(128)}, u32[]{:S(2)}) copy-start(s32[2]{0:T(128)} %param.13) | copy-start | bytes 28
  2.7 38.3 %all-to-all-start = ((bf16[32,8,2048]{2,1,0:T(8,128)(2,1)}), bf16[32,8,2048]{2,1,0:T(8,128)(2,1)}, u32[]{:S(2)}, u32[]{:S(2)}) async-start(bf16[32,8,2048]{2,1,0:T(8,128)(2,1)} %broadcast_in_dim.219), calls=%async_computation | async-start | bytes 2097152 | tf_op jit(solution)/shard_map/all_to_all | solution.py:40
  14.9 34.6 %copy-start.27 = (pred[24]{0:T(512)(128)(4,1)}, pred[24]{0:T(512)(128)(4,1)S(1)}, u32[]{:S(2)}) copy-start(pred[24]{0:T(512)(128)(4,1)S(1)} %iota_compare_fusion) | copy-start | bytes 76
  15.0 52.9 %copy-start.20 = (pred[96]{0:T(512)(128)(4,1)}, pred[96]{0:T(512)(128)(4,1)S(1)}, u32[]{:S(2)}) copy-start(pred[96]{0:T(512)(128)(4,1)S(1)} %broadcast_in_dim.221) | copy-start | bytes 292
  41.0 14.0 %collective-permute-start = (bf16[32,8,2048]{2,1,0:T(8,128)(2,1)}, bf16[32,8,2048]{2,1,0:T(8,128)(2,1)S(1)}, u32[]{:S(2)}, u32[]{:S(2)}) collective-permute-start(bf16[32,8,2048]{2,1,0:T(8,128)(2,1)} %all-to-all-done), channel_id=1, source_target_pairs={{0,4},{4,0},{1,5},{5,1},{2,6},{6,2},{3,7},{7,3},{8,12},{12,8},{9,1... | collective-permute-start | bytes 3145736 | tf_op jit(solution)/shard_map/ppermute | solution.py:36
  56.6 2.0 copy-start.1
  56.6 2.0 copy-start.16
  58.6 20.1 %copy-start.24 = (f32[96]{0:T(128)}, f32[96]{0:T(128)S(1)}, u32[]{:S(2)}) copy-start(f32[96]{0:T(128)S(1)} %add_rsqrt_fusion) | copy-start | bytes 1156
  60.9 1.7 copy-start.4
  61.0 2.5 copy-start.31
  62.7 0.7 copy-start.6
  64.2 1.6 copy-start.12
  65.9 2.1 copy-start.13
  69.2 2.1 collective-permute-start.1
  72.4 20.7 %copy-start.5 = (bf16[96,2048]{1,0:T(8,128)(2,1)S(1)}, bf16[96,2048]{1,0:T(8,128)(2,1)}, u32[]{:S(2)}) copy-start(bf16[96,2048]{1,0:T(8,128)(2,1)} %copy-done.4) | copy-start | bytes 1179652
  73.3 19.7 %all-to-all-start.1 = ((bf16[32,24,256]{2,1,0:T(8,128)(2,1)}), bf16[32,24,256]{2,1,0:T(8,128)(2,1)S(1)}, u32[]{:S(2)}, u32[]{:S(2)}) async-start(bf16[32,24,256]{2,1,0:T(8,128)(2,1)} %bitcast.13), calls=%async_computation.1 | async-start | bytes 786432 | tf_op jit(solution)/shard_map/all_to_all | solution.py:40
  93.8 0.7 collective-permute-start.2
  112.0 3.5 %copy-start.3 = (bf16[12,8,8,256]{3,1,2,0:T(8,128)(2,1)}, bf16[12,8,8,256]{3,1,2,0:T(8,128)(2,1)S(1)}, u32[]{:S(2)}) copy-start(bf16[12,8,8,256]{3,1,2,0:T(8,128)(2,1)S(1)} %copy.22) | copy-start | bytes 1179652
  112.0 4.9 %collective-permute-start.3 = (bf16[96,2048]{1,0:T(8,128)(2,1)S(1)}, bf16[96,2048]{1,0:T(8,128)(2,1)}, u32[]{:S(2)}, u32[]{:S(2)}) collective-permute-start(bf16[96,2048]{1,0:T(8,128)(2,1)S(1)} %bitcast.179), channel_id=1, source_target_pairs={{0,4},{4,0},{1,5},{5,1},{2,6},{6,2},{3,7},{7,3},{8,12},{12,8},{9,1... | collective-permute-start | bytes 1179656 | tf_op jit(solution)/shard_map/ppermute | solution.py:36
  121.3 2.1 copy-start.14
  121.3 2.1 copy-start.21
  124.0 1.8 collective-permute-start.4
  125.9 18.0 %copy-start.17 = (f32[24]{0:T(128)S(1)}, f32[24]{0:T(128)}, u32[]{:S(2)}) copy-start(f32[24]{0:T(128)} %dynamic-slice.4) | copy-start | bytes 292
  144.6 0.7 collective-permute-start.5
  163.0 5.3 %copy-start.10 = (f32[96,224]{1,0:T(8,128)S(1)}, f32[96,224]{1,0:T(8,128)}, u32[]{:S(2)}) copy-start(f32[96,224]{1,0:T(8,128)} %get-tuple-element.41) | copy-start | bytes 258052
  163.0 5.4 %copy-start.32 = (bf16[1,224,4096]{2,1,0:T(8,128)(2,1)S(1)}, bf16[1,224,4096]{2,1,0:T(8,128)(2,1)}, u32[]{:S(2)}) copy-start(bf16[1,224,4096]{2,1,0:T(8,128)(2,1)} %param.11) | copy-start | bytes 5505028
  163.0 5.4 %copy-start.34 = (f32[96,224]{1,0:T(8,128)S(1)}, f32[96,224]{1,0:T(8,128)}, u32[]{:S(2)}) copy-start(f32[96,224]{1,0:T(8,128)} %get-tuple-element.26) | copy-start | bytes 258052
  163.3 5.0 %collective-permute-start.6 = (bf16[96,2048]{1,0:T(8,128)(2,1)S(1)}, bf16[96,2048]{1,0:T(8,128)(2,1)S(1)}, u32[]{:S(2)}, u32[]{:S(2)}) collective-permute-start(bf16[96,2048]{1,0:T(8,128)(2,1)S(1)} %bitcast.181), channel_id=1, source_target_pairs={{0,4},{4,0},{1,5},{5,1},{2,6},{6,2},{3,7},{7,3},{8,12},{12,8},{9,1... | collective-permute-start | bytes 1179656 | tf_op jit(solution)/shard_map/ppermute | solution.py:36
  170.0 2.1 copy-start.15
  170.0 2.1 copy-start.22
  172.6 1.8 collective-permute-start.7
  174.6 17.8 %copy-start.18 = (f32[24]{0:T(128)S(1)}, f32[24]{0:T(128)}, u32[]{:S(2)}) copy-start(f32[24]{0:T(128)} %dynamic-slice.4) | copy-start | bytes 292
  193.1 10.6 %collective-permute-start.8 = (bf16[24,256]{1,0:T(8,128)(2,1)}, bf16[24,256]{1,0:T(8,128)(2,1)S(1)}, u32[]{:S(2)}, u32[]{:S(2)}) collective-permute-start(bf16[24,256]{1,0:T(8,128)(2,1)} %get-tuple-element.13), channel_id=1, source_target_pairs={{1,0},{5,4},{9,8},{13,12},{17,16},{21,20},{25,24},{29,28},{33,32},... | collective-permute-start | bytes 36872 | tf_op jit(solution)/shard_map/ppermute | solution.py:136
  220.8 4.5 %copy-start.2 = (bf16[12,8,8,256]{3,1,2,0:T(8,128)(2,1)}, bf16[12,8,8,256]{3,1,2,0:T(8,128)(2,1)S(1)}, u32[]{:S(2)}) copy-start(bf16[12,8,8,256]{3,1,2,0:T(8,128)(2,1)S(1)} %copy.28) | copy-start | bytes 1179652
  220.8 5.9 %collective-permute-start.9 = (bf16[96,2048]{1,0:T(8,128)(2,1)S(1)}, bf16[96,2048]{1,0:T(8,128)(2,1)}, u32[]{:S(2)}, u32[]{:S(2)}) collective-permute-start(bf16[96,2048]{1,0:T(8,128)(2,1)S(1)} %bitcast.177), channel_id=1, source_target_pairs={{0,4},{4,0},{1,5},{5,1},{2,6},{6,2},{3,7},{7,3},{8,12},{12,8},{9,1... | collective-permute-start | bytes 1179656 | tf_op jit(solution)/shard_map/ppermute | solution.py:36
  225.2 6.2 %copy-start.29 = (pred[24]{0:T(512)(128)(4,1)}, pred[24]{0:T(512)(128)(4,1)S(1)}, u32[]{:S(2)}) copy-start(pred[24]{0:T(512)(128)(4,1)S(1)} %iota_compare_fusion.2) | copy-start | bytes 76
  232.2 2.0 copy-start.8
  232.2 2.0 copy-start.25
  234.2 0.7 copy-start.23
  235.1 1.8 collective-permute-start.10
  237.0 18.0 %copy-start.19 = (f32[24]{0:T(128)S(1)}, f32[24]{0:T(128)}, u32[]{:S(2)}) copy-start(f32[24]{0:T(128)} %dynamic-slice.4) | copy-start | bytes 292
  237.0 18.0 %copy-start.28 = (pred[24]{0:T(512)(128)(4,1)S(1)}, pred[24]{0:T(512)(128)(4,1)}, u32[]{:S(2)}) copy-start(pred[24]{0:T(512)(128)(4,1)} %copy-done.27) | copy-start | bytes 76
  237.1 18.0 %copy-start.30 = (pred[24]{0:T(512)(128)(4,1)S(1)}, pred[24]{0:T(512)(128)(4,1)}, u32[]{:S(2)}) copy-start(pred[24]{0:T(512)(128)(4,1)} %copy-done.29) | copy-start | bytes 76
  256.0 17.9 %all-to-all-start.8 = ((bf16[32,24,256]{2,1,0:T(8,128)(2,1)}), bf16[32,24,256]{2,1,0:T(8,128)(2,1)}, u32[]{:S(2)}, u32[]{:S(2)}) async-start(bf16[32,24,256]{2,1,0:T(8,128)(2,1)} %broadcast_in_dim.239), calls=%async_computation.8 | async-start | bytes 786432 | tf_op jit(solution)/shard_map/all_to_all | solution.py:40
  273.9 4.8 %copy-start.11 = (f32[96,224]{1,0:T(8,128)S(1)}, f32[96,224]{1,0:T(8,128)}, u32[]{:S(2)}) copy-start(f32[96,224]{1,0:T(8,128)} %get-tuple-element.41) | copy-start | bytes 258052
  275.3 5.4 %copy-start.9 = (bf16[96,224]{1,0:T(8,128)(2,1)S(1)}, bf16[96,224]{1,0:T(8,128)(2,1)}, u32[]{:S(2)}) copy-start(bf16[96,224]{1,0:T(8,128)(2,1)} %get-tuple-element.11) | copy-start | bytes 129028
  275.3 9.3 %collective-permute-start.11 = (bf16[96,2048]{1,0:T(8,128)(2,1)S(1)}, bf16[96,2048]{1,0:T(8,128)(2,1)S(1)}, u32[]{:S(2)}, u32[]{:S(2)}) collective-permute-start(bf16[96,2048]{1,0:T(8,128)(2,1)S(1)} %bitcast.175), channel_id=1, source_target_pairs={{0,4},{4,0},{1,5},{5,1},{2,6},{6,2},{3,7},{7,3},{8,12},{12,8},{9,1... | collective-permute-start | bytes 1179656 | tf_op jit(solution)/shard_map/ppermute | solution.py:36
  280.7 1.9 copy-start.7
  284.6 0.7 copy-start.33

commit v2 on v1

v2 whole, which is shorter than its diff:
```python
import jax
import jax.numpy as jnp
from jax import lax
from jax.sharding import Mesh
from jax.sharding import PartitionSpec as P

NZ, NY, NC, NS = 8, 4, 2, 4
DP = ("z", "y", "core")
PLANE = ("z", "y")
LIVE = 85
GROUP = 24
USED = 22
ROWS = NY * GROUP
BF = jnp.bfloat16
F32 = jnp.float32


def dot_nt(a, b):
    return lax.dot_general(a, b, (((1,), (1,)), ((), ())), preferred_element_type=F32)


def dot_nn(a, b):
    return lax.dot_general(a, b, (((1,), (0,)), ((), ())), preferred_element_type=F32)


def dot_tn(a, b):
    return lax.dot_general(a, b, (((0,), (0,)), ((), ())), preferred_element_type=F32)


def row_of(micro, slot):
    position = jnp.where(micro == 0, slot, LIVE - 1 - slot)
    return GROUP * (position // USED) + position % USED


def swap_core(x):
    return lax.ppermute(x, "core", [(0, 1), (1, 0)])


def exchange(x):
    return lax.all_to_all(x, PLANE, 0, 0, tiled=True)


def spread_rows(own):
    count, half = own.shape
    along_z = lax.all_to_all(jnp.broadcast_to(own[None], (NZ, count, half)), "z", 0, 0, tiled=True)
    shifted = [along_z]
    for by in (1, 3, 2):
        shifted.append(lax.ppermute(along_z, "y", [(i, (i + by) % NY) for i in range(NY)]))
    swapped = [swap_core(x) for x in shifted]
    join = lambda xs: jnp.concatenate([x.reshape(NZ * count, half) for x in xs], axis=0)
    return join(shifted), join(swapped)


def selection(counts, y, core):
    shape = (2, 2, ROWS, NY, NZ, 8)
    at = lambda dim: lax.broadcasted_iota(jnp.int32, shape, dim)
    kind, part, row, shift, z, piece = (at(d) for d in range(6))
    by = jnp.where(shift == 0, 0, jnp.where(shift == 1, 1, jnp.where(shift == 2, 3, 2)))
    slot = z * NY * NC + ((y - by + NY) % NY) * NC + core
    micro = (piece // 2) % 2
    limit = jnp.where(micro == 0, counts[0], counts[1])
    hit = (row_of(micro, slot) == row) & (slot < limit) & (piece // 4 == kind) & (piece % 2 == part)
    return hit.astype(BF).reshape(4 * ROWS, NY * NZ * 8)


def gather_rows(hidden, top, counts, y, core):
    half = hidden.shape[-1] // 2
    own = jnp.concatenate([hidden, top], axis=0).reshape(8, half)
    pick_own = lax.optimization_barrier(selection(counts, y, core))
    pick_other = lax.optimization_barrier(selection(counts, y, 1 - core))
    mine, other = spread_rows(own)
    rows = (dot_nn(pick_own, mine) + dot_nn(pick_other, other)).astype(BF).reshape(2, 2, ROWS, half)
    return jnp.concatenate([rows[0, 0], rows[0, 1]], axis=1), rows[1, 0], rows[1, 1]


def wanted_rows(counts, y):
    shape = (NZ, NY, 8, GROUP)
    to_z, to_y, piece, row = (lax.broadcasted_iota(jnp.int32, shape, d) for d in range(4))
    slot = to_z * NY * NC + to_y * NC + piece // 2
    micro = piece % 2
    limit = jnp.where(micro == 0, counts[0], counts[1])
    hit = (piece < 4) & (row_of(micro, slot) == y * GROUP + row) & (slot < limit)
    carry = (y == 0) & ((piece == 4) & (row == USED) | (piece == 5) & (row == USED + 1))
    return (hit | carry).astype(BF).reshape(NZ * NY * 8, GROUP)


def on_device(hidden_in, grad_out, weight_gate, weight_up, weight_down, gain, counts):
    gate_mat, up_mat, down_mat = weight_gate[0], weight_up[0], weight_down[0]
    gain_row = gain[0]
    width = gate_mat.shape[1]
    half = width // 2
    lanes = width // (NC * NZ)
    z, y, core = lax.axis_index("z"), lax.axis_index("y"), lax.axis_index("core")
    section = lax.axis_index("section")

    def halves(x):
        return (
            lax.dynamic_slice_in_dim(x, core * half, half, 1),
            lax.dynamic_slice_in_dim(x, (1 - core) * half, half, 1),
        )

    units = gate_mat.shape[0]
    padded = -(-units // 256) * 256

    def pad_units(x, axis):
        widths = [(0, 0), (0, 0)]
        widths[axis] = (0, padded - units)
        return jnp.pad(x, widths)

    both = jnp.concatenate([pad_units(gate_mat, 0), pad_units(up_mat, 0)], axis=0)
    both_own, both_away = lax.optimization_barrier(halves(both))
    down_own, down_away = lax.optimization_barrier(halves(pad_units(down_mat, 0)))

    hidden, top_low, top_high = gather_rows(hidden_in[0, :, 0], grad_out[:, 0], counts, y, core)
    values = hidden.astype(F32)
    inv_rms = lax.rsqrt(jnp.mean(values * values, axis=-1, keepdims=True) + 1e-05)
    normed = (values * inv_rms * gain_row).astype(BF)
    gate_pre = dot_nt(normed, gate_mat)
    up_pre = dot_nt(normed, up_mat)
    sig = jax.nn.sigmoid(gate_pre)
    silu = gate_pre * sig
    activation = (silu * up_pre).astype(BF)
    gate_factor = pad_units(up_pre * sig * (1.0 + gate_pre * (1.0 - sig)), 1)
    up_factor = pad_units(silu, 1)
    gate_pre, up_pre = pad_units(gate_pre, 1), pad_units(up_pre, 1)
    mine = jnp.where(core == 0, top_low, top_high)
    other = jnp.where(core == 0, top_high, top_low)

    def tile_of(x, start):
        rows = lax.dynamic_slice_in_dim(x, y * GROUP, GROUP, 0)
        return lax.dynamic_slice_in_dim(rows, start, lanes, 1)

    hidden_tile = tile_of(hidden, core * half + z * lanes).astype(F32)
    up_tile = tile_of(mine, z * lanes)
    inv_tile = lax.dynamic_slice_in_dim(inv_rms, y * GROUP, GROUP, 0)
    gain_tile = lax.dynamic_slice_in_dim(gain_row, core * half + z * lanes, lanes, 0)
    in_group = lax.broadcasted_iota(jnp.int32, (NY, GROUP, 1), 1)
    tile_row = lax.broadcasted_iota(jnp.int32, (GROUP, 1), 0)

    for step in range(NS):
        last = step == NS - 1
        grad_act = dot_nt(mine, down_own) + dot_nt(other, down_away)
        grad_gate = (grad_act * gate_factor).astype(BF)
        grad_up = (grad_act * up_factor).astype(BF)
        grads = jnp.concatenate([grad_gate, grad_up], axis=1)
        inner = jnp.sum(grad_gate.astype(F32) * gate_pre + grad_up.astype(F32) * up_pre, axis=1)
        inner = jnp.tile(jnp.pad(inner, (0, lanes - ROWS)), NZ)

        def partial_of(weights, start):
            partial = dot_nn(grads, weights)
            packed = jnp.where(in_group == USED, inner, partial.reshape(NY, GROUP, half))
            if last:
                scaled = lax.dynamic_slice_in_dim(values, start, half, 1) * inv_rms
                packed = jnp.where(in_group == USED + 1, jnp.sum(partial * scaled, axis=0), packed)
            return packed.astype(BF)

        away = swap_core(partial_of(both_away, (1 - core) * half))
        kept = partial_of(both_own, core * half)
        summed = (kept.astype(F32) + away.astype(F32)).astype(BF)
        pieces = summed.reshape(NY, GROUP, NZ, lanes).transpose(2, 0, 1, 3).reshape(NZ * NY, GROUP, lanes)
        total = jnp.sum(exchange(pieces).astype(F32), axis=0)
        row_sum = lax.dynamic_slice_in_dim(total[USED], y * GROUP, GROUP, 0)[:, None]
        grad_tile = (
            up_tile.astype(F32)
            + inv_tile * (gain_tile * total)
            - hidden_tile * inv_tile * inv_tile * row_sum / width
        )
        grad_tile = jnp.where(tile_row < USED, grad_tile, 0.0).astype(BF)
        if last:
            gain_sum = total[USED + 1]
            high = gain_sum.astype(BF)
            low = (gain_sum - high.astype(F32)).astype(BF)
            grad_tile = jnp.where(tile_row == USED, high, grad_tile)
            grad_tile = jnp.where(tile_row == USED + 1, low, grad_tile)
            wanted = lax.optimization_barrier(wanted_rows(counts, y))
            sent = dot_nn(wanted, grad_tile).astype(BF).reshape(NZ * NY, 8, lanes)
            spread = exchange(sent)
            gate_grads = dot_tn(grad_gate[:, :units], normed).astype(BF)
            up_grads = dot_tn(grad_up[:, :units], normed).astype(BF)
            upstream = jnp.concatenate(
                [jnp.where(core == 0, mine, other), jnp.where(core == 0, other, mine)], axis=1
            )
            down_grads = dot_tn(activation, upstream).astype(BF)
            spread, gate_grads, up_grads, down_grads = lax.optimization_barrier(
                (spread, gate_grads, up_grads, down_grads)
            )
            from_mine = jnp.sum(spread.reshape(NZ, NY, 8, lanes).astype(F32), axis=1).astype(BF)
            from_mine = from_mine.transpose(1, 0, 2).reshape(8, half)
            from_other = swap_core(from_mine)
            break
        moved = lax.ppermute(grad_tile, "section", [(NS - 1 - step, NS - 2 - step)])
        grad_tile = jnp.where(section == NS - 2 - step, moved, up_tile)
        spread = exchange(jnp.broadcast_to(grad_tile[None], (NZ * NY, GROUP, lanes)))
        arrived = swap_core(spread)

        def unpack(x):
            return x.reshape(NZ, NY, GROUP, lanes).transpose(1, 2, 0, 3).reshape(ROWS, half)

        mine, other = unpack(spread), unpack(arrived)
        up_tile = grad_tile

    final = jnp.concatenate(
        [jnp.where(core == 0, from_mine, from_other), jnp.where(core == 0, from_other, from_mine)], axis=1
    )
    own_pair = jnp.where(core == 0, final[0:2], final[2:4])
    gain_grads = final[4].astype(F32) + final[5].astype(F32)
    return (
        own_pair[None, :, None],
        gate_grads[None],
        up_grads[None],
        down_grads[None],
        gain_grads[None],
    )


def solution(mesh):
    grid = Mesh(mesh.devices.reshape(NZ, NY, NC, NS), ("z", "y", "core", "section"))
    return jax.shard_map(
        on_device,
        mesh=grid,
        in_specs=(
            P("section", None, DP, None),
            P(None, DP, None),
            P("section", DP, None),
            P("section", DP, None),
            P("section", DP, None),
            P("section", None),
            P(),
        ),
        out_specs=(
            P("section", None, DP, None),
            P("section", DP, None),
            P("section", DP, None),
            P("section", DP, None),
            P("section", None),
        ),
        check_vma=False,
    )
```

time: 287 us -> 264 us (0.920)
  blocking collectives: 104 us -> 52.7 us
  matrix products: 45.6 us -> 18.4 us
  local copies, waits for them, and re-layouts: 10.2 us -> 35 us
  starting transfers between devices: 44.3 us -> 68.6 us
  other arithmetic: 10.3 us -> 25.2 us
  waiting for transfers between devices: 69.7 us -> 58.8 us
    all_to_all x6 -> x3, blocking collectives: 104 us -> 52.7 us  [exchange(): return lax.all_to_all(x, PLANE, 0, 0, tiled=True)]
    dot_general x17 -> x11, matrix products: 28.7 us -> 6.99 us  [dot_nn(): lax.dot_general(a, b, (((1,), (0,)), ((), ())), preferred_element_type=F32)]
    iota x0 -> x45, local copies, waits for them, and re-layouts: none -> 12.6 us  [the longest x16 11.1 us: wanted_rows(): lax.broadcasted_iota(jnp.int32, shape, d)]
    all_to_all x0 -> x1, starting transfers between devices: none -> 9 us  [spread_rows(): lax.all_to_all(jnp.broadcast_to(own[None], (NZ, count, half)), 'z', 0, 0,...]
    all_to_all x3 -> x5, starting transfers between devices: 22.5 us -> 29.2 us  [exchange(): return lax.all_to_all(x, PLANE, 0, 0, tiled=True)]
    ppermute x3, waiting for transfers between devices: 9.32 us -> 2.82 us  [on_device(): moved = lax.ppermute(grad_tile, 'section', [(NS - 1 - step, NS - 2 - step)])]
    convert_element_type x5 -> x12, other arithmetic: 1.57 us -> 7.32 us  [the longest x2 3.05 us: selection(): return hit.astype(BF).reshape(4 * ROWS, NY * NZ * 8)]
    dot_general x6 -> x10, matrix products: 11.1 us -> 5.6 us  [dot_nt(): lax.dot_general(a, b, (((1,), (1,)), ((), ())), preferred_element_type=F32)]
  transfers between devices with their start and end apart: 15 -> 24, of which waited for: 11 -> 14; matrix products, arithmetic and copies ran while one was open for 7% -> 19% of each run, Pallas kernels for 0% -> 0%
where the time goes in v2:
time: 264 us; the launch traced here: 261 us
  starting transfers between devices  68.6 us (26%)
  waiting for transfers between devices  58.8 us (22%)
  blocking collectives  52.7 us (20%)
  local copies, waits for them, and re-layouts  35 us (13%)
  other arithmetic  25.2 us (10%)
  matrix products  18.4 us (7%)
    all_to_all x3, blocking collectives, exchange(): return lax.all_to_all(x, PLANE, 0, 0, tiled=True)  52.7 us
    all_to_all x5, waiting for transfers between devices, exchange(): return lax.all_to_all(x, PLANE, 0, 0, tiled=True)  47.2 us
    all_to_all x5, starting transfers between devices, exchange(): return lax.all_to_all(x, PLANE, 0, 0, tiled=True)  29.2 us
    ppermute x12, starting transfers between devices, swap_core(): return lax.ppermute(x, 'core', [(0, 1), (1, 0)])  22.1 us
    iota x16, local copies, waits for them, and re-layouts, wanted_rows(): lax.broadcasted_iota(jnp.int32, shape, d)  11.1 us
    all_to_all x1, starting transfers between devices, spread_rows(): lax.all_to_all(jnp.broadcast_to(own[None], (NZ, count, half)), 'z', 0, 0,...  9 us
    dot_general x11, matrix products, dot_nn(): lax.dot_general(a, b, (((1,), (0,)), ((), ())), preferred_element_type=F32)  6.99 us
    dynamic_slice x2, local copies, waits for them, and re-layouts, halves(): lax.dynamic_slice_in_dim(x, (1 - core) * half, half, 1)  5.8 us
  transfers between devices with their start and end apart: 24, of which 14 were waited for; matrix products, arithmetic and copies ran while one was open for 19% of the time, Pallas kernels for 0%

profile of v2, /device:TPU:1, one launch (start us, length us, event | category | flops | bytes accessed | tf_op | source)
XLA Modules:
  0.0 261.0 jit_solution(11946760406502186511)
XLA Ops:
  0.6 0.8 pad_maximum_fusion.13
  2.1 9.0 %all-to-all-start = ((bf16[8,8,2048]{2,1,0:T(8,128)(2,1)}), bf16[8,8,2048]{2,1,0:T(8,128)(2,1)}, u32[]{:S(2)}, u32[]{:S(2)}) async-start(bf16[8,8,2048]{2,1,0:T(8,128)(2,1)} %broadcast_in_dim.213), calls=%async_computation | async-start | bytes 524288 | tf_op jit(solution)/shard_map/all_to_all | solution.py:45
  11.4 1.3 fusion.116
  14.6 3.8 %fusion.2 = bf16[512,4096]{1,0:T(8,128)(2,1)} fusion(bf16[224,4096]{1,0:T(8,128)(2,1)} %bitcast.188, bf16[224,4096]{1,0:T(8,128)(2,1)} %bitcast.189), kind=kLoop, calls=%fused_computation.7 | loop fusion | flops 16777216 | bytes 7864320 | tf_op jit(solution)/shard_map/concatenate | solution.py:110
  18.4 4.2 %constant_dynamic-slice_fusion.4 = (bf16[512,2048]{1,0:T(8,128)(2,1)}, bf16[512,2048]{1,0:T(8,128)(2,1)S(1)}) fusion(bf16[512,4096]{1,0:T(8,128)(2,1)} %fusion.2, s32[]{:T(128)S(6)} %select_n.328, s32[]{:T(128)S(6)} %select_n.327), kind=kLoop, calls=%fused_computation.214 | loop fusion | bytes 8388616 | tf_op jit(solution)/shard_map/dynamic_slice | solution.py:99
  22.6 1.5 fusion.43
  24.1 1.5 fusion.44
  25.7 3.0 %collective-permute-start.2 = (bf16[8,8,2048]{2,1,0:T(8,128)(2,1)}, bf16[8,8,2048]{2,1,0:T(8,128)(2,1)S(1)}, u32[]{:S(2)}, u32[]{:S(2)}) collective-permute-start(bf16[8,8,2048]{2,1,0:T(8,128)(2,1)} %all-to-all-done), channel_id=1, source_target_pairs={{0,16},{8,24},{16,0},{24,8},{1,17},{9,25},{17,1},{25,9},{2,18},{10... | collective-permute-start | bytes 786440 | tf_op jit(solution)/shard_map/ppermute | solution.py:48
  28.7 0.8 collective-permute-start.1
  30.1 1.6 pad_dynamic-slice_fusion
  31.8 1.9 collective-permute-start.3
  34.4 3.2 %collective-permute-start.6 = (bf16[8,8,2048]{2,1,0:T(8,128)(2,1)S(1)}, bf16[8,8,2048]{2,1,0:T(8,128)(2,1)S(1)}, u32[]{:S(2)}, u32[]{:S(2)}) collective-permute-start(bf16[8,8,2048]{2,1,0:T(8,128)(2,1)S(1)} %collective-permute-done.2), channel_id=1, source_target_pairs={{0,4},{4,0},{1,5},{5,1},{2,6},{6,2},{3,7},{7,3},{8,12},{12,8},{9,1... | collective-permute-start | bytes 786440 | tf_op jit(solution)/shard_map/ppermute | solution.py:36
  37.6 3.1 %collective-permute-done.1 = bf16[8,8,2048]{2,1,0:T(8,128)(2,1)S(1)} collective-permute-done((bf16[8,8,2048]{2,1,0:T(8,128)(2,1)}, bf16[8,8,2048]{2,1,0:T(8,128)(2,1)S(1)}, u32[]{:S(2)}, u32[]{:S(2)}) %collective-permute-start.1) | collective-permute-done | bytes 262176 | tf_op jit(solution)/shard_map/ppermute | solution.py:48
  40.7 1.4 collective-permute-start.5
  42.2 1.5 fusion.4
  44.8 1.4 copy-done.12
  46.2 0.7 fusion.109
  46.9 0.8 fusion.63
  51.1 0.9 collective-permute-done.7
  52.3 0.8 copy.12
  53.1 9.4 %all-to-all-start.1 = ((bf16[32,24,256]{2,1,0:T(8,128)(2,1)}), bf16[32,24,256]{2,1,0:T(8,128)(2,1)}, u32[]{:S(2)}, u32[]{:S(2)}) async-start(bf16[32,24,256]{2,1,0:T(8,128)(2,1)} %bitcast.190), calls=%async_computation.1 | async-start | bytes 786432 | tf_op jit(solution)/shard_map/all_to_all | solution.py:40
  64.4 11.9 %all-to-all-done.1 = bf16[32,24,256]{2,1,0:T(8,128)(2,1)} async-done(((bf16[32,24,256]{2,1,0:T(8,128)(2,1)}), bf16[32,24,256]{2,1,0:T(8,128)(2,1)}, u32[]{:S(2)}, u32[]{:S(2)}) %all-to-all-start.1) | async-done | bytes 393248 | tf_op jit(solution)/shard_map/all_to_all | solution.py:40
  76.3 1.1 convert_reduce_fusion.3
  77.4 1.5 select_convert_fusion.11
  78.9 1.2 collective-permute-start.8
  80.1 0.8 bitcast_select_fusion
  81.0 17.5 %all_to_all.45 = bf16[32,24,256]{2,1,0:T(8,128)(2,1)S(1)} all-to-all(bf16[32,24,256]{2,1,0:T(8,128)(2,1)S(1)} %broadcast_in_dim.217), channel_id=1, replica_groups=mesh['z'=8,'y'=4,'core'=2,'section'=4] {'z','y'}, dimensions={0} | all-to-all | bytes 786432 | tf_op jit(solution)/shard_map/all_to_all | solution.py:40
  98.5 3.6 %collective-permute-start.9 = (bf16[32,24,256]{2,1,0:T(8,128)(2,1)S(1)}, bf16[32,24,256]{2,1,0:T(8,128)(2,1)S(1)}, u32[]{:S(2)}, u32[]{:S(2)}) collective-permute-start(bf16[32,24,256]{2,1,0:T(8,128)(2,1)S(1)} %all_to_all.45), channel_id=1, source_target_pairs={{0,4},{4,0},{1,5},{5,1},{2,6},{6,2},{3,7},{7,3},{8,12},{12,8},{9,1... | collective-permute-start | bytes 1179656 | tf_op jit(solution)/shard_map/ppermute | solution.py:36
  105.9 1.1 collective-permute-done.10
  107.4 18.1 %all_to_all.46 = bf16[32,24,256]{2,1,0:T(8,128)(2,1)S(1)} all-to-all(bf16[32,24,256]{2,1,0:T(8,128)(2,1)S(1)} %bitcast.203), channel_id=1, replica_groups=mesh['z'=8,'y'=4,'core'=2,'section'=4] {'z','y'}, dimensions={0} | all-to-all | bytes 786432 | tf_op jit(solution)/shard_map/all_to_all | solution.py:40
  126.4 1.2 collective-permute-start.11
  128.4 17.1 %all_to_all.47 = bf16[32,24,256]{2,1,0:T(8,128)(2,1)S(1)} all-to-all(bf16[32,24,256]{2,1,0:T(8,128)(2,1)S(1)} %broadcast_in_dim.219), channel_id=1, replica_groups=mesh['z'=8,'y'=4,'core'=2,'section'=4] {'z','y'}, dimensions={0} | all-to-all | bytes 786432 | tf_op jit(solution)/shard_map/all_to_all | solution.py:40
  145.5 3.5 %collective-permute-start.12 = (bf16[32,24,256]{2,1,0:T(8,128)(2,1)S(1)}, bf16[32,24,256]{2,1,0:T(8,128)(2,1)S(1)}, u32[]{:S(2)}, u32[]{:S(2)}) collective-permute-start(bf16[32,24,256]{2,1,0:T(8,128)(2,1)S(1)} %all_to_all.47), channel_id=1, source_target_pairs={{0,4},{4,0},{1,5},{5,1},{2,6},{6,2},{3,7},{7,3},{8,12},{12,8},{9,1... | collective-permute-start | bytes 1179656 | tf_op jit(solution)/shard_map/ppermute | solution.py:36
  152.9 1.1 collective-permute-done.13
  154.3 0.8 copy.18
  155.1 4.6 %all-to-all-start.5 = ((bf16[32,24,256]{2,1,0:T(8,128)(2,1)}), bf16[32,24,256]{2,1,0:T(8,128)(2,1)}, u32[]{:S(2)}, u32[]{:S(2)}) async-start(bf16[32,24,256]{2,1,0:T(8,128)(2,1)} %bitcast.197), calls=%async_computation.5 | async-start | bytes 786432 | tf_op jit(solution)/shard_map/all_to_all | solution.py:40
  160.2 14.0 %all-to-all-done.5 = bf16[32,24,256]{2,1,0:T(8,128)(2,1)} async-done(((bf16[32,24,256]{2,1,0:T(8,128)(2,1)}), bf16[32,24,256]{2,1,0:T(8,128)(2,1)}, u32[]{:S(2)}, u32[]{:S(2)}) %all-to-all-start.5) | async-done | bytes 393248 | tf_op jit(solution)/shard_map/all_to_all | solution.py:40
  174.2 1.1 convert_reduce_fusion.1
  175.4 1.4 select_convert_fusion.9
  176.7 1.3 collective-permute-start.14
  178.6 1.2 iota.426
  179.8 1.4 iota.427
  181.2 1.3 iota.423
  182.5 1.3 iota.424
  183.8 2.8 %collective-permute-done.14 = bf16[24,256]{1,0:T(8,128)(2,1)} collective-permute-done((bf16[24,256]{1,0:T(8,128)(2,1)}, bf16[24,256]{1,0:T(8,128)(2,1)}, u32[]{:S(2)}, u32[]{:S(2)}) %collective-permute-start.14) | collective-permute-done | bytes 12320 | tf_op jit(solution)/shard_map/ppermute | solution.py:191
  187.9 0.8 broadcast_in_dim.221
  188.7 4.7 %all-to-all-start.6 = ((bf16[32,24,256]{2,1,0:T(8,128)(2,1)}), bf16[32,24,256]{2,1,0:T(8,128)(2,1)}, u32[]{:S(2)}, u32[]{:S(2)}) async-start(bf16[32,24,256]{2,1,0:T(8,128)(2,1)} %broadcast_in_dim.221), calls=%async_computation.6 | async-start | bytes 786432 | tf_op jit(solution)/shard_map/all_to_all | solution.py:40
  193.4 0.7 broadcast_add_fusion
  203.2 2.2 all-to-all-done.6
  205.3 4.3 %collective-permute-start.15 = (bf16[32,24,256]{2,1,0:T(8,128)(2,1)}, bf16[32,24,256]{2,1,0:T(8,128)(2,1)S(1)}, u32[]{:S(2)}, u32[]{:S(2)}) collective-permute-start(bf16[32,24,256]{2,1,0:T(8,128)(2,1)} %all-to-all-done.6), channel_id=1, source_target_pairs={{0,4},{4,0},{1,5},{5,1},{2,6},{6,2},{3,7},{7,3},{8,12},{12,8},{9,1... | collective-permute-start | bytes 1179656 | tf_op jit(solution)/shard_map/ppermute | solution.py:36
  209.6 1.1 fusion.19
  210.8 1.2 copy.19
  216.0 1.9 fusion.62
  217.9 1.9 convolution_convert_fusion.2
  220.2 0.8 copy.21
  221.1 5.5 %all-to-all-start.7 = ((bf16[32,24,256]{2,1,0:T(8,128)(2,1)}), bf16[32,24,256]{2,1,0:T(8,128)(2,1)S(1)}, u32[]{:S(2)}, u32[]{:S(2)}) async-start(bf16[32,24,256]{2,1,0:T(8,128)(2,1)} %bitcast.53), calls=%async_computation.7 | async-start | bytes 786432 | tf_op jit(solution)/shard_map/all_to_all | solution.py:40
  226.8 1.9 convolution_convert_fusion
  228.7 11.7 %all-to-all-done.7 = bf16[32,24,256]{2,1,0:T(8,128)(2,1)S(1)} async-done(((bf16[32,24,256]{2,1,0:T(8,128)(2,1)}), bf16[32,24,256]{2,1,0:T(8,128)(2,1)S(1)}, u32[]{:S(2)}, u32[]{:S(2)}) %all-to-all-start.7) | async-done | bytes 393248 | tf_op jit(solution)/shard_map/all_to_all | solution.py:40
  240.6 0.9 fusion.3
  241.5 5.0 %all-to-all-start.8 = ((bf16[32,8,256]{2,1,0:T(8,128)(2,1)}), bf16[32,8,256]{2,1,0:T(8,128)(2,1)S(1)}, u32[]{:S(2)}, u32[]{:S(2)}) async-start(bf16[32,8,256]{2,1,0:T(8,128)(2,1)} %fusion.3), calls=%async_computation.8 | async-start | bytes 262144 | tf_op jit(solution)/shard_map/all_to_all | solution.py:40
  246.6 1.9 convolution_convert_fusion.1
  248.5 7.4 %all-to-all-done.8 = bf16[32,8,256]{2,1,0:T(8,128)(2,1)S(1)} async-done(((bf16[32,8,256]{2,1,0:T(8,128)(2,1)}), bf16[32,8,256]{2,1,0:T(8,128)(2,1)S(1)}, u32[]{:S(2)}, u32[]{:S(2)}) %all-to-all-start.8) | async-done | bytes 131104 | tf_op jit(solution)/shard_map/all_to_all | solution.py:40
  255.9 3.0 %collective-permute-start.17 = (bf16[8,2048]{1,0:T(8,128)(2,1)S(1)}, bf16[8,2048]{1,0:T(8,128)(2,1)S(1)}, u32[]{:S(2)}, u32[]{:S(2)}) collective-permute-start(bf16[8,2048]{1,0:T(8,128)(2,1)S(1)} %bitcast.230), channel_id=1, source_target_pairs={{0,4},{4,0},{1,5},{5,1},{2,6},{6,2},{3,7},{7,3},{8,12},{12,8},{9,1... | collective-permute-start | bytes 98312 | tf_op jit(solution)/shard_map/ppermute | solution.py:36
  258.9 0.9 collective-permute-done.17
  (317 shorter events, 37.1 us)
Async XLA Ops:
  2.1 23.5 %all-to-all-start = ((bf16[8,8,2048]{2,1,0:T(8,128)(2,1)}), bf16[8,8,2048]{2,1,0:T(8,128)(2,1)}, u32[]{:S(2)}, u32[]{:S(2)}) async-start(bf16[8,8,2048]{2,1,0:T(8,128)(2,1)} %broadcast_in_dim.213), calls=%async_computation | async-start | bytes 524288 | tf_op jit(solution)/shard_map/all_to_all | solution.py:45
  11.2 3.1 %copy-start.71 = (s32[8]{0:T(128)}, s32[8]{0:T(128)S(1)}, u32[]{:S(2)}) copy-start(s32[8]{0:T(128)S(1)} %iota_shift-right-logical_fusion) | copy-start | bytes 100
  11.2 3.2 %copy-start.70 = (s32[8]{0:T(128)}, s32[8]{0:T(128)S(1)}, u32[]{:S(2)}) copy-start(s32[8]{0:T(128)S(1)} %broadcast_add_fusion.2) | copy-start | bytes 100
  11.2 2.0 copy-start.69
  11.2 1.7 copy-start.68
  11.2 3.2 %copy-start.67 = (pred[8]{0:T(512)(128)(4,1)}, pred[8]{0:T(512)(128)(4,1)S(1)}, u32[]{:S(2)}) copy-start(pred[8]{0:T(512)(128)(4,1)S(1)} %compare_and_fusion.2) | copy-start | bytes 28
  11.3 2.3 copy-start.66
  25.7 8.7 %collective-permute-start.2 = (bf16[8,8,2048]{2,1,0:T(8,128)(2,1)}, bf16[8,8,2048]{2,1,0:T(8,128)(2,1)S(1)}, u32[]{:S(2)}, u32[]{:S(2)}) collective-permute-start(bf16[8,8,2048]{2,1,0:T(8,128)(2,1)} %all-to-all-done), channel_id=1, source_target_pairs={{0,16},{8,24},{16,0},{24,8},{1,17},{9,25},{17,1},{25,9},{2,18},{10... | collective-permute-start | bytes 786440 | tf_op jit(solution)/shard_map/ppermute | solution.py:48
  28.7 12.1 %collective-permute-start.1 = (bf16[8,8,2048]{2,1,0:T(8,128)(2,1)}, bf16[8,8,2048]{2,1,0:T(8,128)(2,1)S(1)}, u32[]{:S(2)}, u32[]{:S(2)}) collective-permute-start(bf16[8,8,2048]{2,1,0:T(8,128)(2,1)} %all-to-all-done), channel_id=1, source_target_pairs={{0,24},{8,0},{16,8},{24,16},{1,25},{9,1},{17,9},{25,17},{2,26},{10... | collective-permute-start | bytes 786440 | tf_op jit(solution)/shard_map/ppermute | solution.py:48
  29.4 12.8 %collective-permute-start = (bf16[8,8,2048]{2,1,0:T(8,128)(2,1)}, bf16[8,8,2048]{2,1,0:T(8,128)(2,1)S(1)}, u32[]{:S(2)}, u32[]{:S(2)}) collective-permute-start(bf16[8,8,2048]{2,1,0:T(8,128)(2,1)} %all-to-all-done), channel_id=1, source_target_pairs={{0,8},{8,16},{16,24},{24,0},{1,9},{9,17},{17,25},{25,1},{2,10},{10... | collective-permute-start | bytes 786440 | tf_op jit(solution)/shard_map/ppermute | solution.py:48
  31.8 16.5 %copy-start.4 = (bf16[256,2048]{1,0:T(8,128)(2,1)}, bf16[256,2048]{1,0:T(8,128)(2,1)S(1)}, u32[]{:S(2)}) copy-start(bf16[256,2048]{1,0:T(8,128)(2,1)S(1)} %get-tuple-element.14) | copy-start | bytes 3145732
  31.8 20.2 %copy-start.40 = (pred[24]{0:T(512)(128)(4,1)}, pred[24]{0:T(512)(128)(4,1)S(1)}, u32[]{:S(2)}) copy-start(pred[24]{0:T(512)(128)(4,1)S(1)} %iota_compare_fusion.5) | copy-start | bytes 76
  31.8 11.9 %collective-permute-start.3 = (bf16[8,8,2048]{2,1,0:T(8,128)(2,1)}, bf16[8,8,2048]{2,1,0:T(8,128)(2,1)S(1)}, u32[]{:S(2)}, u32[]{:S(2)}) collective-permute-start(bf16[8,8,2048]{2,1,0:T(8,128)(2,1)} %all-to-all-done), channel_id=1, source_target_pairs={{0,4},{4,0},{1,5},{5,1},{2,6},{6,2},{3,7},{7,3},{8,12},{12,8},{9,1... | collective-permute-start | bytes 786440 | tf_op jit(solution)/shard_map/ppermute | solution.py:36
  34.4 9.4 %collective-permute-start.6 = (bf16[8,8,2048]{2,1,0:T(8,128)(2,1)S(1)}, bf16[8,8,2048]{2,1,0:T(8,128)(2,1)S(1)}, u32[]{:S(2)}, u32[]{:S(2)}) collective-permute-start(bf16[8,8,2048]{2,1,0:T(8,128)(2,1)S(1)} %collective-permute-done.2), channel_id=1, source_target_pairs={{0,4},{4,0},{1,5},{5,1},{2,6},{6,2},{3,7},{7,3},{8,12},{12,8},{9,1... | collective-permute-start | bytes 786440 | tf_op jit(solution)/shard_map/ppermute | solution.py:36
  40.7 3.0 %collective-permute-start.5 = (bf16[8,8,2048]{2,1,0:T(8,128)(2,1)S(1)}, bf16[8,8,2048]{2,1,0:T(8,128)(2,1)S(1)}, u32[]{:S(2)}, u32[]{:S(2)}) collective-permute-start(bf16[8,8,2048]{2,1,0:T(8,128)(2,1)S(1)} %collective-permute-done.1), channel_id=1, source_target_pairs={{0,4},{4,0},{1,5},{5,1},{2,6},{6,2},{3,7},{7,3},{8,12},{12,8},{9,1... | collective-permute-start | bytes 786440 | tf_op jit(solution)/shard_map/ppermute | solution.py:36
  42.2 1.6 collective-permute-start.4
  44.4 1.8 copy-start.12
  44.4 1.8 copy-start.36
  44.5 2.4 copy-start.8
  44.5 3.3 %copy-start.14 = (bf16[1,1,96,2048]{3,2,1,0:T(8,128)(2,1)}, bf16[1,1,96,2048]{3,2,1,0:T(8,128)(2,1)S(1)}, u32[]{:S(2)}) copy-start(bf16[1,1,96,2048]{3,2,1,0:T(8,128)(2,1)S(1)} %get-tuple-element.43) | copy-start | bytes 1179652
  44.8 2.1 copy-start.13
  44.8 2.9 %copy-start.46 = (f32[96]{0:T(128)}, f32[96]{0:T(128)S(1)}, u32[]{:S(2)}) copy-start(f32[96]{0:T(128)S(1)} %add_rsqrt_fusion) | copy-start | bytes 1156
  47.8 1.7 copy-start
  50.0 2.0 collective-permute-start.7
  53.1 23.2 %all-to-all-start.1 = ((bf16[32,24,256]{2,1,0:T(8,128)(2,1)}), bf16[32,24,256]{2,1,0:T(8,128)(2,1)}, u32[]{:S(2)}, u32[]{:S(2)}) async-start(bf16[32,24,256]{2,1,0:T(8,128)(2,1)} %bitcast.190), calls=%async_computation.1 | async-start | bytes 786432 | tf_op jit(solution)/shard_map/all_to_all | solution.py:40
  64.4 38.1 %copy-start.53 = (f32[24]{0:T(128)}, f32[24]{0:T(128)S(1)}, u32[]{:S(2)}) copy-start(f32[24]{0:T(128)S(1)} %dynamic-slice.9) | copy-start | bytes 292
  78.9 46.8 %copy-start.34 = (bf16[24,256]{1,0:T(8,128)(2,1)}, bf16[24,256]{1,0:T(8,128)(2,1)S(1)}, u32[]{:S(2)}) copy-start(bf16[24,256]{1,0:T(8,128)(2,1)S(1)} %get-tuple-element.35) | copy-start | bytes 36868
  78.9 1.2 collective-permute-start.8
  81.0 44.7 %copy-start.33 = (bf16[24,256]{1,0:T(8,128)(2,1)}, bf16[24,256]{1,0:T(8,128)(2,1)S(1)}, u32[]{:S(2)}) copy-start(bf16[24,256]{1,0:T(8,128)(2,1)S(1)} %bitcast_select_fusion) | copy-start | bytes 36868
  98.5 4.9 %collective-permute-start.9 = (bf16[32,24,256]{2,1,0:T(8,128)(2,1)S(1)}, bf16[32,24,256]{2,1,0:T(8,128)(2,1)S(1)}, u32[]{:S(2)}, u32[]{:S(2)}) collective-permute-start(bf16[32,24,256]{2,1,0:T(8,128)(2,1)S(1)} %all_to_all.45), channel_id=1, source_target_pairs={{0,4},{4,0},{1,5},{5,1},{2,6},{6,2},{3,7},{7,3},{8,12},{12,8},{9,1... | collective-permute-start | bytes 1179656 | tf_op jit(solution)/shard_map/ppermute | solution.py:36
  102.3 1.4 copy-start.5
  102.9 1.7 copy-start.1
  105.2 1.8 collective-permute-start.10
  107.2 18.5 %copy-start.43 = (f32[1,256]{1,0:T(1,128)S(1)}, f32[1,256]{1,0:T(1,128)}, u32[]{:S(2)}) copy-start(f32[1,256]{1,0:T(1,128)} %constant_dynamic-slice_fusion.6) | copy-start | bytes 3076
  107.2 18.5 %copy-start.51 = (pred[24]{0:T(512)(128)(4,1)S(1)}, pred[24]{0:T(512)(128)(4,1)}, u32[]{:S(2)}) copy-start(pred[24]{0:T(512)(128)(4,1)} %iota_compare_fusion.8) | copy-start | bytes 76
  107.2 18.5 %copy-start.54 = (f32[24]{0:T(128)S(1)}, f32[24]{0:T(128)}, u32[]{:S(2)}) copy-start(f32[24]{0:T(128)} %copy-done.53) | copy-start | bytes 292
  126.4 1.2 collective-permute-start.11
  145.5 4.9 %collective-permute-start.12 = (bf16[32,24,256]{2,1,0:T(8,128)(2,1)S(1)}, bf16[32,24,256]{2,1,0:T(8,128)(2,1)S(1)}, u32[]{:S(2)}, u32[]{:S(2)}) collective-permute-start(bf16[32,24,256]{2,1,0:T(8,128)(2,1)S(1)} %all_to_all.47), channel_id=1, source_target_pairs={{0,4},{4,0},{1,5},{5,1},{2,6},{6,2},{3,7},{7,3},{8,12},{12,8},{9,1... | collective-permute-start | bytes 1179656 | tf_op jit(solution)/shard_map/ppermute | solution.py:36
  149.3 1.4 copy-start.6
  149.3 1.4 copy-start.17
  149.9 1.7 copy-start.2
  152.2 1.8 collective-permute-start.13
  154.2 21.2 %copy-start.44 = (f32[1,256]{1,0:T(1,128)S(1)}, f32[1,256]{1,0:T(1,128)}, u32[]{:S(2)}) copy-start(f32[1,256]{1,0:T(1,128)} %constant_dynamic-slice_fusion.6) | copy-start | bytes 3076
  155.1 19.1 %all-to-all-start.5 = ((bf16[32,24,256]{2,1,0:T(8,128)(2,1)}), bf16[32,24,256]{2,1,0:T(8,128)(2,1)}, u32[]{:S(2)}, u32[]{:S(2)}) async-start(bf16[32,24,256]{2,1,0:T(8,128)(2,1)} %bitcast.197), calls=%async_computation.5 | async-start | bytes 786432 | tf_op jit(solution)/shard_map/all_to_all | solution.py:40
  176.7 9.9 %collective-permute-start.14 = (bf16[24,256]{1,0:T(8,128)(2,1)}, bf16[24,256]{1,0:T(8,128)(2,1)}, u32[]{:S(2)}, u32[]{:S(2)}) collective-permute-start(bf16[24,256]{1,0:T(8,128)(2,1)} %select_convert_fusion.9), channel_id=1, source_target_pairs={{1,0},{5,4},{9,8},{13,12},{17,16},{21,20},{25,24},{29,28},{33,32},... | collective-permute-start | bytes 36872 | tf_op jit(solution)/shard_map/ppermute | solution.py:191
  188.7 16.6 %all-to-all-start.6 = ((bf16[32,24,256]{2,1,0:T(8,128)(2,1)}), bf16[32,24,256]{2,1,0:T(8,128)(2,1)}, u32[]{:S(2)}, u32[]{:S(2)}) async-start(bf16[32,24,256]{2,1,0:T(8,128)(2,1)} %broadcast_in_dim.221), calls=%async_computation.6 | async-start | bytes 786432 | tf_op jit(solution)/shard_map/all_to_all | solution.py:40
  205.3 7.3 %collective-permute-start.15 = (bf16[32,24,256]{2,1,0:T(8,128)(2,1)}, bf16[32,24,256]{2,1,0:T(8,128)(2,1)S(1)}, u32[]{:S(2)}, u32[]{:S(2)}) collective-permute-start(bf16[32,24,256]{2,1,0:T(8,128)(2,1)} %all-to-all-done.6), channel_id=1, source_target_pairs={{0,4},{4,0},{1,5},{5,1},{2,6},{6,2},{3,7},{7,3},{8,12},{12,8},{9,1... | collective-permute-start | bytes 1179656 | tf_op jit(solution)/shard_map/ppermute | solution.py:36
  212.6 1.7 copy-start.3
  214.9 3.0 %copy-start.9 = (bf16[96,2048]{1,0:T(8,128)(2,1)S(1)}, bf16[96,2048]{1,0:T(8,128)(2,1)}, u32[]{:S(2)}) copy-start(bf16[96,2048]{1,0:T(8,128)(2,1)} %copy-done.8) | copy-start | bytes 1179652
  214.9 3.0 %copy-start.37 = (f32[1,4096]{1,0:T(1,128)S(1)}, f32[1,4096]{1,0:T(1,128)}, u32[]{:S(2)}) copy-start(f32[1,4096]{1,0:T(1,128)} %param.12) | copy-start | bytes 49156
  215.8 4.1 %collective-permute-start.16 = (bf16[4,24,2048]{2,1,0:T(8,128)(2,1)S(1)}, bf16[4,24,2048]{2,1,0:T(8,128)(2,1)S(1)}, u32[]{:S(2)}, u32[]{:S(2)}) collective-permute-start(bf16[4,24,2048]{2,1,0:T(8,128)(2,1)S(1)} %select_convert_fusion), channel_id=1, source_target_pairs={{0,4},{4,0},{1,5},{5,1},{2,6},{6,2},{3,7},{7,3},{8,12},{12,8},{9,1... | collective-permute-start | bytes 1179656 | tf_op jit(solution)/shard_map/ppermute | solution.py:36
  220.1 6.5 %copy-start.11 = (bf16[12,8,8,256]{3,1,2,0:T(8,128)(2,1)S(1)}, bf16[12,8,8,256]{3,1,2,0:T(8,128)(2,1)}, u32[]{:S(2)}) copy-start(bf16[12,8,8,256]{3,1,2,0:T(8,128)(2,1)} %copy-done.10) | copy-start | bytes 1179652
  220.2 6.5 %copy-start.19 = (f32[96,224]{1,0:T(8,128)S(1)}, f32[96,224]{1,0:T(8,128)}, u32[]{:S(2)}) copy-start(f32[96,224]{1,0:T(8,128)} %copy-done.15) | copy-start | bytes 258052
  220.2 6.5 %copy-start.24 = (f32[96,224]{1,0:T(8,128)S(1)}, f32[96,224]{1,0:T(8,128)}, u32[]{:S(2)}) copy-start(f32[96,224]{1,0:T(8,128)} %copy-done.20) | copy-start | bytes 258052
  221.1 19.3 %all-to-all-start.7 = ((bf16[32,24,256]{2,1,0:T(8,128)(2,1)}), bf16[32,24,256]{2,1,0:T(8,128)(2,1)S(1)}, u32[]{:S(2)}, u32[]{:S(2)}) async-start(bf16[32,24,256]{2,1,0:T(8,128)(2,1)} %bitcast.53), calls=%async_computation.7 | async-start | bytes 786432 | tf_op jit(solution)/shard_map/all_to_all | solution.py:40
  226.7 13.9 %copy-start.35 = (bf16[24,256]{1,0:T(8,128)(2,1)S(1)}, bf16[24,256]{1,0:T(8,128)(2,1)}, u32[]{:S(2)}) copy-start(bf16[24,256]{1,0:T(8,128)(2,1)} %copy-done.34) | copy-start | bytes 36868
  226.7 13.9 %copy-start.39 = (bf16[24,256]{1,0:T(8,128)(2,1)S(1)}, bf16[24,256]{1,0:T(8,128)(2,1)}, u32[]{:S(2)}) copy-start(bf16[24,256]{1,0:T(8,128)(2,1)} %copy-done.38) | copy-start | bytes 36868
  226.7 13.9 %copy-start.45 = (f32[1,256]{1,0:T(1,128)S(1)}, f32[1,256]{1,0:T(1,128)}, u32[]{:S(2)}) copy-start(f32[1,256]{1,0:T(1,128)} %constant_dynamic-slice_fusion.6) | copy-start | bytes 3076
  226.7 13.9 %copy-start.50 = (pred[24]{0:T(512)(128)(4,1)S(1)}, pred[24]{0:T(512)(128)(4,1)}, u32[]{:S(2)}) copy-start(pred[24]{0:T(512)(128)(4,1)} %iota_compare_fusion.4) | copy-start | bytes 76
  226.7 13.9 %copy-start.52 = (pred[24]{0:T(512)(128)(4,1)S(1)}, pred[24]{0:T(512)(128)(4,1)}, u32[]{:S(2)}) copy-start(pred[24]{0:T(512)(128)(4,1)} %iota_compare_fusion.8) | copy-start | bytes 76
  226.7 13.9 %copy-start.55 = (f32[24]{0:T(128)S(1)}, f32[24]{0:T(128)}, u32[]{:S(2)}) copy-start(f32[24]{0:T(128)} %copy-done.53) | copy-start | bytes 292
  226.8 19.8 %copy-start.48 = (f32[96]{0:T(128)S(1)}, f32[96]{0:T(128)}, u32[]{:S(2)}) copy-start(f32[96]{0:T(128)} %copy-done.46) | copy-start | bytes 1156
  241.5 14.4 %all-to-all-start.8 = ((bf16[32,8,256]{2,1,0:T(8,128)(2,1)}), bf16[32,8,256]{2,1,0:T(8,128)(2,1)S(1)}, u32[]{:S(2)}, u32[]{:S(2)}) async-start(bf16[32,8,256]{2,1,0:T(8,128)(2,1)} %fusion.3), calls=%async_computation.8 | async-start | bytes 262144 | tf_op jit(solution)/shard_map/all_to_all | solution.py:40
  255.9 3.8 %collective-permute-start.17 = (bf16[8,2048]{1,0:T(8,128)(2,1)S(1)}, bf16[8,2048]{1,0:T(8,128)(2,1)S(1)}, u32[]{:S(2)}, u32[]{:S(2)}) collective-permute-start(bf16[8,2048]{1,0:T(8,128)(2,1)S(1)} %bitcast.230), channel_id=1, source_target_pairs={{0,4},{4,0},{1,5},{5,1},{2,6},{6,2},{3,7},{7,3},{8,12},{12,8},{9,1... | collective-permute-start | bytes 98312 | tf_op jit(solution)/shard_map/ppermute | solution.py:36
  (33 other events, 38.4 us)

commit v3 on v2

--- a/solution.py
+++ b/solution.py
@@ -66,22 +66,24 @@
 def gather_rows(hidden, top, counts, y, core):
     half = hidden.shape[-1] // 2
     own = jnp.concatenate([hidden, top], axis=0).reshape(8, half)
-    pick_own = lax.optimization_barrier(selection(counts, y, core))
-    pick_other = lax.optimization_barrier(selection(counts, y, 1 - core))
+    pick_own, pick_other, wanted = lax.optimization_barrier(
+        (selection(counts, y, core), selection(counts, y, 1 - core), wanted_rows(counts, y))
+    )
     mine, other = spread_rows(own)
     rows = (dot_nn(pick_own, mine) + dot_nn(pick_other, other)).astype(BF).reshape(2, 2, ROWS, half)
-    return jnp.concatenate([rows[0, 0], rows[0, 1]], axis=1), rows[1, 0], rows[1, 1]
+    return jnp.concatenate([rows[0, 0], rows[0, 1]], axis=1), rows[1, 0], rows[1, 1], wanted
 
 
 def wanted_rows(counts, y):
-    shape = (NZ, NY, 8, GROUP)
-    to_z, to_y, piece, row = (lax.broadcasted_iota(jnp.int32, shape, d) for d in range(4))
-    slot = to_z * NY * NC + to_y * NC + piece // 2
+    shape = (NZ * NY * 8, GROUP)
+    index, row = (lax.broadcasted_iota(jnp.int32, shape, d) for d in range(2))
+    place, piece = index // 8, index % 8
+    slot = place * NC + piece // 2
     micro = piece % 2
     limit = jnp.where(micro == 0, counts[0], counts[1])
     hit = (piece < 4) & (row_of(micro, slot) == y * GROUP + row) & (slot < limit)
     carry = (y == 0) & ((piece == 4) & (row == USED) | (piece == 5) & (row == USED + 1))
-    return (hit | carry).astype(BF).reshape(NZ * NY * 8, GROUP)
+    return (hit | carry).astype(BF)
 
 
 def on_device(hidden_in, grad_out, weight_gate, weight_up, weight_down, gain, counts):
@@ -107,11 +109,16 @@
         widths[axis] = (0, padded - units)
         return jnp.pad(x, widths)
 
-    both = jnp.concatenate([pad_units(gate_mat, 0), pad_units(up_mat, 0)], axis=0)
-    both_own, both_away = lax.optimization_barrier(halves(both))
-    down_own, down_away = lax.optimization_barrier(halves(pad_units(down_mat, 0)))
-
-    hidden, top_low, top_high = gather_rows(hidden_in[0, :, 0], grad_out[:, 0], counts, y, core)
+    gate_own, gate_away = halves(gate_mat)
+    up_own, up_away = halves(up_mat)
+    both_own = jnp.concatenate([pad_units(gate_own, 0), pad_units(up_own, 0)], axis=0)
+    both_away = jnp.concatenate([pad_units(gate_away, 0), pad_units(up_away, 0)], axis=0)
+    down_own, down_away = (pad_units(x, 0) for x in halves(down_mat))
+    both_own, both_away, down_own, down_away = lax.optimization_barrier(
+        (both_own, both_away, down_own, down_away)
+    )
+
+    hidden, top_low, top_high, wanted = gather_rows(hidden_in[0, :, 0], grad_out[:, 0], counts, y, core)
     values = hidden.astype(F32)
     inv_rms = lax.rsqrt(jnp.mean(values * values, axis=-1, keepdims=True) + 1e-05)
     normed = (values * inv_rms * gain_row).astype(BF)
@@ -158,6 +165,10 @@
         kept = partial_of(both_own, core * half)
         summed = (kept.astype(F32) + away.astype(F32)).astype(BF)
         pieces = summed.reshape(NY, GROUP, NZ, lanes).transpose(2, 0, 1, 3).reshape(NZ * NY, GROUP, lanes)
+        if last:
+            pieces, grad_gate, grad_up, mine, other = lax.optimization_barrier(
+                (pieces, grad_gate, grad_up, mine, other)
+            )
         total = jnp.sum(exchange(pieces).astype(F32), axis=0)
         row_sum = lax.dynamic_slice_in_dim(total[USED], y * GROUP, GROUP, 0)[:, None]
         grad_tile = (
@@ -172,7 +183,6 @@
             low = (gain_sum - high.astype(F32)).astype(BF)
             grad_tile = jnp.where(tile_row == USED, high, grad_tile)
             grad_tile = jnp.where(tile_row == USED + 1, low, grad_tile)
-            wanted = lax.optimization_barrier(wanted_rows(counts, y))
             sent = dot_nn(wanted, grad_tile).astype(BF).reshape(NZ * NY, 8, lanes)
             spread = exchange(sent)
             gate_grads = dot_tn(grad_gate[:, :units], normed).astype(BF)

time: 264 us -> 254 us (0.962)
  blocking collectives: 52.7 us -> 87 us
  local copies, waits for them, and re-layouts: 35 us -> 18.2 us
  starting transfers between devices: 68.6 us -> 57.3 us
  waiting for transfers between devices: 58.8 us -> 49.5 us
  other arithmetic: 25.2 us -> 19.8 us
    all_to_all x3 -> x5, blocking collectives: 52.7 us -> 87 us  [exchange(): return lax.all_to_all(x, PLANE, 0, 0, tiled=True)]
    all_to_all x5 -> x3, waiting for transfers between devices: 47.2 us -> 29.9 us  [exchange(): return lax.all_to_all(x, PLANE, 0, 0, tiled=True)]
    all_to_all x5 -> x3, starting transfers between devices: 29.2 us -> 17.8 us  [exchange(): return lax.all_to_all(x, PLANE, 0, 0, tiled=True)]
    iota x16 -> x0, local copies, waits for them, and re-layouts: 11.1 us -> none  [wanted_rows(): lax.broadcasted_iota(jnp.int32, shape, d)]
    ppermute x3, waiting for transfers between devices: 2.82 us -> 9.18 us  [on_device(): moved = lax.ppermute(grad_tile, 'section', [(NS - 1 - step, NS - 2 - step)])]
  transfers between devices with their start and end apart: 24 -> 22, of which waited for: 14 -> 13; matrix products, arithmetic and copies ran while one was open for 19% -> 12% of each run, Pallas kernels for 0% -> 0%
where the time goes in v3:
time: 254 us; the launch traced here: 252 us
  blocking collectives  87 us (34%)
  starting transfers between devices  57.3 us (23%)
  waiting for transfers between devices  49.5 us (19%)
  other arithmetic  19.8 us (8%)
  matrix products  18.4 us (7%)
  local copies, waits for them, and re-layouts  18.2 us (7%)
    all_to_all x5, blocking collectives, exchange(): return lax.all_to_all(x, PLANE, 0, 0, tiled=True)  87 us
    all_to_all x3, waiting for transfers between devices, exchange(): return lax.all_to_all(x, PLANE, 0, 0, tiled=True)  29.9 us
    ppermute x12, starting transfers between devices, swap_core(): return lax.ppermute(x, 'core', [(0, 1), (1, 0)])  22.3 us
    all_to_all x3, starting transfers between devices, exchange(): return lax.all_to_all(x, PLANE, 0, 0, tiled=True)  17.8 us
    ppermute x3, waiting for transfers between devices, on_device(): moved = lax.ppermute(grad_tile, 'section', [(NS - 1 - step, NS - 2 - step)])  9.18 us
    all_to_all x1, starting transfers between devices, spread_rows(): lax.all_to_all(jnp.broadcast_to(own[None], (NZ, count, half)), 'z', 0, 0,...  9 us
    dot_general x11, matrix products, dot_nn(): lax.dot_general(a, b, (((1,), (0,)), ((), ())), preferred_element_type=F32)  7.04 us
    ppermute x12, waiting for transfers between devices, swap_core(): return lax.ppermute(x, 'core', [(0, 1), (1, 0)])  6.64 us
  transfers between devices with their start and end apart: 22, of which 13 were waited for; matrix products, arithmetic and copies ran while one was open for 12% of the time, Pallas kernels for 0%

profile of v3, /device:TPU:1, one launch (start us, length us, event | category | flops | bytes accessed | tf_op | source)
XLA Modules:
  0.0 252.4 jit_solution(10984106684353610077)
XLA Ops:
  0.6 0.9 pad_maximum_fusion.13
  1.6 0.7 broadcast_in_dim.213
  2.3 9.0 %all-to-all-start = ((bf16[8,8,2048]{2,1,0:T(8,128)(2,1)}), bf16[8,8,2048]{2,1,0:T(8,128)(2,1)}, u32[]{:S(2)}, u32[]{:S(2)}) async-start(bf16[8,8,2048]{2,1,0:T(8,128)(2,1)} %broadcast_in_dim.213), calls=%async_computation | async-start | bytes 524288 | tf_op jit(solution)/shard_map/all_to_all | solution.py:45
  12.1 1.3 fusion.127
  14.7 2.2 fusion.50
  16.9 2.2 fusion.51
  19.1 2.4 fusion.70
  21.4 2.7 %dynamic-slice_bitcast_fusion = (bf16[224,2048]{1,0:T(8,128)(2,1)S(1)}, bf16[224,2048]{1,0:T(8,128)(2,1)S(1)}, bf16[224,2048]{1,0:T(8,128)(2,1)S(1)}, bf16[224,2048]{1,0:T(8,128)(2,1)}) fusion(bf16[1,224,4096]{2,1,0:T(8,128)(2,1)S(1)} %copy-done.16, s32[]{:T(128)S(6)} %select_n.343, s32[]{:T(128)S(6)} %select_n.342, bf16[1,224,4096]{2,1,0:T(8,128)(2,1)} %param.10), kind=kLoop, calls=%fused_computation.39 | loop fusion | bytes 7340040 | tf_op jit(solution)/shard_map/dynamic_slice | solution.py:101
  24.3 1.1 pad.50
  25.4 0.7 copy-done.14
  26.0 1.1 dynamic-slice_bitcast_fusion.3
  27.4 3.0 %collective-permute-start.2 = (bf16[8,8,2048]{2,1,0:T(8,128)(2,1)}, bf16[8,8,2048]{2,1,0:T(8,128)(2,1)S(1)}, u32[]{:S(2)}, u32[]{:S(2)}) collective-permute-start(bf16[8,8,2048]{2,1,0:T(8,128)(2,1)} %all-to-all-done), channel_id=1, source_target_pairs={{0,16},{8,24},{16,0},{24,8},{1,17},{9,25},{17,1},{25,9},{2,18},{10... | collective-permute-start | bytes 786440 | tf_op jit(solution)/shard_map/ppermute | solution.py:48
  30.4 0.8 collective-permute-start.1
  31.2 0.7 collective-permute-start
  31.9 1.7 fusion.5
  33.6 1.9 collective-permute-start.3
  35.4 0.7 collective-permute-done.2
  36.1 3.2 %collective-permute-start.6 = (bf16[8,8,2048]{2,1,0:T(8,128)(2,1)S(1)}, bf16[8,8,2048]{2,1,0:T(8,128)(2,1)S(1)}, u32[]{:S(2)}, u32[]{:S(2)}) collective-permute-start(bf16[8,8,2048]{2,1,0:T(8,128)(2,1)S(1)} %collective-permute-done.2), channel_id=1, source_target_pairs={{0,4},{4,0},{1,5},{5,1},{2,6},{6,2},{3,7},{7,3},{8,12},{12,8},{9,1... | collective-permute-start | bytes 786440 | tf_op jit(solution)/shard_map/ppermute | solution.py:36
  39.3 3.1 %collective-permute-done.1 = bf16[8,8,2048]{2,1,0:T(8,128)(2,1)S(1)} collective-permute-done((bf16[8,8,2048]{2,1,0:T(8,128)(2,1)}, bf16[8,8,2048]{2,1,0:T(8,128)(2,1)S(1)}, u32[]{:S(2)}, u32[]{:S(2)}) %collective-permute-start.1) | collective-permute-done | bytes 262176 | tf_op jit(solution)/shard_map/ppermute | solution.py:48
  42.5 1.4 collective-permute-start.5
  43.9 1.6 fusion.11
  46.6 1.4 copy-done.17
  47.9 0.7 fusion.8
  48.7 0.8 fusion.76
  51.3 0.8 collective-permute-start.7
  52.5 0.9 collective-permute-done.7
  53.7 0.8 copy.12
  54.5 9.3 %all-to-all-start.1 = ((bf16[32,24,256]{2,1,0:T(8,128)(2,1)}), bf16[32,24,256]{2,1,0:T(8,128)(2,1)}, u32[]{:S(2)}, u32[]{:S(2)}) async-start(bf16[32,24,256]{2,1,0:T(8,128)(2,1)} %bitcast.198), calls=%async_computation.1 | async-start | bytes 786432 | tf_op jit(solution)/shard_map/all_to_all | solution.py:40
  64.9 0.7 dynamic-slice.15
  65.6 12.1 %all-to-all-done.1 = bf16[32,24,256]{2,1,0:T(8,128)(2,1)} async-done(((bf16[32,24,256]{2,1,0:T(8,128)(2,1)}), bf16[32,24,256]{2,1,0:T(8,128)(2,1)}, u32[]{:S(2)}, u32[]{:S(2)}) %all-to-all-start.1) | async-done | bytes 393248 | tf_op jit(solution)/shard_map/all_to_all | solution.py:40
  77.8 1.1 convert_reduce_fusion.3
  78.9 1.5 select_convert_fusion.11
  80.4 1.2 collective-permute-start.8
  81.6 0.8 bitcast_select_fusion
  82.5 17.4 %all_to_all.45 = bf16[32,24,256]{2,1,0:T(8,128)(2,1)S(1)} all-to-all(bf16[32,24,256]{2,1,0:T(8,128)(2,1)S(1)} %broadcast_in_dim.217), channel_id=1, replica_groups=mesh['z'=8,'y'=4,'core'=2,'section'=4] {'z','y'}, dimensions={0} | all-to-all | bytes 786432 | tf_op jit(solution)/shard_map/all_to_all | solution.py:40
  99.9 3.6 %collective-permute-start.9 = (bf16[32,24,256]{2,1,0:T(8,128)(2,1)S(1)}, bf16[32,24,256]{2,1,0:T(8,128)(2,1)S(1)}, u32[]{:S(2)}, u32[]{:S(2)}) collective-permute-start(bf16[32,24,256]{2,1,0:T(8,128)(2,1)S(1)} %all_to_all.45), channel_id=1, source_target_pairs={{0,4},{4,0},{1,5},{5,1},{2,6},{6,2},{3,7},{7,3},{8,12},{12,8},{9,1... | collective-permute-start | bytes 1179656 | tf_op jit(solution)/shard_map/ppermute | solution.py:36
  107.3 1.1 collective-permute-done.10
  108.8 18.1 %all_to_all.46 = bf16[32,24,256]{2,1,0:T(8,128)(2,1)S(1)} all-to-all(bf16[32,24,256]{2,1,0:T(8,128)(2,1)S(1)} %bitcast.211), channel_id=1, replica_groups=mesh['z'=8,'y'=4,'core'=2,'section'=4] {'z','y'}, dimensions={0} | all-to-all | bytes 786432 | tf_op jit(solution)/shard_map/all_to_all | solution.py:40
  127.1 0.7 select_convert_fusion.10
  127.8 1.2 collective-permute-start.11
  129.1 17.1 %all_to_all.47 = bf16[32,24,256]{2,1,0:T(8,128)(2,1)S(1)} all-to-all(bf16[32,24,256]{2,1,0:T(8,128)(2,1)S(1)} %broadcast_in_dim.219), channel_id=1, replica_groups=mesh['z'=8,'y'=4,'core'=2,'section'=4] {'z','y'}, dimensions={0} | all-to-all | bytes 786432 | tf_op jit(solution)/shard_map/all_to_all | solution.py:40
  146.2 3.5 %collective-permute-start.12 = (bf16[32,24,256]{2,1,0:T(8,128)(2,1)S(1)}, bf16[32,24,256]{2,1,0:T(8,128)(2,1)S(1)}, u32[]{:S(2)}, u32[]{:S(2)}) collective-permute-start(bf16[32,24,256]{2,1,0:T(8,128)(2,1)S(1)} %all_to_all.47), channel_id=1, source_target_pairs={{0,4},{4,0},{1,5},{5,1},{2,6},{6,2},{3,7},{7,3},{8,12},{12,8},{9,1... | collective-permute-start | bytes 1179656 | tf_op jit(solution)/shard_map/ppermute | solution.py:36
  153.6 1.1 collective-permute-done.13
  155.1 18.1 %all_to_all.48 = bf16[32,24,256]{2,1,0:T(8,128)(2,1)S(1)} all-to-all(bf16[32,24,256]{2,1,0:T(8,128)(2,1)S(1)} %bitcast.214), channel_id=1, replica_groups=mesh['z'=8,'y'=4,'core'=2,'section'=4] {'z','y'}, dimensions={0} | all-to-all | bytes 786432 | tf_op jit(solution)/shard_map/all_to_all | solution.py:40
  173.3 0.7 select_convert_fusion.9
  174.0 1.3 collective-permute-start.14
  175.3 9.2 %collective-permute-done.14 = bf16[24,256]{1,0:T(8,128)(2,1)} collective-permute-done((bf16[24,256]{1,0:T(8,128)(2,1)}, bf16[24,256]{1,0:T(8,128)(2,1)}, u32[]{:S(2)}, u32[]{:S(2)}) %collective-permute-start.14) | collective-permute-done | bytes 12320 | tf_op jit(solution)/shard_map/ppermute | solution.py:201
  184.5 0.7 broadcast_select_fusion.7
  185.2 16.2 %all_to_all.49 = bf16[32,24,256]{2,1,0:T(8,128)(2,1)S(1)} all-to-all(bf16[32,24,256]{2,1,0:T(8,128)(2,1)S(1)} %broadcast_in_dim.221), channel_id=1, replica_groups=mesh['z'=8,'y'=4,'core'=2,'section'=4] {'z','y'}, dimensions={0} | all-to-all | bytes 786432 | tf_op jit(solution)/shard_map/all_to_all | solution.py:40
  201.5 4.3 %collective-permute-start.15 = (bf16[32,24,256]{2,1,0:T(8,128)(2,1)S(1)}, bf16[32,24,256]{2,1,0:T(8,128)(2,1)S(1)}, u32[]{:S(2)}, u32[]{:S(2)}) collective-permute-start(bf16[32,24,256]{2,1,0:T(8,128)(2,1)S(1)} %all_to_all.49), channel_id=1, source_target_pairs={{0,4},{4,0},{1,5},{5,1},{2,6},{6,2},{3,7},{7,3},{8,12},{12,8},{9,1... | collective-permute-start | bytes 1179656 | tf_op jit(solution)/shard_map/ppermute | solution.py:36
  205.8 1.1 fusion.26
  210.1 0.7 multiply_reduce_fusion.2
  211.0 1.7 collective-permute-done.16
  213.1 0.8 copy.21
  213.9 4.0 %all-to-all-start.7 = ((bf16[32,24,256]{2,1,0:T(8,128)(2,1)}), bf16[32,24,256]{2,1,0:T(8,128)(2,1)S(1)}, u32[]{:S(2)}, u32[]{:S(2)}) async-start(bf16[32,24,256]{2,1,0:T(8,128)(2,1)} %bitcast.58), calls=%async_computation.7 | async-start | bytes 786432 | tf_op jit(solution)/shard_map/all_to_all | solution.py:40
  218.0 1.9 convolution_convert_fusion.2
  220.1 1.9 convolution_convert_fusion
  222.0 10.3 %all-to-all-done.7 = bf16[32,24,256]{2,1,0:T(8,128)(2,1)S(1)} async-done(((bf16[32,24,256]{2,1,0:T(8,128)(2,1)}), bf16[32,24,256]{2,1,0:T(8,128)(2,1)S(1)}, u32[]{:S(2)}, u32[]{:S(2)}) %all-to-all-start.7) | async-done | bytes 393248 | tf_op jit(solution)/shard_map/all_to_all | solution.py:40
  232.5 0.9 fusion.10
  233.4 4.5 %all-to-all-start.8 = ((bf16[32,8,256]{2,1,0:T(8,128)(2,1)}), bf16[32,8,256]{2,1,0:T(8,128)(2,1)S(1)}, u32[]{:S(2)}, u32[]{:S(2)}) async-start(bf16[32,8,256]{2,1,0:T(8,128)(2,1)} %fusion.10), calls=%async_computation.8 | async-start | bytes 262144 | tf_op jit(solution)/shard_map/all_to_all | solution.py:40
  237.9 1.9 convolution_convert_fusion.1
  239.9 7.4 %all-to-all-done.8 = bf16[32,8,256]{2,1,0:T(8,128)(2,1)S(1)} async-done(((bf16[32,8,256]{2,1,0:T(8,128)(2,1)}), bf16[32,8,256]{2,1,0:T(8,128)(2,1)S(1)}, u32[]{:S(2)}, u32[]{:S(2)}) %all-to-all-start.8) | async-done | bytes 131104 | tf_op jit(solution)/shard_map/all_to_all | solution.py:40
  247.3 3.0 %collective-permute-start.17 = (bf16[8,2048]{1,0:T(8,128)(2,1)S(1)}, bf16[8,2048]{1,0:T(8,128)(2,1)S(1)}, u32[]{:S(2)}, u32[]{:S(2)}) collective-permute-start(bf16[8,2048]{1,0:T(8,128)(2,1)S(1)} %bitcast.239), channel_id=1, source_target_pairs={{0,4},{4,0},{1,5},{5,1},{2,6},{6,2},{3,7},{7,3},{8,12},{12,8},{9,1... | collective-permute-start | bytes 98312 | tf_op jit(solution)/shard_map/ppermute | solution.py:36
  250.2 0.9 collective-permute-done.17
  (279 shorter events, 20.5 us)
Async XLA Ops:
  0.6 20.8 %copy-start.16 = (bf16[1,224,4096]{2,1,0:T(8,128)(2,1)S(1)}, bf16[1,224,4096]{2,1,0:T(8,128)(2,1)}, u32[]{:S(2)}) copy-start(bf16[1,224,4096]{2,1,0:T(8,128)(2,1)} %param.11) | copy-start | bytes 5505028
  2.3 25.1 %all-to-all-start = ((bf16[8,8,2048]{2,1,0:T(8,128)(2,1)}), bf16[8,8,2048]{2,1,0:T(8,128)(2,1)}, u32[]{:S(2)}, u32[]{:S(2)}) async-start(bf16[8,8,2048]{2,1,0:T(8,128)(2,1)} %broadcast_in_dim.213), calls=%async_computation | async-start | bytes 524288 | tf_op jit(solution)/shard_map/all_to_all | solution.py:45
  11.5 12.7 %copy-start.47 = (pred[24]{0:T(512)(128)(4,1)}, pred[24]{0:T(512)(128)(4,1)S(1)}, u32[]{:S(2)}) copy-start(pred[24]{0:T(512)(128)(4,1)S(1)} %get-tuple-element.85) | copy-start | bytes 76
  11.5 12.7 %copy-start.53 = (pred[24]{0:T(512)(128)(4,1)}, pred[24]{0:T(512)(128)(4,1)S(1)}, u32[]{:S(2)}) copy-start(pred[24]{0:T(512)(128)(4,1)S(1)} %get-tuple-element.84) | copy-start | bytes 76
  24.2 1.9 copy-start.14
  27.4 16.6 %copy-start.38 = (bf16[384,256]{1,0:T(8,128)(2,1)S(1)}, bf16[384,256]{1,0:T(8,128)(2,1)}, u32[]{:S(2)}) copy-start(bf16[384,256]{1,0:T(8,128)(2,1)} %fusion.50) | copy-start | bytes 589828
  27.4 8.7 %collective-permute-start.2 = (bf16[8,8,2048]{2,1,0:T(8,128)(2,1)}, bf16[8,8,2048]{2,1,0:T(8,128)(2,1)S(1)}, u32[]{:S(2)}, u32[]{:S(2)}) collective-permute-start(bf16[8,8,2048]{2,1,0:T(8,128)(2,1)} %all-to-all-done), channel_id=1, source_target_pairs={{0,16},{8,24},{16,0},{24,8},{1,17},{9,25},{17,1},{25,9},{2,18},{10... | collective-permute-start | bytes 786440 | tf_op jit(solution)/shard_map/ppermute | solution.py:48
  30.4 12.1 %collective-permute-start.1 = (bf16[8,8,2048]{2,1,0:T(8,128)(2,1)}, bf16[8,8,2048]{2,1,0:T(8,128)(2,1)S(1)}, u32[]{:S(2)}, u32[]{:S(2)}) collective-permute-start(bf16[8,8,2048]{2,1,0:T(8,128)(2,1)} %all-to-all-done), channel_id=1, source_target_pairs={{0,24},{8,0},{16,8},{24,16},{1,25},{9,1},{17,9},{25,17},{2,26},{10... | collective-permute-start | bytes 786440 | tf_op jit(solution)/shard_map/ppermute | solution.py:48
  31.2 12.8 %collective-permute-start = (bf16[8,8,2048]{2,1,0:T(8,128)(2,1)}, bf16[8,8,2048]{2,1,0:T(8,128)(2,1)S(1)}, u32[]{:S(2)}, u32[]{:S(2)}) collective-permute-start(bf16[8,8,2048]{2,1,0:T(8,128)(2,1)} %all-to-all-done), channel_id=1, source_target_pairs={{0,8},{8,16},{16,24},{24,0},{1,9},{9,17},{17,25},{25,1},{2,10},{10... | collective-permute-start | bytes 786440 | tf_op jit(solution)/shard_map/ppermute | solution.py:48
  33.5 17.1 %copy-start = (bf16[512,2048]{1,0:T(8,128)(2,1)}, bf16[512,2048]{1,0:T(8,128)(2,1)S(1)}, u32[]{:S(2)}) copy-start(bf16[512,2048]{1,0:T(8,128)(2,1)S(1)} %fusion.5) | copy-start | bytes 6291460
  33.6 12.0 %collective-permute-start.3 = (bf16[8,8,2048]{2,1,0:T(8,128)(2,1)}, bf16[8,8,2048]{2,1,0:T(8,128)(2,1)S(1)}, u32[]{:S(2)}, u32[]{:S(2)}) collective-permute-start(bf16[8,8,2048]{2,1,0:T(8,128)(2,1)} %all-to-all-done), channel_id=1, source_target_pairs={{0,4},{4,0},{1,5},{5,1},{2,6},{6,2},{3,7},{7,3},{8,12},{12,8},{9,1... | collective-permute-start | bytes 786440 | tf_op jit(solution)/shard_map/ppermute | solution.py:36
  36.1 9.4 %collective-permute-start.6 = (bf16[8,8,2048]{2,1,0:T(8,128)(2,1)S(1)}, bf16[8,8,2048]{2,1,0:T(8,128)(2,1)S(1)}, u32[]{:S(2)}, u32[]{:S(2)}) collective-permute-start(bf16[8,8,2048]{2,1,0:T(8,128)(2,1)S(1)} %collective-permute-done.2), channel_id=1, source_target_pairs={{0,4},{4,0},{1,5},{5,1},{2,6},{6,2},{3,7},{7,3},{8,12},{12,8},{9,1... | collective-permute-start | bytes 786440 | tf_op jit(solution)/shard_map/ppermute | solution.py:36
  42.5 3.1 %collective-permute-start.5 = (bf16[8,8,2048]{2,1,0:T(8,128)(2,1)S(1)}, bf16[8,8,2048]{2,1,0:T(8,128)(2,1)S(1)}, u32[]{:S(2)}, u32[]{:S(2)}) collective-permute-start(bf16[8,8,2048]{2,1,0:T(8,128)(2,1)S(1)} %collective-permute-done.1), channel_id=1, source_target_pairs={{0,4},{4,0},{1,5},{5,1},{2,6},{6,2},{3,7},{7,3},{8,12},{12,8},{9,1... | collective-permute-start | bytes 786440 | tf_op jit(solution)/shard_map/ppermute | solution.py:36
  43.9 1.6 collective-permute-start.4
  43.9 1.6 copy-start.29
  46.2 1.8 copy-start.17
  46.2 1.8 copy-start.42
  46.3 2.4 copy-start.8
  46.3 3.3 %copy-start.18 = (bf16[1,1,96,2048]{3,2,1,0:T(8,128)(2,1)}, bf16[1,1,96,2048]{3,2,1,0:T(8,128)(2,1)S(1)}, u32[]{:S(2)}) copy-start(bf16[1,1,96,2048]{3,2,1,0:T(8,128)(2,1)S(1)} %get-tuple-element.61) | copy-start | bytes 1179652
  46.3 2.4 copy-start.15
  46.6 2.9 %copy-start.55 = (f32[96]{0:T(128)}, f32[96]{0:T(128)S(1)}, u32[]{:S(2)}) copy-start(f32[96]{0:T(128)S(1)} %add_rsqrt_fusion) | copy-start | bytes 1156
  49.5 1.6 copy-start.24
  51.3 2.1 collective-permute-start.7
  54.5 23.2 %all-to-all-start.1 = ((bf16[32,24,256]{2,1,0:T(8,128)(2,1)}), bf16[32,24,256]{2,1,0:T(8,128)(2,1)}, u32[]{:S(2)}, u32[]{:S(2)}) async-start(bf16[32,24,256]{2,1,0:T(8,128)(2,1)} %bitcast.198), calls=%async_computation.1 | async-start | bytes 786432 | tf_op jit(solution)/shard_map/all_to_all | solution.py:40
  65.6 38.7 %copy-start.61 = (f32[24]{0:T(128)}, f32[24]{0:T(128)S(1)}, u32[]{:S(2)}) copy-start(f32[24]{0:T(128)S(1)} %dynamic-slice.15) | copy-start | bytes 292
  80.4 1.2 collective-permute-start.8
  99.9 4.9 %collective-permute-start.9 = (bf16[32,24,256]{2,1,0:T(8,128)(2,1)S(1)}, bf16[32,24,256]{2,1,0:T(8,128)(2,1)S(1)}, u32[]{:S(2)}, u32[]{:S(2)}) collective-permute-start(bf16[32,24,256]{2,1,0:T(8,128)(2,1)S(1)} %all_to_all.45), channel_id=1, source_target_pairs={{0,4},{4,0},{1,5},{5,1},{2,6},{6,2},{3,7},{7,3},{8,12},{12,8},{9,1... | collective-permute-start | bytes 1179656 | tf_op jit(solution)/shard_map/ppermute | solution.py:36
  104.3 1.7 copy-start.1
  106.6 1.8 collective-permute-start.10
  108.4 18.7 %copy-start.40 = (bf16[24,256]{1,0:T(8,128)(2,1)S(1)}, bf16[24,256]{1,0:T(8,128)(2,1)}, u32[]{:S(2)}) copy-start(bf16[24,256]{1,0:T(8,128)(2,1)} %get-tuple-element.51) | copy-start | bytes 36868
  108.4 18.7 %copy-start.50 = (f32[1,256]{1,0:T(1,128)S(1)}, f32[1,256]{1,0:T(1,128)}, u32[]{:S(2)}) copy-start(f32[1,256]{1,0:T(1,128)} %constant_dynamic-slice_fusion.4) | copy-start | bytes 3076
  108.4 18.7 %copy-start.58 = (pred[24]{0:T(512)(128)(4,1)S(1)}, pred[24]{0:T(512)(128)(4,1)}, u32[]{:S(2)}) copy-start(pred[24]{0:T(512)(128)(4,1)} %iota_compare_fusion.6) | copy-start | bytes 76
  108.4 18.7 %copy-start.62 = (f32[24]{0:T(128)S(1)}, f32[24]{0:T(128)}, u32[]{:S(2)}) copy-start(f32[24]{0:T(128)} %copy-done.61) | copy-start | bytes 292
  127.8 1.2 collective-permute-start.11
  129.0 44.3 %copy-start.39 = (bf16[24,256]{1,0:T(8,128)(2,1)}, bf16[24,256]{1,0:T(8,128)(2,1)S(1)}, u32[]{:S(2)}) copy-start(bf16[24,256]{1,0:T(8,128)(2,1)S(1)} %broadcast_select_fusion.6) | copy-start | bytes 36868
  146.2 4.9 %collective-permute-start.12 = (bf16[32,24,256]{2,1,0:T(8,128)(2,1)S(1)}, bf16[32,24,256]{2,1,0:T(8,128)(2,1)S(1)}, u32[]{:S(2)}, u32[]{:S(2)}) collective-permute-start(bf16[32,24,256]{2,1,0:T(8,128)(2,1)S(1)} %all_to_all.47), channel_id=1, source_target_pairs={{0,4},{4,0},{1,5},{5,1},{2,6},{6,2},{3,7},{7,3},{8,12},{12,8},{9,1... | collective-permute-start | bytes 1179656 | tf_op jit(solution)/shard_map/ppermute | solution.py:36
  150.0 1.4 copy-start.6
  150.6 1.7 copy-start.2
  152.9 1.8 collective-permute-start.13
  154.7 18.6 %copy-start.41 = (bf16[24,256]{1,0:T(8,128)(2,1)S(1)}, bf16[24,256]{1,0:T(8,128)(2,1)}, u32[]{:S(2)}) copy-start(bf16[24,256]{1,0:T(8,128)(2,1)} %get-tuple-element.51) | copy-start | bytes 36868
  154.7 18.6 %copy-start.51 = (f32[1,256]{1,0:T(1,128)S(1)}, f32[1,256]{1,0:T(1,128)}, u32[]{:S(2)}) copy-start(f32[1,256]{1,0:T(1,128)} %constant_dynamic-slice_fusion.4) | copy-start | bytes 3076
  154.7 18.6 %copy-start.59 = (pred[24]{0:T(512)(128)(4,1)S(1)}, pred[24]{0:T(512)(128)(4,1)}, u32[]{:S(2)}) copy-start(pred[24]{0:T(512)(128)(4,1)} %iota_compare_fusion.6) | copy-start | bytes 76
  154.7 18.6 %copy-start.63 = (f32[24]{0:T(128)S(1)}, f32[24]{0:T(128)}, u32[]{:S(2)}) copy-start(f32[24]{0:T(128)} %copy-done.61) | copy-start | bytes 292
  174.0 10.5 %collective-permute-start.14 = (bf16[24,256]{1,0:T(8,128)(2,1)}, bf16[24,256]{1,0:T(8,128)(2,1)}, u32[]{:S(2)}, u32[]{:S(2)}) collective-permute-start(bf16[24,256]{1,0:T(8,128)(2,1)} %select_convert_fusion.9), channel_id=1, source_target_pairs={{1,0},{5,4},{9,8},{13,12},{17,16},{21,20},{25,24},{29,28},{33,32},... | collective-permute-start | bytes 36872 | tf_op jit(solution)/shard_map/ppermute | solution.py:201
  185.2 16.3 %copy-start.45 = (bf16[24,256]{1,0:T(8,128)(2,1)}, bf16[24,256]{1,0:T(8,128)(2,1)S(1)}, u32[]{:S(2)}) copy-start(bf16[24,256]{1,0:T(8,128)(2,1)S(1)} %broadcast_select_fusion.7) | copy-start | bytes 36868
  201.5 6.3 %collective-permute-start.15 = (bf16[32,24,256]{2,1,0:T(8,128)(2,1)S(1)}, bf16[32,24,256]{2,1,0:T(8,128)(2,1)S(1)}, u32[]{:S(2)}, u32[]{:S(2)}) collective-permute-start(bf16[32,24,256]{2,1,0:T(8,128)(2,1)S(1)} %all_to_all.49), channel_id=1, source_target_pairs={{0,4},{4,0},{1,5},{5,1},{2,6},{6,2},{3,7},{7,3},{8,12},{12,8},{9,1... | collective-permute-start | bytes 1179656 | tf_op jit(solution)/shard_map/ppermute | solution.py:36
  207.7 1.8 copy-start.3
  208.6 1.5 copy-start.56
  210.9 1.8 collective-permute-start.16
  212.7 5.2 %copy-start.9 = (bf16[96,2048]{1,0:T(8,128)(2,1)S(1)}, bf16[96,2048]{1,0:T(8,128)(2,1)}, u32[]{:S(2)}) copy-start(bf16[96,2048]{1,0:T(8,128)(2,1)} %copy-done.8) | copy-start | bytes 1179652
  212.7 5.2 %copy-start.43 = (f32[1,4096]{1,0:T(1,128)S(1)}, f32[1,4096]{1,0:T(1,128)}, u32[]{:S(2)}) copy-start(f32[1,4096]{1,0:T(1,128)} %param.12) | copy-start | bytes 49156
  213.1 6.9 %copy-start.11 = (bf16[12,8,8,256]{3,1,2,0:T(8,128)(2,1)S(1)}, bf16[12,8,8,256]{3,1,2,0:T(8,128)(2,1)}, u32[]{:S(2)}) copy-start(bf16[12,8,8,256]{3,1,2,0:T(8,128)(2,1)} %copy-done.10) | copy-start | bytes 1179652
  213.1 6.9 %copy-start.13 = (bf16[12,8,8,256]{3,1,2,0:T(8,128)(2,1)S(1)}, bf16[12,8,8,256]{3,1,2,0:T(8,128)(2,1)}, u32[]{:S(2)}) copy-start(bf16[12,8,8,256]{3,1,2,0:T(8,128)(2,1)} %copy-done.12) | copy-start | bytes 1179652
  213.9 18.4 %all-to-all-start.7 = ((bf16[32,24,256]{2,1,0:T(8,128)(2,1)}), bf16[32,24,256]{2,1,0:T(8,128)(2,1)S(1)}, u32[]{:S(2)}, u32[]{:S(2)}) async-start(bf16[32,24,256]{2,1,0:T(8,128)(2,1)} %bitcast.58), calls=%async_computation.7 | async-start | bytes 786432 | tf_op jit(solution)/shard_map/all_to_all | solution.py:40
  218.0 2.1 copy-start.23
  218.0 2.1 copy-start.28
  219.9 12.5 %copy-start.44 = (bf16[256,24]{1,0:T(8,128)(2,1)S(1)}, bf16[256,24]{1,0:T(8,128)(2,1)}, u32[]{:S(2)}) copy-start(bf16[256,24]{1,0:T(8,128)(2,1)} %fusion.70) | copy-start | bytes 36868
  219.9 12.5 %copy-start.46 = (bf16[24,256]{1,0:T(8,128)(2,1)S(1)}, bf16[24,256]{1,0:T(8,128)(2,1)}, u32[]{:S(2)}) copy-start(bf16[24,256]{1,0:T(8,128)(2,1)} %copy-done.45) | copy-start | bytes 36868
  220.0 12.5 %copy-start.52 = (f32[1,256]{1,0:T(1,128)S(1)}, f32[1,256]{1,0:T(1,128)}, u32[]{:S(2)}) copy-start(f32[1,256]{1,0:T(1,128)} %constant_dynamic-slice_fusion.4) | copy-start | bytes 3076
  220.0 12.5 %copy-start.60 = (pred[24]{0:T(512)(128)(4,1)S(1)}, pred[24]{0:T(512)(128)(4,1)}, u32[]{:S(2)}) copy-start(pred[24]{0:T(512)(128)(4,1)} %iota_compare_fusion.6) | copy-start | bytes 76
  220.0 12.5 %copy-start.64 = (f32[24]{0:T(128)S(1)}, f32[24]{0:T(128)}, u32[]{:S(2)}) copy-start(f32[24]{0:T(128)} %copy-done.61) | copy-start | bytes 292
  220.1 17.9 %copy-start.57 = (f32[96]{0:T(128)S(1)}, f32[96]{0:T(128)}, u32[]{:S(2)}) copy-start(f32[96]{0:T(128)} %copy-done.55) | copy-start | bytes 1156
  233.4 13.8 %all-to-all-start.8 = ((bf16[32,8,256]{2,1,0:T(8,128)(2,1)}), bf16[32,8,256]{2,1,0:T(8,128)(2,1)S(1)}, u32[]{:S(2)}, u32[]{:S(2)}) async-start(bf16[32,8,256]{2,1,0:T(8,128)(2,1)} %fusion.10), calls=%async_computation.8 | async-start | bytes 262144 | tf_op jit(solution)/shard_map/all_to_all | solution.py:40
  247.3 3.8 %collective-permute-start.17 = (bf16[8,2048]{1,0:T(8,128)(2,1)S(1)}, bf16[8,2048]{1,0:T(8,128)(2,1)S(1)}, u32[]{:S(2)}, u32[]{:S(2)}) collective-permute-start(bf16[8,2048]{1,0:T(8,128)(2,1)S(1)} %bitcast.239), channel_id=1, source_target_pairs={{0,4},{4,0},{1,5},{5,1},{2,6},{6,2},{3,7},{7,3},{8,12},{12,8},{9,1... | collective-permute-start | bytes 98312 | tf_op jit(solution)/shard_map/ppermute | solution.py:36
  (23 other events, 29.7 us)

commit v4 on v3

--- a/solution.py
+++ b/solution.py
@@ -40,18 +40,19 @@
     return lax.all_to_all(x, PLANE, 0, 0, tiled=True)
 
 
-def spread_rows(own):
+def spread_rows(own, weights):
     count, half = own.shape
     along_z = lax.all_to_all(jnp.broadcast_to(own[None], (NZ, count, half)), "z", 0, 0, tiled=True)
+    along_z, weights = lax.optimization_barrier((along_z, weights))
     shifted = [along_z]
     for by in (1, 3, 2):
         shifted.append(lax.ppermute(along_z, "y", [(i, (i + by) % NY) for i in range(NY)]))
     swapped = [swap_core(x) for x in shifted]
     join = lambda xs: jnp.concatenate([x.reshape(NZ * count, half) for x in xs], axis=0)
-    return join(shifted), join(swapped)
-
-
-def selection(counts, y, core):
+    return join(shifted), join(swapped), weights
+
+
+def selection(counts, y, core, first_half):
     shape = (2, 2, ROWS, NY, NZ, 8)
     at = lambda dim: lax.broadcasted_iota(jnp.int32, shape, dim)
     kind, part, row, shift, z, piece = (at(d) for d in range(6))
@@ -59,19 +60,19 @@
     slot = z * NY * NC + ((y - by + NY) % NY) * NC + core
     micro = (piece // 2) % 2
     limit = jnp.where(micro == 0, counts[0], counts[1])
-    hit = (row_of(micro, slot) == row) & (slot < limit) & (piece // 4 == kind) & (piece % 2 == part)
+    hit = (row_of(micro, slot) == row) & (slot < limit) & (piece // 4 == kind) & (piece % 2 == (part ^ first_half))
     return hit.astype(BF).reshape(4 * ROWS, NY * NZ * 8)
 
 
-def gather_rows(hidden, top, counts, y, core):
+def gather_rows(hidden, top, weights, counts, y, core):
     half = hidden.shape[-1] // 2
     own = jnp.concatenate([hidden, top], axis=0).reshape(8, half)
     pick_own, pick_other, wanted = lax.optimization_barrier(
-        (selection(counts, y, core), selection(counts, y, 1 - core), wanted_rows(counts, y))
-    )
-    mine, other = spread_rows(own)
+        (selection(counts, y, core, core), selection(counts, y, 1 - core, core), wanted_rows(counts, y))
+    )
+    mine, other, weights = spread_rows(own, weights)
     rows = (dot_nn(pick_own, mine) + dot_nn(pick_other, other)).astype(BF).reshape(2, 2, ROWS, half)
-    return jnp.concatenate([rows[0, 0], rows[0, 1]], axis=1), rows[1, 0], rows[1, 1], wanted
+    return (rows[0, 0], rows[0, 1]), (rows[1, 0], rows[1, 1]), wanted, weights
 
 
 def wanted_rows(counts, y):
@@ -101,44 +102,49 @@
             lax.dynamic_slice_in_dim(x, (1 - core) * half, half, 1),
         )
 
+    def whole(own, away):
+        return jnp.concatenate(
+            [jnp.where(core == 0, own, away), jnp.where(core == 0, away, own)], axis=1
+        )
+
     units = gate_mat.shape[0]
     padded = -(-units // 256) * 256
 
-    def pad_units(x, axis):
-        widths = [(0, 0), (0, 0)]
-        widths[axis] = (0, padded - units)
-        return jnp.pad(x, widths)
-
+    def pad_units(x):
+        return jnp.pad(x, ((0, padded - units), (0, 0)))
+
+    hidden, (mine, other), wanted, (gate_mat, up_mat, down_mat) = gather_rows(
+        hidden_in[0, :, 0], grad_out[:, 0], (gate_mat, up_mat, down_mat), counts, y, core
+    )
     gate_own, gate_away = halves(gate_mat)
     up_own, up_away = halves(up_mat)
-    both_own = jnp.concatenate([pad_units(gate_own, 0), pad_units(up_own, 0)], axis=0)
-    both_away = jnp.concatenate([pad_units(gate_away, 0), pad_units(up_away, 0)], axis=0)
-    down_own, down_away = (pad_units(x, 0) for x in halves(down_mat))
+    both_own = jnp.concatenate([pad_units(gate_own), pad_units(up_own)], axis=0)
+    both_away = jnp.concatenate([pad_units(gate_away), pad_units(up_away)], axis=0)
+    down_own, down_away = (pad_units(x) for x in halves(down_mat))
     both_own, both_away, down_own, down_away = lax.optimization_barrier(
         (both_own, both_away, down_own, down_away)
     )
 
-    hidden, top_low, top_high, wanted = gather_rows(hidden_in[0, :, 0], grad_out[:, 0], counts, y, core)
-    values = hidden.astype(F32)
-    inv_rms = lax.rsqrt(jnp.mean(values * values, axis=-1, keepdims=True) + 1e-05)
-    normed = (values * inv_rms * gain_row).astype(BF)
-    gate_pre = dot_nt(normed, gate_mat)
-    up_pre = dot_nt(normed, up_mat)
+    values = [x.astype(F32) for x in hidden]
+    squares = sum(jnp.sum(x * x, axis=-1, keepdims=True) for x in values)
+    inv_rms = lax.rsqrt(squares / width + 1e-05)
+    gain_halves = halves(gain_row[None])
+    unit_own, unit_away = (x * inv_rms for x in values)
+    normed_own = (unit_own * gain_halves[0]).astype(BF)
+    normed_away = (unit_away * gain_halves[1]).astype(BF)
+    pre = dot_nt(normed_own, both_own) + dot_nt(normed_away, both_away)
+    gate_pre, up_pre = pre[:, :padded], pre[:, padded:]
     sig = jax.nn.sigmoid(gate_pre)
-    silu = gate_pre * sig
-    activation = (silu * up_pre).astype(BF)
-    gate_factor = pad_units(up_pre * sig * (1.0 + gate_pre * (1.0 - sig)), 1)
-    up_factor = pad_units(silu, 1)
-    gate_pre, up_pre = pad_units(gate_pre, 1), pad_units(up_pre, 1)
-    mine = jnp.where(core == 0, top_low, top_high)
-    other = jnp.where(core == 0, top_high, top_low)
-
-    def tile_of(x, start):
+    up_factor = gate_pre * sig
+    activation = (up_factor * up_pre).astype(BF)
+    gate_factor = up_pre * sig * (1.0 + gate_pre * (1.0 - sig))
+
+    def tile_of(x):
         rows = lax.dynamic_slice_in_dim(x, y * GROUP, GROUP, 0)
-        return lax.dynamic_slice_in_dim(rows, start, lanes, 1)
-
-    hidden_tile = tile_of(hidden, core * half + z * lanes).astype(F32)
-    up_tile = tile_of(mine, z * lanes)
+        return lax.dynamic_slice_in_dim(rows, z * lanes, lanes, 1)
+
+    hidden_tile = tile_of(hidden[0]).astype(F32)
+    up_tile = tile_of(mine)
     inv_tile = lax.dynamic_slice_in_dim(inv_rms, y * GROUP, GROUP, 0)
     gain_tile = lax.dynamic_slice_in_dim(gain_row, core * half + z * lanes, lanes, 0)
     in_group = lax.broadcasted_iota(jnp.int32, (NY, GROUP, 1), 1)
@@ -153,16 +159,15 @@
         inner = jnp.sum(grad_gate.astype(F32) * gate_pre + grad_up.astype(F32) * up_pre, axis=1)
         inner = jnp.tile(jnp.pad(inner, (0, lanes - ROWS)), NZ)
 
-        def partial_of(weights, start):
+        def partial_of(weights, unit_rows):
             partial = dot_nn(grads, weights)
             packed = jnp.where(in_group == USED, inner, partial.reshape(NY, GROUP, half))
             if last:
-                scaled = lax.dynamic_slice_in_dim(values, start, half, 1) * inv_rms
-                packed = jnp.where(in_group == USED + 1, jnp.sum(partial * scaled, axis=0), packed)
+                packed = jnp.where(in_group == USED + 1, jnp.sum(partial * unit_rows, axis=0), packed)
             return packed.astype(BF)
 
-        away = swap_core(partial_of(both_away, (1 - core) * half))
-        kept = partial_of(both_own, core * half)
+        away = swap_core(partial_of(both_away, unit_away))
+        kept = partial_of(both_own, unit_own)
         summed = (kept.astype(F32) + away.astype(F32)).astype(BF)
         pieces = summed.reshape(NY, GROUP, NZ, lanes).transpose(2, 0, 1, 3).reshape(NZ * NY, GROUP, lanes)
         if last:
@@ -185,12 +190,10 @@
             grad_tile = jnp.where(tile_row == USED + 1, low, grad_tile)
             sent = dot_nn(wanted, grad_tile).astype(BF).reshape(NZ * NY, 8, lanes)
             spread = exchange(sent)
+            normed = whole(normed_own, normed_away)
             gate_grads = dot_tn(grad_gate[:, :units], normed).astype(BF)
             up_grads = dot_tn(grad_up[:, :units], normed).astype(BF)
-            upstream = jnp.concatenate(
-                [jnp.where(core == 0, mine, other), jnp.where(core == 0, other, mine)], axis=1
-            )
-            down_grads = dot_tn(activation, upstream).astype(BF)
+            down_grads = dot_tn(activation[:, :units], whole(mine, other)).astype(BF)
             spread, gate_grads, up_grads, down_grads = lax.optimization_barrier(
                 (spread, gate_grads, up_grads, down_grads)
             )
@@ -209,9 +212,7 @@
         mine, other = unpack(spread), unpack(arrived)
         up_tile = grad_tile
 
-    final = jnp.concatenate(
-        [jnp.where(core == 0, from_mine, from_other), jnp.where(core == 0, from_other, from_mine)], axis=1
-    )
+    final = whole(from_mine, from_other)
     own_pair = jnp.where(core == 0, final[0:2], final[2:4])
     gain_grads = final[4].astype(F32) + final[5].astype(F32)
     return (

time: 254 us -> 245 us (0.965)
  other arithmetic: 19.8 us -> 14.2 us
  starting transfers between devices: 57.3 us -> 52.1 us
    ppermute x3, waiting for transfers between devices: 3.8 us -> 8.25 us  [spread_rows(): lax.ppermute(along_z, 'y', [(i, (i + by) % NY) for i in range(NY)])]
    all_to_all x3, waiting for transfers between devices: 29.9 us -> 26.8 us  [exchange(): return lax.all_to_all(x, PLANE, 0, 0, tiled=True)]
    dynamic_slice x2 -> x3, local copies, waits for them, and re-layouts: 3.82 us -> 1.22 us  [halves(): lax.dynamic_slice_in_dim(x, (1 - core) * half, half, 1)]
    unnamed x148 -> x100, local copies, waits for them, and re-layouts: 4.45 us -> 1.88 us
  transfers between devices with their start and end apart: 22 -> 22, of which waited for: 13 -> 14; matrix products, arithmetic and copies ran while one was open for 12% -> 11% of each run, Pallas kernels for 0% -> 0%
where the time goes in v4:
time: 245 us; the launch traced here: 244 us
  blocking collectives  87.1 us (36%)
  starting transfers between devices  52.1 us (21%)
  waiting for transfers between devices  51.1 us (21%)
  matrix products  19.7 us (8%)
  local copies, waits for them, and re-layouts  17.7 us (7%)
  other arithmetic  14.2 us (6%)
    all_to_all x5, blocking collectives, exchange(): return lax.all_to_all(x, PLANE, 0, 0, tiled=True)  87.1 us
    all_to_all x3, waiting for transfers between devices, exchange(): return lax.all_to_all(x, PLANE, 0, 0, tiled=True)  26.8 us
    ppermute x12, starting transfers between devices, swap_core(): return lax.ppermute(x, 'core', [(0, 1), (1, 0)])  20.5 us
    all_to_all x3, starting transfers between devices, exchange(): return lax.all_to_all(x, PLANE, 0, 0, tiled=True)  15.7 us
    all_to_all x1, starting transfers between devices, spread_rows(): lax.all_to_all(jnp.broadcast_to(own[None], (NZ, count, half)), 'z', 0, 0,...  9 us
    ppermute x3, waiting for transfers between devices, on_device(): moved = lax.ppermute(grad_tile, 'section', [(NS - 1 - step, NS - 2 - step)])  8.89 us
    ppermute x3, waiting for transfers between devices, spread_rows(): lax.ppermute(along_z, 'y', [(i, (i + by) % NY) for i in range(NY)])  8.25 us
    dot_general x11, matrix products, dot_nn(): lax.dot_general(a, b, (((1,), (0,)), ((), ())), preferred_element_type=F32)  7.73 us
  transfers between devices with their start and end apart: 22, of which 14 were waited for; matrix products, arithmetic and copies ran while one was open for 11% of the time, Pallas kernels for 0%

profile of v4, /device:TPU:1, one launch (start us, length us, event | category | flops | bytes accessed | tf_op | source)
XLA Modules:
  0.0 243.9 jit_solution(4002055439033131695)
XLA Ops:
  0.6 0.9 pad_maximum_fusion.15
  1.6 0.7 broadcast_in_dim.214
  2.3 9.0 %all-to-all-start = ((bf16[8,8,2048]{2,1,0:T(8,128)(2,1)}), bf16[8,8,2048]{2,1,0:T(8,128)(2,1)}, u32[]{:S(2)}, u32[]{:S(2)}) async-start(bf16[8,8,2048]{2,1,0:T(8,128)(2,1)} %broadcast_in_dim.214), calls=%async_computation | async-start | bytes 524288 | tf_op jit(solution)/shard_map/all_to_all | solution.py:45
  11.5 1.3 fusion.157
  14.8 1.5 fusion.53
  16.3 1.5 fusion.54
  17.8 2.4 fusion.70
  20.2 0.7 constant_dynamic-slice_fusion.4
  20.9 1.0 all-to-all-done
  21.9 2.3 collective-permute-start.3
  24.2 2.9 %collective-permute-start.2 = (bf16[8,8,2048]{2,1,0:T(8,128)(2,1)}, bf16[8,8,2048]{2,1,0:T(8,128)(2,1)S(1)}, u32[]{:S(2)}, u32[]{:S(2)}) collective-permute-start(bf16[8,8,2048]{2,1,0:T(8,128)(2,1)} %all-to-all-done), channel_id=1, source_target_pairs={{0,16},{8,24},{16,0},{24,8},{1,17},{9,25},{17,1},{25,9},{2,18},{10... | collective-permute-start | bytes 786440 | tf_op jit(solution)/shard_map/ppermute | solution.py:49
  27.2 0.8 collective-permute-start.1
  27.9 0.7 collective-permute-start
  30.0 3.8 %collective-permute-done.2 = bf16[8,8,2048]{2,1,0:T(8,128)(2,1)S(1)} collective-permute-done((bf16[8,8,2048]{2,1,0:T(8,128)(2,1)}, bf16[8,8,2048]{2,1,0:T(8,128)(2,1)S(1)}, u32[]{:S(2)}, u32[]{:S(2)}) %collective-permute-start.2) | collective-permute-done | bytes 262176 | tf_op jit(solution)/shard_map/ppermute | solution.py:49
  33.8 1.5 collective-permute-start.6
  35.2 4.5 %collective-permute-done.1 = bf16[8,8,2048]{2,1,0:T(8,128)(2,1)S(1)} collective-permute-done((bf16[8,8,2048]{2,1,0:T(8,128)(2,1)}, bf16[8,8,2048]{2,1,0:T(8,128)(2,1)S(1)}, u32[]{:S(2)}, u32[]{:S(2)}) %collective-permute-start.1) | collective-permute-done | bytes 262176 | tf_op jit(solution)/shard_map/ppermute | solution.py:49
  39.7 0.9 collective-permute-start.5
  40.7 1.5 fusion.7
  42.3 0.6 add_convert_fusion
  43.6 0.8 fusion.152
  44.4 0.8 convolution_add_fusion
  45.3 1.2 add_reduce_fusion.3
  48.2 0.9 collective-permute-done.7
  49.4 0.8 copy.14
  50.2 7.1 %all-to-all-start.1 = ((bf16[32,24,256]{2,1,0:T(8,128)(2,1)}), bf16[32,24,256]{2,1,0:T(8,128)(2,1)S(1)}, u32[]{:S(2)}, u32[]{:S(2)}) async-start(bf16[32,24,256]{2,1,0:T(8,128)(2,1)} %bitcast.222), calls=%async_computation.1 | async-start | bytes 786432 | tf_op jit(solution)/shard_map/all_to_all | solution.py:40
  57.9 1.2 constant_dynamic-slice_fusion.12
  59.1 1.2 dynamic-slice.14
  60.3 2.1 fusion.155
  62.4 8.9 %all-to-all-done.1 = bf16[32,24,256]{2,1,0:T(8,128)(2,1)S(1)} async-done(((bf16[32,24,256]{2,1,0:T(8,128)(2,1)}), bf16[32,24,256]{2,1,0:T(8,128)(2,1)S(1)}, u32[]{:S(2)}, u32[]{:S(2)}) %all-to-all-start.1) | async-done | bytes 393248 | tf_op jit(solution)/shard_map/all_to_all | solution.py:40
  71.4 0.9 fusion.97
  72.3 0.7 collective-permute-start.8
  73.0 0.8 bitcast_select_fusion
  73.9 17.5 %all_to_all.45 = bf16[32,24,256]{2,1,0:T(8,128)(2,1)S(1)} all-to-all(bf16[32,24,256]{2,1,0:T(8,128)(2,1)S(1)} %broadcast_in_dim.218), channel_id=1, replica_groups=mesh['z'=8,'y'=4,'core'=2,'section'=4] {'z','y'}, dimensions={0} | all-to-all | bytes 786432 | tf_op jit(solution)/shard_map/all_to_all | solution.py:40
  91.4 3.5 %collective-permute-start.9 = (bf16[32,24,256]{2,1,0:T(8,128)(2,1)S(1)}, bf16[32,24,256]{2,1,0:T(8,128)(2,1)S(1)}, u32[]{:S(2)}, u32[]{:S(2)}) collective-permute-start(bf16[32,24,256]{2,1,0:T(8,128)(2,1)S(1)} %all_to_all.45), channel_id=1, source_target_pairs={{0,4},{4,0},{1,5},{5,1},{2,6},{6,2},{3,7},{7,3},{8,12},{12,8},{9,1... | collective-permute-start | bytes 1179656 | tf_op jit(solution)/shard_map/ppermute | solution.py:36
  98.8 1.1 collective-permute-done.10
  100.2 18.1 %all_to_all.46 = bf16[32,24,256]{2,1,0:T(8,128)(2,1)S(1)} all-to-all(bf16[32,24,256]{2,1,0:T(8,128)(2,1)S(1)} %bitcast.231), channel_id=1, replica_groups=mesh['z'=8,'y'=4,'core'=2,'section'=4] {'z','y'}, dimensions={0} | all-to-all | bytes 786432 | tf_op jit(solution)/shard_map/all_to_all | solution.py:40
  118.5 0.8 fusion.101
  119.3 0.7 collective-permute-start.11
  120.0 17.1 %all_to_all.47 = bf16[32,24,256]{2,1,0:T(8,128)(2,1)S(1)} all-to-all(bf16[32,24,256]{2,1,0:T(8,128)(2,1)S(1)} %broadcast_in_dim.220), channel_id=1, replica_groups=mesh['z'=8,'y'=4,'core'=2,'section'=4] {'z','y'}, dimensions={0} | all-to-all | bytes 786432 | tf_op jit(solution)/shard_map/all_to_all | solution.py:40
  137.2 3.5 %collective-permute-start.12 = (bf16[32,24,256]{2,1,0:T(8,128)(2,1)S(1)}, bf16[32,24,256]{2,1,0:T(8,128)(2,1)S(1)}, u32[]{:S(2)}, u32[]{:S(2)}) collective-permute-start(bf16[32,24,256]{2,1,0:T(8,128)(2,1)S(1)} %all_to_all.47), channel_id=1, source_target_pairs={{0,4},{4,0},{1,5},{5,1},{2,6},{6,2},{3,7},{7,3},{8,12},{12,8},{9,1... | collective-permute-start | bytes 1179656 | tf_op jit(solution)/shard_map/ppermute | solution.py:36
  144.5 1.1 collective-permute-done.13
  145.9 18.0 %all_to_all.48 = bf16[32,24,256]{2,1,0:T(8,128)(2,1)S(1)} all-to-all(bf16[32,24,256]{2,1,0:T(8,128)(2,1)S(1)} %bitcast.234), channel_id=1, replica_groups=mesh['z'=8,'y'=4,'core'=2,'section'=4] {'z','y'}, dimensions={0} | all-to-all | bytes 786432 | tf_op jit(solution)/shard_map/all_to_all | solution.py:40
  164.1 0.8 fusion.105
  164.9 1.3 collective-permute-start.14
  166.2 8.9 %collective-permute-done.14 = bf16[24,256]{1,0:T(8,128)(2,1)S(1)} collective-permute-done((bf16[24,256]{1,0:T(8,128)(2,1)S(1)}, bf16[24,256]{1,0:T(8,128)(2,1)S(1)}, u32[]{:S(2)}, u32[]{:S(2)}) %collective-permute-start.14) | collective-permute-done | bytes 12320 | tf_op jit(solution)/shard_map/ppermute | solution.py:204
  175.2 16.4 %all_to_all.49 = bf16[32,24,256]{2,1,0:T(8,128)(2,1)} all-to-all(bf16[32,24,256]{2,1,0:T(8,128)(2,1)S(1)} %broadcast_in_dim.222), channel_id=1, replica_groups=mesh['z'=8,'y'=4,'core'=2,'section'=4] {'z','y'}, dimensions={0} | all-to-all | bytes 786432 | tf_op jit(solution)/shard_map/all_to_all | solution.py:40
  191.5 4.3 %collective-permute-start.15 = (bf16[32,24,256]{2,1,0:T(8,128)(2,1)}, bf16[32,24,256]{2,1,0:T(8,128)(2,1)}, u32[]{:S(2)}, u32[]{:S(2)}) collective-permute-start(bf16[32,24,256]{2,1,0:T(8,128)(2,1)} %all_to_all.49), channel_id=1, source_target_pairs={{0,4},{4,0},{1,5},{5,1},{2,6},{6,2},{3,7},{7,3},{8,12},{12,8},{9,1... | collective-permute-start | bytes 1179656 | tf_op jit(solution)/shard_map/ppermute | solution.py:36
  195.8 1.2 copy.21
  197.7 1.5 copy.22
  200.9 0.7 fusion.29
  202.3 1.3 collective-permute-done.16
  203.9 0.8 copy.23
  204.7 4.0 %all-to-all-start.7 = ((bf16[32,24,256]{2,1,0:T(8,128)(2,1)}), bf16[32,24,256]{2,1,0:T(8,128)(2,1)S(1)}, u32[]{:S(2)}, u32[]{:S(2)}) async-start(bf16[32,24,256]{2,1,0:T(8,128)(2,1)} %bitcast.57), calls=%async_computation.7 | async-start | bytes 786432 | tf_op jit(solution)/shard_map/all_to_all | solution.py:40
  208.8 1.9 convolution_convert_fusion.2
  210.8 1.9 convolution_convert_fusion
  212.7 10.4 %all-to-all-done.7 = bf16[32,24,256]{2,1,0:T(8,128)(2,1)S(1)} async-done(((bf16[32,24,256]{2,1,0:T(8,128)(2,1)}), bf16[32,24,256]{2,1,0:T(8,128)(2,1)S(1)}, u32[]{:S(2)}, u32[]{:S(2)}) %all-to-all-start.7) | async-done | bytes 393248 | tf_op jit(solution)/shard_map/all_to_all | solution.py:40
  223.3 1.7 fusion.6
  225.0 4.5 %all-to-all-start.8 = ((bf16[32,8,256]{2,1,0:T(8,128)(2,1)}), bf16[32,8,256]{2,1,0:T(8,128)(2,1)S(1)}, u32[]{:S(2)}, u32[]{:S(2)}) async-start(bf16[32,8,256]{2,1,0:T(8,128)(2,1)} %fusion.6), calls=%async_computation.8 | async-start | bytes 262144 | tf_op jit(solution)/shard_map/all_to_all | solution.py:40
  229.5 1.9 convolution_convert_fusion.1
  231.4 7.5 %all-to-all-done.8 = bf16[32,8,256]{2,1,0:T(8,128)(2,1)S(1)} async-done(((bf16[32,8,256]{2,1,0:T(8,128)(2,1)}), bf16[32,8,256]{2,1,0:T(8,128)(2,1)S(1)}, u32[]{:S(2)}, u32[]{:S(2)}) %all-to-all-start.8) | async-done | bytes 131104 | tf_op jit(solution)/shard_map/all_to_all | solution.py:40
  238.8 3.0 %collective-permute-start.17 = (bf16[8,2048]{1,0:T(8,128)(2,1)S(1)}, bf16[8,2048]{1,0:T(8,128)(2,1)S(1)}, u32[]{:S(2)}, u32[]{:S(2)}) collective-permute-start(bf16[8,2048]{1,0:T(8,128)(2,1)S(1)} %bitcast.261), channel_id=1, source_target_pairs={{0,4},{4,0},{1,5},{5,1},{2,6},{6,2},{3,7},{7,3},{8,12},{12,8},{9,1... | collective-permute-start | bytes 98312 | tf_op jit(solution)/shard_map/ppermute | solution.py:36
  241.8 0.9 collective-permute-done.17
  242.7 0.6 fusion.110
  243.3 0.6 fusion.115
  (233 shorter events, 18.6 us)
Async XLA Ops:
  0.6 28.0 %copy-start.12 = (bf16[1,224,4096]{2,1,0:T(8,128)(2,1)S(1)}, bf16[1,224,4096]{2,1,0:T(8,128)(2,1)}, u32[]{:S(2)}) copy-start(bf16[1,224,4096]{2,1,0:T(8,128)(2,1)} %param.9) | copy-start | bytes 5505028
  2.3 19.6 %all-to-all-start = ((bf16[8,8,2048]{2,1,0:T(8,128)(2,1)}), bf16[8,8,2048]{2,1,0:T(8,128)(2,1)}, u32[]{:S(2)}, u32[]{:S(2)}) async-start(bf16[8,8,2048]{2,1,0:T(8,128)(2,1)} %broadcast_in_dim.214), calls=%async_computation | async-start | bytes 524288 | tf_op jit(solution)/shard_map/all_to_all | solution.py:45
  11.4 17.3 %copy-start.25 = (pred[24]{0:T(512)(128)(4,1)}, pred[24]{0:T(512)(128)(4,1)S(1)}, u32[]{:S(2)}) copy-start(pred[24]{0:T(512)(128)(4,1)S(1)} %get-tuple-element.96) | copy-start | bytes 76
  11.4 17.3 %copy-start.34 = (pred[24]{0:T(512)(128)(4,1)}, pred[24]{0:T(512)(128)(4,1)S(1)}, u32[]{:S(2)}) copy-start(pred[24]{0:T(512)(128)(4,1)S(1)} %get-tuple-element.95) | copy-start | bytes 76
  21.9 6.9 %copy-start.13 = (bf16[1,224,4096]{2,1,0:T(8,128)(2,1)S(1)}, bf16[1,224,4096]{2,1,0:T(8,128)(2,1)}, u32[]{:S(2)}) copy-start(bf16[1,224,4096]{2,1,0:T(8,128)(2,1)} %param.11) | copy-start | bytes 5505028
  21.9 6.9 %copy-start.14 = (bf16[1,224,4096]{2,1,0:T(8,128)(2,1)S(1)}, bf16[1,224,4096]{2,1,0:T(8,128)(2,1)}, u32[]{:S(2)}) copy-start(bf16[1,224,4096]{2,1,0:T(8,128)(2,1)} %param.10) | copy-start | bytes 5505028
  21.9 20.3 %collective-permute-start.3 = (bf16[8,8,2048]{2,1,0:T(8,128)(2,1)}, bf16[8,8,2048]{2,1,0:T(8,128)(2,1)S(1)}, u32[]{:S(2)}, u32[]{:S(2)}) collective-permute-start(bf16[8,8,2048]{2,1,0:T(8,128)(2,1)} %all-to-all-done), channel_id=1, source_target_pairs={{0,4},{4,0},{1,5},{5,1},{2,6},{6,2},{3,7},{7,3},{8,12},{12,8},{9,1... | collective-permute-start | bytes 786440 | tf_op jit(solution)/shard_map/ppermute | solution.py:36
  24.2 9.5 %collective-permute-start.2 = (bf16[8,8,2048]{2,1,0:T(8,128)(2,1)}, bf16[8,8,2048]{2,1,0:T(8,128)(2,1)S(1)}, u32[]{:S(2)}, u32[]{:S(2)}) collective-permute-start(bf16[8,8,2048]{2,1,0:T(8,128)(2,1)} %all-to-all-done), channel_id=1, source_target_pairs={{0,16},{8,24},{16,0},{24,8},{1,17},{9,25},{17,1},{25,9},{2,18},{10... | collective-permute-start | bytes 786440 | tf_op jit(solution)/shard_map/ppermute | solution.py:49
  27.2 12.6 %collective-permute-start.1 = (bf16[8,8,2048]{2,1,0:T(8,128)(2,1)}, bf16[8,8,2048]{2,1,0:T(8,128)(2,1)S(1)}, u32[]{:S(2)}, u32[]{:S(2)}) collective-permute-start(bf16[8,8,2048]{2,1,0:T(8,128)(2,1)} %all-to-all-done), channel_id=1, source_target_pairs={{0,24},{8,0},{16,8},{24,16},{1,25},{9,1},{17,9},{25,17},{2,26},{10... | collective-permute-start | bytes 786440 | tf_op jit(solution)/shard_map/ppermute | solution.py:49
  27.9 12.8 %collective-permute-start = (bf16[8,8,2048]{2,1,0:T(8,128)(2,1)}, bf16[8,8,2048]{2,1,0:T(8,128)(2,1)S(1)}, u32[]{:S(2)}, u32[]{:S(2)}) collective-permute-start(bf16[8,8,2048]{2,1,0:T(8,128)(2,1)} %all-to-all-done), channel_id=1, source_target_pairs={{0,8},{8,16},{16,24},{24,0},{1,9},{9,17},{17,25},{25,1},{2,10},{10... | collective-permute-start | bytes 786440 | tf_op jit(solution)/shard_map/ppermute | solution.py:49
  29.3 15.9 %copy-start.6 = (bf16[256,2048]{1,0:T(8,128)(2,1)}, bf16[256,2048]{1,0:T(8,128)(2,1)S(1)}, u32[]{:S(2)}) copy-start(bf16[256,2048]{1,0:T(8,128)(2,1)S(1)} %pad.37) | copy-start | bytes 3145732
  30.0 16.5 %copy-start = (bf16[512,2048]{1,0:T(8,128)(2,1)}, bf16[512,2048]{1,0:T(8,128)(2,1)S(1)}, u32[]{:S(2)}) copy-start(bf16[512,2048]{1,0:T(8,128)(2,1)S(1)} %fusion.5) | copy-start | bytes 6291460
  33.8 8.5 %collective-permute-start.6 = (bf16[8,8,2048]{2,1,0:T(8,128)(2,1)S(1)}, bf16[8,8,2048]{2,1,0:T(8,128)(2,1)S(1)}, u32[]{:S(2)}, u32[]{:S(2)}) collective-permute-start(bf16[8,8,2048]{2,1,0:T(8,128)(2,1)S(1)} %collective-permute-done.2), channel_id=1, source_target_pairs={{0,4},{4,0},{1,5},{5,1},{2,6},{6,2},{3,7},{7,3},{8,12},{12,8},{9,1... | collective-permute-start | bytes 786440 | tf_op jit(solution)/shard_map/ppermute | solution.py:36
  39.7 2.5 %collective-permute-start.5 = (bf16[8,8,2048]{2,1,0:T(8,128)(2,1)S(1)}, bf16[8,8,2048]{2,1,0:T(8,128)(2,1)S(1)}, u32[]{:S(2)}, u32[]{:S(2)}) collective-permute-start(bf16[8,8,2048]{2,1,0:T(8,128)(2,1)S(1)} %collective-permute-done.1), channel_id=1, source_target_pairs={{0,4},{4,0},{1,5},{5,1},{2,6},{6,2},{3,7},{7,3},{8,12},{12,8},{9,1... | collective-permute-start | bytes 786440 | tf_op jit(solution)/shard_map/ppermute | solution.py:36
  40.7 1.6 collective-permute-start.4
  42.9 2.4 copy-start.4
  43.6 0.8 copy-start.32
  45.2 1.8 copy-start.15
  45.2 1.8 copy-start.26
  47.1 1.9 collective-permute-start.7
  50.2 21.1 %all-to-all-start.1 = ((bf16[32,24,256]{2,1,0:T(8,128)(2,1)}), bf16[32,24,256]{2,1,0:T(8,128)(2,1)S(1)}, u32[]{:S(2)}, u32[]{:S(2)}) async-start(bf16[32,24,256]{2,1,0:T(8,128)(2,1)} %bitcast.222), calls=%async_computation.1 | async-start | bytes 786432 | tf_op jit(solution)/shard_map/all_to_all | solution.py:40
  72.3 0.7 collective-permute-start.8
  91.4 4.9 %collective-permute-start.9 = (bf16[32,24,256]{2,1,0:T(8,128)(2,1)S(1)}, bf16[32,24,256]{2,1,0:T(8,128)(2,1)S(1)}, u32[]{:S(2)}, u32[]{:S(2)}) collective-permute-start(bf16[32,24,256]{2,1,0:T(8,128)(2,1)S(1)} %all_to_all.45), channel_id=1, source_target_pairs={{0,4},{4,0},{1,5},{5,1},{2,6},{6,2},{3,7},{7,3},{8,12},{12,8},{9,1... | collective-permute-start | bytes 1179656 | tf_op jit(solution)/shard_map/ppermute | solution.py:36
  95.2 1.4 copy-start.7
  95.2 1.4 copy-start.16
  95.2 1.4 copy-start.18
  95.8 1.7 copy-start.1
  96.6 1.3 copy-start.27
  98.0 1.8 collective-permute-start.10
  99.8 18.6 %copy-start.30 = (f32[1,256]{1,0:T(1,128)S(1)}, f32[1,256]{1,0:T(1,128)}, u32[]{:S(2)}) copy-start(f32[1,256]{1,0:T(1,128)} %constant_dynamic-slice_fusion.12) | copy-start | bytes 3076
  99.8 18.6 %copy-start.37 = (pred[24]{0:T(512)(128)(4,1)S(1)}, pred[24]{0:T(512)(128)(4,1)}, u32[]{:S(2)}) copy-start(pred[24]{0:T(512)(128)(4,1)} %iota_compare_fusion.6) | copy-start | bytes 76
  99.8 18.6 %copy-start.39 = (f32[24]{0:T(128)S(1)}, f32[24]{0:T(128)}, u32[]{:S(2)}) copy-start(f32[24]{0:T(128)} %dynamic-slice.14) | copy-start | bytes 292
  119.3 0.7 collective-permute-start.11
  137.2 4.9 %collective-permute-start.12 = (bf16[32,24,256]{2,1,0:T(8,128)(2,1)S(1)}, bf16[32,24,256]{2,1,0:T(8,128)(2,1)S(1)}, u32[]{:S(2)}, u32[]{:S(2)}) collective-permute-start(bf16[32,24,256]{2,1,0:T(8,128)(2,1)S(1)} %all_to_all.47), channel_id=1, source_target_pairs={{0,4},{4,0},{1,5},{5,1},{2,6},{6,2},{3,7},{7,3},{8,12},{12,8},{9,1... | collective-permute-start | bytes 1179656 | tf_op jit(solution)/shard_map/ppermute | solution.py:36
  140.9 1.4 copy-start.8
  141.5 1.7 copy-start.2
  143.7 1.8 collective-permute-start.13
  164.9 10.2 %collective-permute-start.14 = (bf16[24,256]{1,0:T(8,128)(2,1)S(1)}, bf16[24,256]{1,0:T(8,128)(2,1)S(1)}, u32[]{:S(2)}, u32[]{:S(2)}) collective-permute-start(bf16[24,256]{1,0:T(8,128)(2,1)S(1)} %fusion.105), channel_id=1, source_target_pairs={{1,0},{5,4},{9,8},{13,12},{17,16},{21,20},{25,24},{29,28},{33,32},... | collective-permute-start | bytes 36872 | tf_op jit(solution)/shard_map/ppermute | solution.py:204
  175.1 21.9 %copy-start.23 = (bf16[24,256]{1,0:T(8,128)(2,1)}, bf16[24,256]{1,0:T(8,128)(2,1)S(1)}, u32[]{:S(2)}) copy-start(bf16[24,256]{1,0:T(8,128)(2,1)S(1)} %broadcast_select_fusion.8) | copy-start | bytes 36868
  191.5 6.1 %collective-permute-start.15 = (bf16[32,24,256]{2,1,0:T(8,128)(2,1)}, bf16[32,24,256]{2,1,0:T(8,128)(2,1)}, u32[]{:S(2)}, u32[]{:S(2)}) collective-permute-start(bf16[32,24,256]{2,1,0:T(8,128)(2,1)} %all_to_all.49), channel_id=1, source_target_pairs={{0,4},{4,0},{1,5},{5,1},{2,6},{6,2},{3,7},{7,3},{8,12},{12,8},{9,1... | collective-permute-start | bytes 1179656 | tf_op jit(solution)/shard_map/ppermute | solution.py:36
  197.1 2.2 copy-start.9
  197.1 2.2 copy-start.17
  197.1 2.2 copy-start.19
  197.2 2.8 %copy-start.3 = (bf16[512,2048]{1,0:T(8,128)(2,1)S(1)}, bf16[512,2048]{1,0:T(8,128)(2,1)}, u32[]{:S(2)}) copy-start(bf16[512,2048]{1,0:T(8,128)(2,1)} %copy-done) | copy-start | bytes 6291460
  199.3 0.7 copy-start.10
  199.3 1.5 copy-start.5
  199.3 1.5 copy-start.33
  200.8 0.7 copy-start.28
  200.8 0.7 copy-start.35
  201.7 1.8 collective-permute-start.16
  203.9 6.8 %copy-start.11 = (bf16[12,8,8,256]{3,1,2,0:T(8,128)(2,1)S(1)}, bf16[12,8,8,256]{3,1,2,0:T(8,128)(2,1)}, u32[]{:S(2)}) copy-start(bf16[12,8,8,256]{3,1,2,0:T(8,128)(2,1)} %copy-done.10) | copy-start | bytes 1179652
  204.7 18.4 %all-to-all-start.7 = ((bf16[32,24,256]{2,1,0:T(8,128)(2,1)}), bf16[32,24,256]{2,1,0:T(8,128)(2,1)S(1)}, u32[]{:S(2)}, u32[]{:S(2)}) async-start(bf16[32,24,256]{2,1,0:T(8,128)(2,1)} %bitcast.57), calls=%async_computation.7 | async-start | bytes 786432 | tf_op jit(solution)/shard_map/all_to_all | solution.py:40
  208.7 2.0 copy-start.20
  208.7 2.0 copy-start.21
  210.7 12.6 %copy-start.22 = (bf16[256,24]{1,0:T(8,128)(2,1)S(1)}, bf16[256,24]{1,0:T(8,128)(2,1)}, u32[]{:S(2)}) copy-start(bf16[256,24]{1,0:T(8,128)(2,1)} %fusion.70) | copy-start | bytes 36868
  210.7 12.6 %copy-start.24 = (bf16[24,256]{1,0:T(8,128)(2,1)S(1)}, bf16[24,256]{1,0:T(8,128)(2,1)}, u32[]{:S(2)}) copy-start(bf16[24,256]{1,0:T(8,128)(2,1)} %copy-done.23) | copy-start | bytes 36868
  210.7 12.6 %copy-start.29 = (pred[24]{0:T(512)(128)(4,1)S(1)}, pred[24]{0:T(512)(128)(4,1)}, u32[]{:S(2)}) copy-start(pred[24]{0:T(512)(128)(4,1)} %copy-done.25) | copy-start | bytes 76
  210.7 12.6 %copy-start.31 = (f32[1,256]{1,0:T(1,128)S(1)}, f32[1,256]{1,0:T(1,128)}, u32[]{:S(2)}) copy-start(f32[1,256]{1,0:T(1,128)} %constant_dynamic-slice_fusion.12) | copy-start | bytes 3076
  210.7 12.6 %copy-start.36 = (pred[24]{0:T(512)(128)(4,1)S(1)}, pred[24]{0:T(512)(128)(4,1)}, u32[]{:S(2)}) copy-start(pred[24]{0:T(512)(128)(4,1)} %copy-done.34) | copy-start | bytes 76
  210.7 12.6 %copy-start.38 = (pred[24]{0:T(512)(128)(4,1)S(1)}, pred[24]{0:T(512)(128)(4,1)}, u32[]{:S(2)}) copy-start(pred[24]{0:T(512)(128)(4,1)} %iota_compare_fusion.6) | copy-start | bytes 76
  210.7 12.6 %copy-start.40 = (f32[24]{0:T(128)S(1)}, f32[24]{0:T(128)}, u32[]{:S(2)}) copy-start(f32[24]{0:T(128)} %dynamic-slice.14) | copy-start | bytes 292
  225.0 13.8 %all-to-all-start.8 = ((bf16[32,8,256]{2,1,0:T(8,128)(2,1)}), bf16[32,8,256]{2,1,0:T(8,128)(2,1)S(1)}, u32[]{:S(2)}, u32[]{:S(2)}) async-start(bf16[32,8,256]{2,1,0:T(8,128)(2,1)} %fusion.6), calls=%async_computation.8 | async-start | bytes 262144 | tf_op jit(solution)/shard_map/all_to_all | solution.py:40
  238.8 3.8 %collective-permute-start.17 = (bf16[8,2048]{1,0:T(8,128)(2,1)S(1)}, bf16[8,2048]{1,0:T(8,128)(2,1)S(1)}, u32[]{:S(2)}, u32[]{:S(2)}) collective-permute-start(bf16[8,2048]{1,0:T(8,128)(2,1)S(1)} %bitcast.261), channel_id=1, source_target_pairs={{0,4},{4,0},{1,5},{5,1},{2,6},{6,2},{3,7},{7,3},{8,12},{12,8},{9,1... | collective-permute-start | bytes 98312 | tf_op jit(solution)/shard_map/ppermute | solution.py:36

commit v5 on v4

--- a/solution.py
+++ b/solution.py
@@ -8,6 +8,7 @@
 DP = ("z", "y", "core")
 PLANE = ("z", "y")
 LIVE = 85
+PACK = 12
 GROUP = 24
 USED = 22
 ROWS = NY * GROUP
@@ -40,37 +41,55 @@
     return lax.all_to_all(x, PLANE, 0, 0, tiled=True)
 
 
-def spread_rows(own, weights):
+def packed_slot(counts, index, residue):
+    first = jnp.clip((counts[0] - residue + NY * NC - 1) // (NY * NC), 0, NZ)
+    micro = (index >= first).astype(jnp.int32)
+    at_z = index - first * micro
+    slot = at_z * NY * NC + residue
+    return micro, at_z, slot, slot < jnp.where(micro == 0, counts[0], counts[1])
+
+
+def packing(counts, y, core):
+    shape = (4, PACK, NZ, 8)
+    kind_half, index, z, piece = (lax.broadcasted_iota(jnp.int32, shape, d) for d in range(4))
+    micro, at_z, _, live = packed_slot(counts, index, y * NC + core)
+    hit = live & (at_z == z) & (piece == (kind_half // 2) * 4 + micro * 2 + kind_half % 2)
+    return hit.astype(BF).reshape(4 * PACK, NZ * 8)
+
+
+def spread_rows(own, weights, pack):
     count, half = own.shape
     along_z = lax.all_to_all(jnp.broadcast_to(own[None], (NZ, count, half)), "z", 0, 0, tiled=True)
     along_z, weights = lax.optimization_barrier((along_z, weights))
-    shifted = [along_z]
+    packed = dot_nn(pack, along_z.reshape(NZ * count, half)).astype(BF)
+    shifted = [packed]
     for by in (1, 3, 2):
-        shifted.append(lax.ppermute(along_z, "y", [(i, (i + by) % NY) for i in range(NY)]))
+        shifted.append(lax.ppermute(packed, "y", [(i, (i + by) % NY) for i in range(NY)]))
     swapped = [swap_core(x) for x in shifted]
-    join = lambda xs: jnp.concatenate([x.reshape(NZ * count, half) for x in xs], axis=0)
-    return join(shifted), join(swapped), weights
+    return jnp.concatenate(shifted, axis=0), jnp.concatenate(swapped, axis=0), weights
 
 
 def selection(counts, y, core, first_half):
-    shape = (2, 2, ROWS, NY, NZ, 8)
-    at = lambda dim: lax.broadcasted_iota(jnp.int32, shape, dim)
-    kind, part, row, shift, z, piece = (at(d) for d in range(6))
+    shape = (4, ROWS, NY, 4, PACK)
+    out, row, shift, kind_half, index = (lax.broadcasted_iota(jnp.int32, shape, d) for d in range(5))
     by = jnp.where(shift == 0, 0, jnp.where(shift == 1, 1, jnp.where(shift == 2, 3, 2)))
-    slot = z * NY * NC + ((y - by + NY) % NY) * NC + core
-    micro = (piece // 2) % 2
-    limit = jnp.where(micro == 0, counts[0], counts[1])
-    hit = (row_of(micro, slot) == row) & (slot < limit) & (piece // 4 == kind) & (piece % 2 == (part ^ first_half))
-    return hit.astype(BF).reshape(4 * ROWS, NY * NZ * 8)
+    micro, _, slot, live = packed_slot(counts, index, ((y - by + NY) % NY) * NC + core)
+    hit = live & (row_of(micro, slot) == row) & (kind_half == (out ^ first_half))
+    return hit.astype(BF).reshape(4 * ROWS, NY * 4 * PACK)
 
 
 def gather_rows(hidden, top, weights, counts, y, core):
     half = hidden.shape[-1] // 2
     own = jnp.concatenate([hidden, top], axis=0).reshape(8, half)
-    pick_own, pick_other, wanted = lax.optimization_barrier(
-        (selection(counts, y, core, core), selection(counts, y, 1 - core, core), wanted_rows(counts, y))
-    )
-    mine, other, weights = spread_rows(own, weights)
+    pack, pick_own, pick_other, wanted = lax.optimization_barrier(
+        (
+            packing(counts, y, core),
+            selection(counts, y, core, core),
+            selection(counts, y, 1 - core, core),
+            wanted_rows(counts, y),
+        )
+    )
+    mine, other, weights = spread_rows(own, weights, pack)
     rows = (dot_nn(pick_own, mine) + dot_nn(pick_other, other)).astype(BF).reshape(2, 2, ROWS, half)
     return (rows[0, 0], rows[0, 1]), (rows[1, 0], rows[1, 1]), wanted, weights
 
@@ -106,6 +125,9 @@
         return jnp.concatenate(
             [jnp.where(core == 0, own, away), jnp.where(core == 0, away, own)], axis=1
         )
+
+    def unpack(x):
+        return x.reshape(NZ, NY, GROUP, lanes).transpose(1, 2, 0, 3).reshape(ROWS, half)
 
     units = gate_mat.shape[0]
     padded = -(-units // 256) * 256
@@ -171,9 +193,10 @@
         summed = (kept.astype(F32) + away.astype(F32)).astype(BF)
         pieces = summed.reshape(NY, GROUP, NZ, lanes).transpose(2, 0, 1, 3).reshape(NZ * NY, GROUP, lanes)
         if last:
-            pieces, grad_gate, grad_up, mine, other = lax.optimization_barrier(
-                (pieces, grad_gate, grad_up, mine, other)
+            pieces, grad_gate, grad_up, spread, arrived = lax.optimization_barrier(
+                (pieces, grad_gate, grad_up, spread, arrived)
             )
+            upstream = whole(unpack(spread), unpack(arrived))
         total = jnp.sum(exchange(pieces).astype(F32), axis=0)
         row_sum = lax.dynamic_slice_in_dim(total[USED], y * GROUP, GROUP, 0)[:, None]
         grad_tile = (
@@ -193,7 +216,7 @@
             normed = whole(normed_own, normed_away)
             gate_grads = dot_tn(grad_gate[:, :units], normed).astype(BF)
             up_grads = dot_tn(grad_up[:, :units], normed).astype(BF)
-            down_grads = dot_tn(activation[:, :units], whole(mine, other)).astype(BF)
+            down_grads = dot_tn(activation[:, :units], upstream).astype(BF)
             spread, gate_grads, up_grads, down_grads = lax.optimization_barrier(
                 (spread, gate_grads, up_grads, down_grads)
             )
@@ -205,10 +228,6 @@
         grad_tile = jnp.where(section == NS - 2 - step, moved, up_tile)
         spread = exchange(jnp.broadcast_to(grad_tile[None], (NZ * NY, GROUP, lanes)))
         arrived = swap_core(spread)
-
-        def unpack(x):
-            return x.reshape(NZ, NY, GROUP, lanes).transpose(1, 2, 0, 3).reshape(ROWS, half)
-
         mine, other = unpack(spread), unpack(arrived)
         up_tile = grad_tile
 

time: 245 us -> 242 us (0.988)
  waiting for transfers between devices: 51.1 us -> 39.4 us
  starting transfers between devices: 52.1 us -> 57.9 us
    ppermute x3, waiting for transfers between devices: 8.25 us -> 0.01 us  [spread_rows(): lax.ppermute(packed, 'y', [(i, (i + by) % NY) for i in range(NY)])]
    ppermute x12, starting transfers between devices: 20.5 us -> 24.1 us  [swap_core(): return lax.ppermute(x, 'core', [(0, 1), (1, 0)])]
    dot_general x11 -> x12, matrix products: 7.73 us -> 6.97 us  [dot_nn(): lax.dot_general(a, b, (((1,), (0,)), ((), ())), preferred_element_type=F32)]
  transfers between devices with their start and end apart: 22 -> 22, of which waited for: 14 -> 13; matrix products, arithmetic and copies ran while one was open for 11% -> 12% of each run, Pallas kernels for 0% -> 0%
where the time goes in v5:
time: 242 us; the launch traced here: 241 us
  blocking collectives  86.8 us (36%)
  starting transfers between devices  57.9 us (24%)
  waiting for transfers between devices  39.4 us (16%)
  local copies, waits for them, and re-layouts  19.4 us (8%)
  matrix products  18.9 us (8%)
  other arithmetic  15.5 us (6%)
  between operations  2.58 us (1%)
    all_to_all x5, blocking collectives, exchange(): return lax.all_to_all(x, PLANE, 0, 0, tiled=True)  86.8 us
    all_to_all x3, waiting for transfers between devices, exchange(): return lax.all_to_all(x, PLANE, 0, 0, tiled=True)  24.8 us
    ppermute x12, starting transfers between devices, swap_core(): return lax.ppermute(x, 'core', [(0, 1), (1, 0)])  24.1 us
    all_to_all x3, starting transfers between devices, exchange(): return lax.all_to_all(x, PLANE, 0, 0, tiled=True)  17.7 us
    all_to_all x1, starting transfers between devices, spread_rows(): lax.all_to_all(jnp.broadcast_to(own[None], (NZ, count, half)), 'z', 0, 0,...  9 us
    ppermute x3, waiting for transfers between devices, on_device(): moved = lax.ppermute(grad_tile, 'section', [(NS - 1 - step, NS - 2 - step)])  8.89 us
    dot_general x12, matrix products, dot_nn(): lax.dot_general(a, b, (((1,), (0,)), ((), ())), preferred_element_type=F32)  6.97 us
    dot_general x10, matrix products, dot_nt(): lax.dot_general(a, b, (((1,), (1,)), ((), ())), preferred_element_type=F32)  6.3 us
  transfers between devices with their start and end apart: 22, of which 13 were waited for; matrix products, arithmetic and copies ran while one was open for 12% of the time, Pallas kernels for 0%

profile of v5, /device:TPU:1, one launch (start us, length us, event | category | flops | bytes accessed | tf_op | source)
XLA Modules:
  0.0 240.6 jit_solution(1578975549103213481)
XLA Ops:
  0.6 0.9 pad_maximum_fusion.15
  1.6 0.7 broadcast_in_dim.221
  2.3 9.0 %all-to-all-start = ((bf16[8,8,2048]{2,1,0:T(8,128)(2,1)}), bf16[8,8,2048]{2,1,0:T(8,128)(2,1)S(1)}, u32[]{:S(2)}, u32[]{:S(2)}) async-start(bf16[8,8,2048]{2,1,0:T(8,128)(2,1)} %broadcast_in_dim.221), calls=%async_computation | async-start | bytes 524288 | tf_op jit(solution)/shard_map/all_to_all | solution.py:62
  11.3 1.3 fusion.169
  13.5 1.3 compare_select_fusion.3
  17.2 1.8 fusion.64
  19.1 2.4 fusion.78
  21.5 0.7 constant_dynamic-slice_fusion.4
  22.4 1.4 collective-permute-start
  23.8 1.5 collective-permute-start.1
  25.3 1.6 collective-permute-start.2
  26.9 2.8 %collective-permute-start.3 = (bf16[48,2048]{1,0:T(8,128)(2,1)S(1)}, bf16[48,2048]{1,0:T(8,128)(2,1)S(1)}, u32[]{:S(2)}, u32[]{:S(2)}) collective-permute-start(bf16[48,2048]{1,0:T(8,128)(2,1)S(1)} %convolution_convert_fusion.3), channel_id=1, source_target_pairs={{0,4},{4,0},{1,5},{5,1},{2,6},{6,2},{3,7},{7,3},{8,12},{12,8},{9,1... | collective-permute-start | bytes 589832 | tf_op jit(solution)/shard_map/ppermute | solution.py:37
  31.3 1.4 collective-permute-start.4
  32.7 2.0 collective-permute-start.5
  34.7 1.8 collective-permute-start.6
  36.5 0.6 fusion.17
  37.5 0.6 add_convert_fusion
  38.9 0.8 fusion.164
  39.7 0.8 convolution_add_fusion
  40.5 1.2 add_reduce_fusion.3
  43.3 0.9 collective-permute-done.7
  44.5 0.8 copy.12
  45.3 8.7 %all-to-all-start.1 = ((bf16[32,24,256]{2,1,0:T(8,128)(2,1)}), bf16[32,24,256]{2,1,0:T(8,128)(2,1)S(1)}, u32[]{:S(2)}, u32[]{:S(2)}) async-start(bf16[32,24,256]{2,1,0:T(8,128)(2,1)} %bitcast.227), calls=%async_computation.1 | async-start | bytes 786432 | tf_op jit(solution)/shard_map/all_to_all | solution.py:41
  54.1 0.6 iota_compare_fusion.6
  54.7 1.2 constant_dynamic-slice_fusion.12
  55.9 1.2 dynamic-slice.14
  57.1 2.1 fusion.167
  59.2 9.0 %all-to-all-done.1 = bf16[32,24,256]{2,1,0:T(8,128)(2,1)S(1)} async-done(((bf16[32,24,256]{2,1,0:T(8,128)(2,1)}), bf16[32,24,256]{2,1,0:T(8,128)(2,1)S(1)}, u32[]{:S(2)}, u32[]{:S(2)}) %all-to-all-start.1) | async-done | bytes 393248 | tf_op jit(solution)/shard_map/all_to_all | solution.py:41
  68.3 0.9 fusion.105
  69.2 0.7 collective-permute-start.8
  69.9 0.8 bitcast_select_fusion
  70.7 17.3 %all_to_all.45 = bf16[32,24,256]{2,1,0:T(8,128)(2,1)S(1)} all-to-all(bf16[32,24,256]{2,1,0:T(8,128)(2,1)S(1)} %broadcast_in_dim.225), channel_id=1, replica_groups=mesh['z'=8,'y'=4,'core'=2,'section'=4] {'z','y'}, dimensions={0} | all-to-all | bytes 786432 | tf_op jit(solution)/shard_map/all_to_all | solution.py:41
  88.0 3.6 %collective-permute-start.9 = (bf16[32,24,256]{2,1,0:T(8,128)(2,1)S(1)}, bf16[32,24,256]{2,1,0:T(8,128)(2,1)S(1)}, u32[]{:S(2)}, u32[]{:S(2)}) collective-permute-start(bf16[32,24,256]{2,1,0:T(8,128)(2,1)S(1)} %all_to_all.45), channel_id=1, source_target_pairs={{0,4},{4,0},{1,5},{5,1},{2,6},{6,2},{3,7},{7,3},{8,12},{12,8},{9,1... | collective-permute-start | bytes 1179656 | tf_op jit(solution)/shard_map/ppermute | solution.py:37
  96.7 17.6 %all_to_all.46 = bf16[32,24,256]{2,1,0:T(8,128)(2,1)S(1)} all-to-all(bf16[32,24,256]{2,1,0:T(8,128)(2,1)S(1)} %bitcast.236), channel_id=1, replica_groups=mesh['z'=8,'y'=4,'core'=2,'section'=4] {'z','y'}, dimensions={0} | all-to-all | bytes 786432 | tf_op jit(solution)/shard_map/all_to_all | solution.py:41
  114.5 0.8 fusion.109
  115.3 0.7 collective-permute-start.11
  116.1 17.6 %all_to_all.47 = bf16[32,24,256]{2,1,0:T(8,128)(2,1)S(1)} all-to-all(bf16[32,24,256]{2,1,0:T(8,128)(2,1)S(1)} %broadcast_in_dim.227), channel_id=1, replica_groups=mesh['z'=8,'y'=4,'core'=2,'section'=4] {'z','y'}, dimensions={0} | all-to-all | bytes 786432 | tf_op jit(solution)/shard_map/all_to_all | solution.py:41
  133.7 3.5 %collective-permute-start.12 = (bf16[32,24,256]{2,1,0:T(8,128)(2,1)S(1)}, bf16[32,24,256]{2,1,0:T(8,128)(2,1)S(1)}, u32[]{:S(2)}, u32[]{:S(2)}) collective-permute-start(bf16[32,24,256]{2,1,0:T(8,128)(2,1)S(1)} %all_to_all.47), channel_id=1, source_target_pairs={{0,4},{4,0},{1,5},{5,1},{2,6},{6,2},{3,7},{7,3},{8,12},{12,8},{9,1... | collective-permute-start | bytes 1179656 | tf_op jit(solution)/shard_map/ppermute | solution.py:37
  138.0 0.6 collective-permute-done.12
  142.3 17.6 %all_to_all.48 = bf16[32,24,256]{2,1,0:T(8,128)(2,1)S(1)} all-to-all(bf16[32,24,256]{2,1,0:T(8,128)(2,1)S(1)} %bitcast.239), channel_id=1, replica_groups=mesh['z'=8,'y'=4,'core'=2,'section'=4] {'z','y'}, dimensions={0} | all-to-all | bytes 786432 | tf_op jit(solution)/shard_map/all_to_all | solution.py:41
  160.0 0.8 fusion.113
  160.8 1.3 collective-permute-start.14
  162.1 8.9 %collective-permute-done.14 = bf16[24,256]{1,0:T(8,128)(2,1)S(1)} collective-permute-done((bf16[24,256]{1,0:T(8,128)(2,1)S(1)}, bf16[24,256]{1,0:T(8,128)(2,1)S(1)}, u32[]{:S(2)}, u32[]{:S(2)}) %collective-permute-start.14) | collective-permute-done | bytes 12320 | tf_op jit(solution)/shard_map/ppermute | solution.py:227
  171.0 0.6 copy-done.21
  171.6 16.7 %all_to_all.49 = bf16[32,24,256]{2,1,0:T(8,128)(2,1)S(1)} all-to-all(bf16[32,24,256]{2,1,0:T(8,128)(2,1)S(1)} %broadcast_in_dim.229), channel_id=1, replica_groups=mesh['z'=8,'y'=4,'core'=2,'section'=4] {'z','y'}, dimensions={0} | all-to-all | bytes 786432 | tf_op jit(solution)/shard_map/all_to_all | solution.py:41
  188.4 4.3 %collective-permute-start.15 = (bf16[32,24,256]{2,1,0:T(8,128)(2,1)S(1)}, bf16[32,24,256]{2,1,0:T(8,128)(2,1)}, u32[]{:S(2)}, u32[]{:S(2)}) collective-permute-start(bf16[32,24,256]{2,1,0:T(8,128)(2,1)S(1)} %all_to_all.49), channel_id=1, source_target_pairs={{0,4},{4,0},{1,5},{5,1},{2,6},{6,2},{3,7},{7,3},{8,12},{12,8},{9,1... | collective-permute-start | bytes 1179656 | tf_op jit(solution)/shard_map/ppermute | solution.py:37
  193.5 0.7 collective-permute-done.15
  194.2 1.2 copy.20
  197.5 0.7 fusion.14
  199.2 1.0 collective-permute-done.16
  200.6 0.8 copy.21
  201.4 4.0 %all-to-all-start.7 = ((bf16[32,24,256]{2,1,0:T(8,128)(2,1)}), bf16[32,24,256]{2,1,0:T(8,128)(2,1)S(1)}, u32[]{:S(2)}, u32[]{:S(2)}) async-start(bf16[32,24,256]{2,1,0:T(8,128)(2,1)} %bitcast.50), calls=%async_computation.7 | async-start | bytes 786432 | tf_op jit(solution)/shard_map/all_to_all | solution.py:41
  205.4 1.1 broadcast_select_fusion.1
  207.1 1.9 convolution_convert_fusion.1
  209.0 1.9 convolution_convert_fusion
  210.9 8.3 %all-to-all-done.7 = bf16[32,24,256]{2,1,0:T(8,128)(2,1)S(1)} async-done(((bf16[32,24,256]{2,1,0:T(8,128)(2,1)}), bf16[32,24,256]{2,1,0:T(8,128)(2,1)S(1)}, u32[]{:S(2)}, u32[]{:S(2)}) %all-to-all-start.7) | async-done | bytes 393248 | tf_op jit(solution)/shard_map/all_to_all | solution.py:41
  219.5 1.7 fusion.6
  221.1 5.0 %all-to-all-start.8 = ((bf16[32,8,256]{2,1,0:T(8,128)(2,1)}), bf16[32,8,256]{2,1,0:T(8,128)(2,1)S(1)}, u32[]{:S(2)}, u32[]{:S(2)}) async-start(bf16[32,8,256]{2,1,0:T(8,128)(2,1)} %fusion.6), calls=%async_computation.8 | async-start | bytes 262144 | tf_op jit(solution)/shard_map/all_to_all | solution.py:41
  226.1 1.9 convolution_convert_fusion.2
  228.0 7.5 %all-to-all-done.8 = bf16[32,8,256]{2,1,0:T(8,128)(2,1)S(1)} async-done(((bf16[32,8,256]{2,1,0:T(8,128)(2,1)}), bf16[32,8,256]{2,1,0:T(8,128)(2,1)S(1)}, u32[]{:S(2)}, u32[]{:S(2)}) %all-to-all-start.8) | async-done | bytes 131104 | tf_op jit(solution)/shard_map/all_to_all | solution.py:41
  235.5 3.0 %collective-permute-start.17 = (bf16[8,2048]{1,0:T(8,128)(2,1)S(1)}, bf16[8,2048]{1,0:T(8,128)(2,1)S(1)}, u32[]{:S(2)}, u32[]{:S(2)}) collective-permute-start(bf16[8,2048]{1,0:T(8,128)(2,1)S(1)} %bitcast.267), channel_id=1, source_target_pairs={{0,4},{4,0},{1,5},{5,1},{2,6},{6,2},{3,7},{7,3},{8,12},{12,8},{9,1... | collective-permute-start | bytes 98312 | tf_op jit(solution)/shard_map/ppermute | solution.py:37
  238.5 0.9 collective-permute-done.17
  239.3 0.6 fusion.125
  240.0 0.6 fusion.120
  (233 shorter events, 22.2 us)
Async XLA Ops:
  0.6 29.0 %copy-start.10 = (bf16[1,224,4096]{2,1,0:T(8,128)(2,1)S(1)}, bf16[1,224,4096]{2,1,0:T(8,128)(2,1)}, u32[]{:S(2)}) copy-start(bf16[1,224,4096]{2,1,0:T(8,128)(2,1)} %param.9) | copy-start | bytes 5505028
  2.3 19.9 %all-to-all-start = ((bf16[8,8,2048]{2,1,0:T(8,128)(2,1)}), bf16[8,8,2048]{2,1,0:T(8,128)(2,1)S(1)}, u32[]{:S(2)}, u32[]{:S(2)}) async-start(bf16[8,8,2048]{2,1,0:T(8,128)(2,1)} %broadcast_in_dim.221), calls=%async_computation | async-start | bytes 524288 | tf_op jit(solution)/shard_map/all_to_all | solution.py:62
  13.3 16.5 %copy-start.23 = (pred[24]{0:T(512)(128)(4,1)}, pred[24]{0:T(512)(128)(4,1)S(1)}, u32[]{:S(2)}) copy-start(pred[24]{0:T(512)(128)(4,1)S(1)} %get-tuple-element.102) | copy-start | bytes 76
  13.3 16.5 %copy-start.31 = (pred[24]{0:T(512)(128)(4,1)}, pred[24]{0:T(512)(128)(4,1)S(1)}, u32[]{:S(2)}) copy-start(pred[24]{0:T(512)(128)(4,1)S(1)} %get-tuple-element.101) | copy-start | bytes 76
  22.2 7.7 %copy-start.11 = (bf16[1,224,4096]{2,1,0:T(8,128)(2,1)S(1)}, bf16[1,224,4096]{2,1,0:T(8,128)(2,1)}, u32[]{:S(2)}) copy-start(bf16[1,224,4096]{2,1,0:T(8,128)(2,1)} %param.11) | copy-start | bytes 5505028
  22.2 7.7 %copy-start.12 = (bf16[1,224,4096]{2,1,0:T(8,128)(2,1)S(1)}, bf16[1,224,4096]{2,1,0:T(8,128)(2,1)}, u32[]{:S(2)}) copy-start(bf16[1,224,4096]{2,1,0:T(8,128)(2,1)} %param.10) | copy-start | bytes 5505028
  22.4 8.9 %collective-permute-start = (bf16[48,2048]{1,0:T(8,128)(2,1)S(1)}, bf16[48,2048]{1,0:T(8,128)(2,1)S(1)}, u32[]{:S(2)}, u32[]{:S(2)}) collective-permute-start(bf16[48,2048]{1,0:T(8,128)(2,1)S(1)} %convolution_convert_fusion.3), channel_id=1, source_target_pairs={{0,8},{8,16},{16,24},{24,0},{1,9},{9,17},{17,25},{25,1},{2,10},{10... | collective-permute-start | bytes 589832 | tf_op jit(solution)/shard_map/ppermute | solution.py:67
  23.8 8.9 %collective-permute-start.1 = (bf16[48,2048]{1,0:T(8,128)(2,1)S(1)}, bf16[48,2048]{1,0:T(8,128)(2,1)S(1)}, u32[]{:S(2)}, u32[]{:S(2)}) collective-permute-start(bf16[48,2048]{1,0:T(8,128)(2,1)S(1)} %convolution_convert_fusion.3), channel_id=1, source_target_pairs={{0,24},{8,0},{16,8},{24,16},{1,25},{9,1},{17,9},{25,17},{2,26},{10... | collective-permute-start | bytes 589832 | tf_op jit(solution)/shard_map/ppermute | solution.py:67
  25.3 9.4 %collective-permute-start.2 = (bf16[48,2048]{1,0:T(8,128)(2,1)S(1)}, bf16[48,2048]{1,0:T(8,128)(2,1)S(1)}, u32[]{:S(2)}, u32[]{:S(2)}) collective-permute-start(bf16[48,2048]{1,0:T(8,128)(2,1)S(1)} %convolution_convert_fusion.3), channel_id=1, source_target_pairs={{0,16},{8,24},{16,0},{24,8},{1,17},{9,25},{17,1},{25,9},{2,18},{10... | collective-permute-start | bytes 589832 | tf_op jit(solution)/shard_map/ppermute | solution.py:67
  26.9 10.2 %collective-permute-start.3 = (bf16[48,2048]{1,0:T(8,128)(2,1)S(1)}, bf16[48,2048]{1,0:T(8,128)(2,1)S(1)}, u32[]{:S(2)}, u32[]{:S(2)}) collective-permute-start(bf16[48,2048]{1,0:T(8,128)(2,1)S(1)} %convolution_convert_fusion.3), channel_id=1, source_target_pairs={{0,4},{4,0},{1,5},{5,1},{2,6},{6,2},{3,7},{7,3},{8,12},{12,8},{9,1... | collective-permute-start | bytes 589832 | tf_op jit(solution)/shard_map/ppermute | solution.py:37
  30.6 9.8 %copy-start.6 = (bf16[256,2048]{1,0:T(8,128)(2,1)}, bf16[256,2048]{1,0:T(8,128)(2,1)S(1)}, u32[]{:S(2)}) copy-start(bf16[256,2048]{1,0:T(8,128)(2,1)S(1)} %pad.37) | copy-start | bytes 3145732
  31.3 11.5 %copy-start = (bf16[512,2048]{1,0:T(8,128)(2,1)}, bf16[512,2048]{1,0:T(8,128)(2,1)S(1)}, u32[]{:S(2)}) copy-start(bf16[512,2048]{1,0:T(8,128)(2,1)S(1)} %fusion.4) | copy-start | bytes 6291460
  31.3 5.7 %collective-permute-start.4 = (bf16[48,2048]{1,0:T(8,128)(2,1)S(1)}, bf16[48,2048]{1,0:T(8,128)(2,1)S(1)}, u32[]{:S(2)}, u32[]{:S(2)}) collective-permute-start(bf16[48,2048]{1,0:T(8,128)(2,1)S(1)} %collective-permute-done), channel_id=1, source_target_pairs={{0,4},{4,0},{1,5},{5,1},{2,6},{6,2},{3,7},{7,3},{8,12},{12,8},{9,1... | collective-permute-start | bytes 589832 | tf_op jit(solution)/shard_map/ppermute | solution.py:37
  32.7 4.4 %collective-permute-start.5 = (bf16[48,2048]{1,0:T(8,128)(2,1)S(1)}, bf16[48,2048]{1,0:T(8,128)(2,1)S(1)}, u32[]{:S(2)}, u32[]{:S(2)}) collective-permute-start(bf16[48,2048]{1,0:T(8,128)(2,1)S(1)} %collective-permute-done.1), channel_id=1, source_target_pairs={{0,4},{4,0},{1,5},{5,1},{2,6},{6,2},{3,7},{7,3},{8,12},{12,8},{9,1... | collective-permute-start | bytes 589832 | tf_op jit(solution)/shard_map/ppermute | solution.py:37
  34.7 2.9 %collective-permute-start.6 = (bf16[48,2048]{1,0:T(8,128)(2,1)S(1)}, bf16[48,2048]{1,0:T(8,128)(2,1)S(1)}, u32[]{:S(2)}, u32[]{:S(2)}) collective-permute-start(bf16[48,2048]{1,0:T(8,128)(2,1)S(1)} %collective-permute-done.2), channel_id=1, source_target_pairs={{0,4},{4,0},{1,5},{5,1},{2,6},{6,2},{3,7},{7,3},{8,12},{12,8},{9,1... | collective-permute-start | bytes 589832 | tf_op jit(solution)/shard_map/ppermute | solution.py:37
  38.1 2.4 copy-start.4
  38.9 0.8 copy-start.29
  40.5 1.8 copy-start.13
  40.5 1.8 copy-start.24
  42.4 1.8 collective-permute-start.7
  45.3 22.8 %all-to-all-start.1 = ((bf16[32,24,256]{2,1,0:T(8,128)(2,1)}), bf16[32,24,256]{2,1,0:T(8,128)(2,1)S(1)}, u32[]{:S(2)}, u32[]{:S(2)}) async-start(bf16[32,24,256]{2,1,0:T(8,128)(2,1)} %bitcast.227), calls=%async_computation.1 | async-start | bytes 786432 | tf_op jit(solution)/shard_map/all_to_all | solution.py:41
  69.2 0.7 collective-permute-start.8
  88.0 4.9 %collective-permute-start.9 = (bf16[32,24,256]{2,1,0:T(8,128)(2,1)S(1)}, bf16[32,24,256]{2,1,0:T(8,128)(2,1)S(1)}, u32[]{:S(2)}, u32[]{:S(2)}) collective-permute-start(bf16[32,24,256]{2,1,0:T(8,128)(2,1)S(1)} %all_to_all.45), channel_id=1, source_target_pairs={{0,4},{4,0},{1,5},{5,1},{2,6},{6,2},{3,7},{7,3},{8,12},{12,8},{9,1... | collective-permute-start | bytes 1179656 | tf_op jit(solution)/shard_map/ppermute | solution.py:37
  91.8 1.4 copy-start.7
  91.8 1.4 copy-start.14
  91.9 1.4 copy-start.16
  93.3 1.1 copy-start.25
  93.9 1.6 copy-start.1
  94.5 1.8 collective-permute-start.10
  96.3 18.2 %copy-start.27 = (f32[1,256]{1,0:T(1,128)S(1)}, f32[1,256]{1,0:T(1,128)}, u32[]{:S(2)}) copy-start(f32[1,256]{1,0:T(1,128)} %constant_dynamic-slice_fusion.12) | copy-start | bytes 3076
  96.3 18.2 %copy-start.33 = (pred[24]{0:T(512)(128)(4,1)S(1)}, pred[24]{0:T(512)(128)(4,1)}, u32[]{:S(2)}) copy-start(pred[24]{0:T(512)(128)(4,1)} %iota_compare_fusion.6) | copy-start | bytes 76
  96.3 18.2 %copy-start.35 = (f32[24]{0:T(128)S(1)}, f32[24]{0:T(128)}, u32[]{:S(2)}) copy-start(f32[24]{0:T(128)} %dynamic-slice.14) | copy-start | bytes 292
  115.3 0.7 collective-permute-start.11
  133.7 4.9 %collective-permute-start.12 = (bf16[32,24,256]{2,1,0:T(8,128)(2,1)S(1)}, bf16[32,24,256]{2,1,0:T(8,128)(2,1)S(1)}, u32[]{:S(2)}, u32[]{:S(2)}) collective-permute-start(bf16[32,24,256]{2,1,0:T(8,128)(2,1)S(1)} %all_to_all.47), channel_id=1, source_target_pairs={{0,4},{4,0},{1,5},{5,1},{2,6},{6,2},{3,7},{7,3},{8,12},{12,8},{9,1... | collective-permute-start | bytes 1179656 | tf_op jit(solution)/shard_map/ppermute | solution.py:37
  137.4 1.4 copy-start.8
  139.4 1.6 copy-start.2
  140.1 1.8 collective-permute-start.13
  160.8 10.2 %collective-permute-start.14 = (bf16[24,256]{1,0:T(8,128)(2,1)S(1)}, bf16[24,256]{1,0:T(8,128)(2,1)S(1)}, u32[]{:S(2)}, u32[]{:S(2)}) collective-permute-start(bf16[24,256]{1,0:T(8,128)(2,1)S(1)} %fusion.113), channel_id=1, source_target_pairs={{1,0},{5,4},{9,8},{13,12},{17,16},{21,20},{25,24},{29,28},{33,32},... | collective-permute-start | bytes 36872 | tf_op jit(solution)/shard_map/ppermute | solution.py:227
  171.0 0.6 copy-start.21
  188.4 5.8 %collective-permute-start.15 = (bf16[32,24,256]{2,1,0:T(8,128)(2,1)S(1)}, bf16[32,24,256]{2,1,0:T(8,128)(2,1)}, u32[]{:S(2)}, u32[]{:S(2)}) collective-permute-start(bf16[32,24,256]{2,1,0:T(8,128)(2,1)S(1)} %all_to_all.49), channel_id=1, source_target_pairs={{0,4},{4,0},{1,5},{5,1},{2,6},{6,2},{3,7},{7,3},{8,12},{12,8},{9,1... | collective-permute-start | bytes 1179656 | tf_op jit(solution)/shard_map/ppermute | solution.py:37
  192.9 2.6 %copy-start.9 = (bf16[256,2048]{1,0:T(8,128)(2,1)S(1)}, bf16[256,2048]{1,0:T(8,128)(2,1)}, u32[]{:S(2)}) copy-start(bf16[256,2048]{1,0:T(8,128)(2,1)} %copy-done.6) | copy-start | bytes 3145732
  192.9 2.6 %copy-start.15 = (f32[96,512]{1,0:T(8,128)S(1)}, f32[96,512]{1,0:T(8,128)}, u32[]{:S(2)}) copy-start(f32[96,512]{1,0:T(8,128)} %copy-done.13) | copy-start | bytes 589828
  192.9 2.6 %copy-start.17 = (f32[96,256]{1,0:T(8,128)S(1)}, f32[96,256]{1,0:T(8,128)}, u32[]{:S(2)}) copy-start(f32[96,256]{1,0:T(8,128)} %get-tuple-element.64) | copy-start | bytes 294916
  195.5 1.6 copy-start.3
  195.5 2.0 copy-start.5
  195.5 2.0 copy-start.30
  197.5 0.7 copy-start.26
  197.5 0.7 copy-start.32
  198.4 1.8 collective-permute-start.16
  201.4 17.9 %all-to-all-start.7 = ((bf16[32,24,256]{2,1,0:T(8,128)(2,1)}), bf16[32,24,256]{2,1,0:T(8,128)(2,1)S(1)}, u32[]{:S(2)}, u32[]{:S(2)}) async-start(bf16[32,24,256]{2,1,0:T(8,128)(2,1)} %bitcast.50), calls=%async_computation.7 | async-start | bytes 786432 | tf_op jit(solution)/shard_map/all_to_all | solution.py:41
  206.8 2.2 copy-start.18
  206.8 2.2 copy-start.19
  209.0 10.5 %copy-start.20 = (bf16[256,24]{1,0:T(8,128)(2,1)S(1)}, bf16[256,24]{1,0:T(8,128)(2,1)}, u32[]{:S(2)}) copy-start(bf16[256,24]{1,0:T(8,128)(2,1)} %fusion.78) | copy-start | bytes 36868
  209.0 10.5 %copy-start.22 = (bf16[24,256]{1,0:T(8,128)(2,1)S(1)}, bf16[24,256]{1,0:T(8,128)(2,1)}, u32[]{:S(2)}) copy-start(bf16[24,256]{1,0:T(8,128)(2,1)} %copy-done.21) | copy-start | bytes 36868
  209.0 10.5 %copy-start.28 = (f32[1,256]{1,0:T(1,128)S(1)}, f32[1,256]{1,0:T(1,128)}, u32[]{:S(2)}) copy-start(f32[1,256]{1,0:T(1,128)} %constant_dynamic-slice_fusion.12) | copy-start | bytes 3076
  209.0 10.5 %copy-start.34 = (pred[24]{0:T(512)(128)(4,1)S(1)}, pred[24]{0:T(512)(128)(4,1)}, u32[]{:S(2)}) copy-start(pred[24]{0:T(512)(128)(4,1)} %iota_compare_fusion.6) | copy-start | bytes 76
  209.0 10.5 %copy-start.36 = (f32[24]{0:T(128)S(1)}, f32[24]{0:T(128)}, u32[]{:S(2)}) copy-start(f32[24]{0:T(128)} %dynamic-slice.14) | copy-start | bytes 292
  221.1 14.3 %all-to-all-start.8 = ((bf16[32,8,256]{2,1,0:T(8,128)(2,1)}), bf16[32,8,256]{2,1,0:T(8,128)(2,1)S(1)}, u32[]{:S(2)}, u32[]{:S(2)}) async-start(bf16[32,8,256]{2,1,0:T(8,128)(2,1)} %fusion.6), calls=%async_computation.8 | async-start | bytes 262144 | tf_op jit(solution)/shard_map/all_to_all | solution.py:41
  235.5 3.8 %collective-permute-start.17 = (bf16[8,2048]{1,0:T(8,128)(2,1)S(1)}, bf16[8,2048]{1,0:T(8,128)(2,1)S(1)}, u32[]{:S(2)}, u32[]{:S(2)}) collective-permute-start(bf16[8,2048]{1,0:T(8,128)(2,1)S(1)} %bitcast.267), channel_id=1, source_target_pairs={{0,4},{4,0},{1,5},{5,1},{2,6},{6,2},{3,7},{7,3},{8,12},{12,8},{9,1... | collective-permute-start | bytes 98312 | tf_op jit(solution)/shard_map/ppermute | solution.py:37

commit v6 on v5

--- a/solution.py
+++ b/solution.py
@@ -6,12 +6,14 @@
 
 NZ, NY, NC, NS = 8, 4, 2, 4
 DP = ("z", "y", "core")
-PLANE = ("z", "y")
+PLANE = ("y", "z")
 LIVE = 85
 PACK = 12
-GROUP = 24
-USED = 22
-ROWS = NY * GROUP
+GROUP = 48
+USED = 43
+PARTS = 2
+BLOCKS = NZ * NY // PARTS
+ROWS = PARTS * GROUP
 BF = jnp.bfloat16
 F32 = jnp.float32
 
@@ -63,7 +65,7 @@
     along_z, weights = lax.optimization_barrier((along_z, weights))
     packed = dot_nn(pack, along_z.reshape(NZ * count, half)).astype(BF)
     shifted = [packed]
-    for by in (1, 3, 2):
+    for by in (2, 1, 3):
         shifted.append(lax.ppermute(packed, "y", [(i, (i + by) % NY) for i in range(NY)]))
     swapped = [swap_core(x) for x in shifted]
     return jnp.concatenate(shifted, axis=0), jnp.concatenate(swapped, axis=0), weights
@@ -72,7 +74,7 @@
 def selection(counts, y, core, first_half):
     shape = (4, ROWS, NY, 4, PACK)
     out, row, shift, kind_half, index = (lax.broadcasted_iota(jnp.int32, shape, d) for d in range(5))
-    by = jnp.where(shift == 0, 0, jnp.where(shift == 1, 1, jnp.where(shift == 2, 3, 2)))
+    by = jnp.where(shift == 1, 2, jnp.where(shift == 2, 1, shift))
     micro, _, slot, live = packed_slot(counts, index, ((y - by + NY) % NY) * NC + core)
     hit = live & (row_of(micro, slot) == row) & (kind_half == (out ^ first_half))
     return hit.astype(BF).reshape(4 * ROWS, NY * 4 * PACK)
@@ -86,7 +88,7 @@
             packing(counts, y, core),
             selection(counts, y, core, core),
             selection(counts, y, 1 - core, core),
-            wanted_rows(counts, y),
+            wanted_rows(counts, y // 2),
         )
     )
     mine, other, weights = spread_rows(own, weights, pack)
@@ -94,15 +96,15 @@
     return (rows[0, 0], rows[0, 1]), (rows[1, 0], rows[1, 1]), wanted, weights
 
 
-def wanted_rows(counts, y):
+def wanted_rows(counts, part):
     shape = (NZ * NY * 8, GROUP)
     index, row = (lax.broadcasted_iota(jnp.int32, shape, d) for d in range(2))
     place, piece = index // 8, index % 8
-    slot = place * NC + piece // 2
+    slot = (place % NZ) * NY * NC + (place // NZ) * NC + piece // 2
     micro = piece % 2
     limit = jnp.where(micro == 0, counts[0], counts[1])
-    hit = (piece < 4) & (row_of(micro, slot) == y * GROUP + row) & (slot < limit)
-    carry = (y == 0) & ((piece == 4) & (row == USED) | (piece == 5) & (row == USED + 1))
+    hit = (piece < 4) & (row_of(micro, slot) == part * GROUP + row) & (slot < limit)
+    carry = (part == 0) & ((piece == 4) & (row == USED) | (piece == 5) & (row == USED + 1))
     return (hit | carry).astype(BF)
 
 
@@ -111,9 +113,10 @@
     gain_row = gain[0]
     width = gate_mat.shape[1]
     half = width // 2
-    lanes = width // (NC * NZ)
+    lanes = half // BLOCKS
     z, y, core = lax.axis_index("z"), lax.axis_index("y"), lax.axis_index("core")
     section = lax.axis_index("section")
+    part, block = y // 2, (y % 2) * NZ + z
 
     def halves(x):
         return (
@@ -127,7 +130,7 @@
         )
 
     def unpack(x):
-        return x.reshape(NZ, NY, GROUP, lanes).transpose(1, 2, 0, 3).reshape(ROWS, half)
+        return x.reshape(PARTS, BLOCKS, GROUP, lanes).transpose(0, 2, 1, 3).reshape(ROWS, half)
 
     units = gate_mat.shape[0]
     padded = -(-units // 256) * 256
@@ -162,14 +165,14 @@
     gate_factor = up_pre * sig * (1.0 + gate_pre * (1.0 - sig))
 
     def tile_of(x):
-        rows = lax.dynamic_slice_in_dim(x, y * GROUP, GROUP, 0)
-        return lax.dynamic_slice_in_dim(rows, z * lanes, lanes, 1)
+        rows = lax.dynamic_slice_in_dim(x, part * GROUP, GROUP, 0)
+        return lax.dynamic_slice_in_dim(rows, block * lanes, lanes, 1)
 
     hidden_tile = tile_of(hidden[0]).astype(F32)
     up_tile = tile_of(mine)
-    inv_tile = lax.dynamic_slice_in_dim(inv_rms, y * GROUP, GROUP, 0)
-    gain_tile = lax.dynamic_slice_in_dim(gain_row, core * half + z * lanes, lanes, 0)
-    in_group = lax.broadcasted_iota(jnp.int32, (NY, GROUP, 1), 1)
+    inv_tile = lax.dynamic_slice_in_dim(inv_rms, part * GROUP, GROUP, 0)
+    gain_tile = lax.dynamic_slice_in_dim(gain_row, core * half + block * lanes, lanes, 0)
+    in_group = lax.broadcasted_iota(jnp.int32, (PARTS, GROUP, 1), 1)
     tile_row = lax.broadcasted_iota(jnp.int32, (GROUP, 1), 0)
 
     for step in range(NS):
@@ -179,11 +182,11 @@
         grad_up = (grad_act * up_factor).astype(BF)
         grads = jnp.concatenate([grad_gate, grad_up], axis=1)
         inner = jnp.sum(grad_gate.astype(F32) * gate_pre + grad_up.astype(F32) * up_pre, axis=1)
-        inner = jnp.tile(jnp.pad(inner, (0, lanes - ROWS)), NZ)
+        inner = jnp.tile(jnp.pad(inner, (0, lanes - ROWS)), BLOCKS)
 
         def partial_of(weights, unit_rows):
             partial = dot_nn(grads, weights)
-            packed = jnp.where(in_group == USED, inner, partial.reshape(NY, GROUP, half))
+            packed = jnp.where(in_group == USED, inner, partial.reshape(PARTS, GROUP, half))
             if last:
                 packed = jnp.where(in_group == USED + 1, jnp.sum(partial * unit_rows, axis=0), packed)
             return packed.astype(BF)
@@ -191,14 +194,14 @@
         away = swap_core(partial_of(both_away, unit_away))
         kept = partial_of(both_own, unit_own)
         summed = (kept.astype(F32) + away.astype(F32)).astype(BF)
-        pieces = summed.reshape(NY, GROUP, NZ, lanes).transpose(2, 0, 1, 3).reshape(NZ * NY, GROUP, lanes)
+        pieces = summed.reshape(PARTS, GROUP, BLOCKS, lanes).transpose(0, 2, 1, 3).reshape(NZ * NY, GROUP, lanes)
         if last:
             pieces, grad_gate, grad_up, spread, arrived = lax.optimization_barrier(
                 (pieces, grad_gate, grad_up, spread, arrived)
             )
             upstream = whole(unpack(spread), unpack(arrived))
         total = jnp.sum(exchange(pieces).astype(F32), axis=0)
-        row_sum = lax.dynamic_slice_in_dim(total[USED], y * GROUP, GROUP, 0)[:, None]
+        row_sum = lax.dynamic_slice_in_dim(total[USED], part * GROUP, GROUP, 0)[:, None]
         grad_tile = (
             up_tile.astype(F32)
             + inv_tile * (gain_tile * total)
@@ -220,7 +223,7 @@
             spread, gate_grads, up_grads, down_grads = lax.optimization_barrier(
                 (spread, gate_grads, up_grads, down_grads)
             )
-            from_mine = jnp.sum(spread.reshape(NZ, NY, 8, lanes).astype(F32), axis=1).astype(BF)
+            from_mine = jnp.sum(spread.reshape(PARTS, BLOCKS, 8, lanes).astype(F32), axis=0).astype(BF)
             from_mine = from_mine.transpose(1, 0, 2).reshape(8, half)
             from_other = swap_core(from_mine)
             break

time: 242 us -> 243 us (level)
  starting transfers between devices: 57.9 us -> 62.1 us
  waiting for transfers between devices: 39.4 us -> 36.6 us
    all_to_all x3, waiting for transfers between devices: 24.8 us -> 20.2 us  [exchange(): return lax.all_to_all(x, PLANE, 0, 0, tiled=True)]
    all_to_all x3, starting transfers between devices: 17.7 us -> 21.2 us  [exchange(): return lax.all_to_all(x, PLANE, 0, 0, tiled=True)]
  transfers between devices with their start and end apart: 22 -> 22, of which waited for: 13 -> 15; matrix products, arithmetic and copies ran while one was open for 12% -> 11% of each run, Pallas kernels for 0% -> 0%
where the time goes in v6:
time: 243 us; the launch traced here: 242 us
  blocking collectives  87.6 us (36%)
  starting transfers between devices  62.1 us (26%)
  waiting for transfers between devices  36.6 us (15%)
  matrix products  18.9 us (8%)
  local copies, waits for them, and re-layouts  18.1 us (7%)
  other arithmetic  15.6 us (6%)
  between operations  2.53 us (1%)
    all_to_all x5, blocking collectives, exchange(): return lax.all_to_all(x, PLANE, 0, 0, tiled=True)  87.6 us
    ppermute x12, starting transfers between devices, swap_core(): return lax.ppermute(x, 'core', [(0, 1), (1, 0)])  23.6 us
    all_to_all x3, starting transfers between devices, exchange(): return lax.all_to_all(x, PLANE, 0, 0, tiled=True)  21.2 us
    all_to_all x3, waiting for transfers between devices, exchange(): return lax.all_to_all(x, PLANE, 0, 0, tiled=True)  20.2 us
    all_to_all x1, starting transfers between devices, spread_rows(): lax.all_to_all(jnp.broadcast_to(own[None], (NZ, count, half)), 'z', 0, 0,...  9 us
    ppermute x3, waiting for transfers between devices, on_device(): moved = lax.ppermute(grad_tile, 'section', [(NS - 1 - step, NS - 2 - step)])  8.87 us
    dot_general x12, matrix products, dot_nn(): lax.dot_general(a, b, (((1,), (0,)), ((), ())), preferred_element_type=F32)  6.92 us
    ppermute x12, waiting for transfers between devices, swap_core(): return lax.ppermute(x, 'core', [(0, 1), (1, 0)])  6.89 us
  transfers between devices with their start and end apart: 22, of which 15 were waited for; matrix products, arithmetic and copies ran while one was open for 11% of the time, Pallas kernels for 0%

profile of v6, /device:TPU:1, one launch (start us, length us, event | category | flops | bytes accessed | tf_op | source)
XLA Modules:
  0.0 241.5 jit_solution(3181309449940251289)
XLA Ops:
  0.6 0.9 pad_maximum_fusion.15
  1.6 0.7 broadcast_in_dim.215
  2.3 9.0 %all-to-all-start = ((bf16[8,8,2048]{2,1,0:T(8,128)(2,1)}), bf16[8,8,2048]{2,1,0:T(8,128)(2,1)S(1)}, u32[]{:S(2)}, u32[]{:S(2)}) async-start(bf16[8,8,2048]{2,1,0:T(8,128)(2,1)} %broadcast_in_dim.215), calls=%async_computation | async-start | bytes 524288 | tf_op jit(solution)/shard_map/all_to_all | solution.py:64
  11.3 1.3 fusion.192
  13.5 1.3 compare_select_fusion.2
  17.1 1.8 fusion.79
  19.1 2.5 %fusion.100 = bf16[256,48]{1,0:T(8,128)(2,1)} fusion(s32[]{:T(128)} %bitcast.1, s32[]{:T(128)} %bitcast, s32[48]{0:T(128)S(1)} %iota_add_fusion, s32[256]{0:T(256)S(1)} %get-tuple-element.93, s32[256]{0:T(256)S(1)} %get-tuple-element.96, s32[256]{0:T(256)S(1)} %get-tuple-element.94, s32[256]{0:T(256)S(1)} %get-tuple-element.95, ...), kind=kLoop, calls=%fused_computation.203 | loop fusion | flops 921600 | bytes 29481 | tf_op jit(solution)/shard_map/convert_element_type | solution.py:108
  21.6 0.7 constant_dynamic-slice_fusion.4
  22.5 3.0 %collective-permute-start = (bf16[48,2048]{1,0:T(8,128)(2,1)S(1)}, bf16[48,2048]{1,0:T(8,128)(2,1)S(1)}, u32[]{:S(2)}, u32[]{:S(2)}) collective-permute-start(bf16[48,2048]{1,0:T(8,128)(2,1)S(1)} %convolution_convert_fusion.3), channel_id=1, source_target_pairs={{0,16},{8,24},{16,0},{24,8},{1,17},{9,25},{17,1},{25,9},{2,18},{10... | collective-permute-start | bytes 589832 | tf_op jit(solution)/shard_map/ppermute | solution.py:69
  25.9 2.3 collective-permute-start.2
  28.2 2.7 %collective-permute-start.3 = (bf16[48,2048]{1,0:T(8,128)(2,1)S(1)}, bf16[48,2048]{1,0:T(8,128)(2,1)S(1)}, u32[]{:S(2)}, u32[]{:S(2)}) collective-permute-start(bf16[48,2048]{1,0:T(8,128)(2,1)S(1)} %convolution_convert_fusion.3), channel_id=1, source_target_pairs={{0,4},{4,0},{1,5},{5,1},{2,6},{6,2},{3,7},{7,3},{8,12},{12,8},{9,1... | collective-permute-start | bytes 589832 | tf_op jit(solution)/shard_map/ppermute | solution.py:39
  32.5 1.0 collective-permute-start.4
  33.6 0.7 collective-permute-done.1
  34.3 1.7 collective-permute-start.5
  36.0 0.6 fusion.17
  37.4 0.6 add_convert_fusion
  38.7 0.8 fusion.188
  39.5 0.8 convolution_add_fusion
  40.4 1.2 add_reduce_fusion.3
  43.1 1.0 collective-permute-done.7
  44.3 0.8 copy.12
  45.2 8.8 %all-to-all-start.1 = ((bf16[32,48,128]{2,1,0:T(8,128)(2,1)}), bf16[32,48,128]{2,1,0:T(8,128)(2,1)S(1)}, u32[]{:S(2)}, u32[]{:S(2)}) async-start(bf16[32,48,128]{2,1,0:T(8,128)(2,1)} %bitcast.248), calls=%async_computation.1 | async-start | bytes 786432 | tf_op jit(solution)/shard_map/all_to_all | solution.py:43
  54.5 1.2 fusion.164
  55.7 1.3 dynamic-slice.14
  56.9 2.1 fusion.191
  59.0 6.8 %all-to-all-done.1 = bf16[32,48,128]{2,1,0:T(8,128)(2,1)S(1)} async-done(((bf16[32,48,128]{2,1,0:T(8,128)(2,1)}), bf16[32,48,128]{2,1,0:T(8,128)(2,1)S(1)}, u32[]{:S(2)}, u32[]{:S(2)}) %all-to-all-start.1) | async-done | bytes 393248 | tf_op jit(solution)/shard_map/all_to_all | solution.py:43
  65.9 0.9 fusion.127
  66.8 0.7 collective-permute-start.8
  67.5 0.8 bitcast_select_fusion
  68.4 18.4 %all_to_all.45 = bf16[32,48,128]{2,1,0:T(8,128)(2,1)S(1)} all-to-all(bf16[32,48,128]{2,1,0:T(8,128)(2,1)S(1)} %broadcast_in_dim.219), channel_id=1, replica_groups=mesh['z'=8,'y'=4,'core'=2,'section'=4] {'y','z'}, dimensions={0} | all-to-all | bytes 786432 | tf_op jit(solution)/shard_map/all_to_all | solution.py:43
  86.8 4.5 %collective-permute-start.9 = (bf16[32,48,128]{2,1,0:T(8,128)(2,1)S(1)}, bf16[32,48,128]{2,1,0:T(8,128)(2,1)S(1)}, u32[]{:S(2)}, u32[]{:S(2)}) collective-permute-start(bf16[32,48,128]{2,1,0:T(8,128)(2,1)S(1)} %all_to_all.45), channel_id=1, source_target_pairs={{0,4},{4,0},{1,5},{5,1},{2,6},{6,2},{3,7},{7,3},{8,12},{12,8},{9,1... | collective-permute-start | bytes 1179656 | tf_op jit(solution)/shard_map/ppermute | solution.py:39
  91.9 0.8 collective-permute-done.9
  96.3 16.5 %all_to_all.46 = bf16[32,48,128]{2,1,0:T(8,128)(2,1)S(1)} all-to-all(bf16[32,48,128]{2,1,0:T(8,128)(2,1)S(1)} %bitcast.256), channel_id=1, replica_groups=mesh['z'=8,'y'=4,'core'=2,'section'=4] {'y','z'}, dimensions={0} | all-to-all | bytes 786432 | tf_op jit(solution)/shard_map/all_to_all | solution.py:43
  112.9 0.8 fusion.131
  113.8 0.7 collective-permute-start.11
  114.5 18.4 %all_to_all.47 = bf16[32,48,128]{2,1,0:T(8,128)(2,1)S(1)} all-to-all(bf16[32,48,128]{2,1,0:T(8,128)(2,1)S(1)} %broadcast_in_dim.221), channel_id=1, replica_groups=mesh['z'=8,'y'=4,'core'=2,'section'=4] {'y','z'}, dimensions={0} | all-to-all | bytes 786432 | tf_op jit(solution)/shard_map/all_to_all | solution.py:43
  132.9 4.5 %collective-permute-start.12 = (bf16[32,48,128]{2,1,0:T(8,128)(2,1)S(1)}, bf16[32,48,128]{2,1,0:T(8,128)(2,1)S(1)}, u32[]{:S(2)}, u32[]{:S(2)}) collective-permute-start(bf16[32,48,128]{2,1,0:T(8,128)(2,1)S(1)} %all_to_all.47), channel_id=1, source_target_pairs={{0,4},{4,0},{1,5},{5,1},{2,6},{6,2},{3,7},{7,3},{8,12},{12,8},{9,1... | collective-permute-start | bytes 1179656 | tf_op jit(solution)/shard_map/ppermute | solution.py:39
  138.1 0.8 collective-permute-done.12
  138.9 0.6 add_reduce_fusion.1
  142.3 16.5 %all_to_all.48 = bf16[32,48,128]{2,1,0:T(8,128)(2,1)S(1)} all-to-all(bf16[32,48,128]{2,1,0:T(8,128)(2,1)S(1)} %bitcast.258), channel_id=1, replica_groups=mesh['z'=8,'y'=4,'core'=2,'section'=4] {'y','z'}, dimensions={0} | all-to-all | bytes 786432 | tf_op jit(solution)/shard_map/all_to_all | solution.py:43
  159.0 0.8 fusion.135
  159.8 1.3 collective-permute-start.14
  161.1 8.9 %collective-permute-done.14 = bf16[48,128]{1,0:T(8,128)(2,1)S(1)} collective-permute-done((bf16[48,128]{1,0:T(8,128)(2,1)S(1)}, bf16[48,128]{1,0:T(8,128)(2,1)S(1)}, u32[]{:S(2)}, u32[]{:S(2)}) %collective-permute-start.14) | collective-permute-done | bytes 12320 | tf_op jit(solution)/shard_map/ppermute | solution.py:230
  170.0 0.6 copy-done.19
  170.6 17.9 %all_to_all.49 = bf16[32,48,128]{2,1,0:T(8,128)(2,1)S(1)} all-to-all(bf16[32,48,128]{2,1,0:T(8,128)(2,1)S(1)} %broadcast_in_dim.223), channel_id=1, replica_groups=mesh['z'=8,'y'=4,'core'=2,'section'=4] {'y','z'}, dimensions={0} | all-to-all | bytes 786432 | tf_op jit(solution)/shard_map/all_to_all | solution.py:43
  188.5 4.9 %collective-permute-start.15 = (bf16[32,48,128]{2,1,0:T(8,128)(2,1)S(1)}, bf16[32,48,128]{2,1,0:T(8,128)(2,1)}, u32[]{:S(2)}, u32[]{:S(2)}) collective-permute-start(bf16[32,48,128]{2,1,0:T(8,128)(2,1)S(1)} %all_to_all.49), channel_id=1, source_target_pairs={{0,4},{4,0},{1,5},{5,1},{2,6},{6,2},{3,7},{7,3},{8,12},{12,8},{9,1... | collective-permute-start | bytes 1179656 | tf_op jit(solution)/shard_map/ppermute | solution.py:39
  194.0 0.9 collective-permute-done.15
  194.9 1.1 copy.20
  198.0 0.7 fusion.14
  199.7 1.0 collective-permute-done.16
  201.0 0.8 copy.21
  201.9 4.9 %all-to-all-start.7 = ((bf16[32,48,128]{2,1,0:T(8,128)(2,1)}), bf16[32,48,128]{2,1,0:T(8,128)(2,1)S(1)}, u32[]{:S(2)}, u32[]{:S(2)}) async-start(bf16[32,48,128]{2,1,0:T(8,128)(2,1)} %bitcast.54), calls=%async_computation.7 | async-start | bytes 786432 | tf_op jit(solution)/shard_map/all_to_all | solution.py:43
  206.8 1.1 broadcast_select_fusion.1
  208.4 1.9 convolution_convert_fusion.1
  210.3 1.9 convolution_convert_fusion
  212.2 6.5 %all-to-all-done.7 = bf16[32,48,128]{2,1,0:T(8,128)(2,1)S(1)} async-done(((bf16[32,48,128]{2,1,0:T(8,128)(2,1)}), bf16[32,48,128]{2,1,0:T(8,128)(2,1)S(1)}, u32[]{:S(2)}, u32[]{:S(2)}) %all-to-all-start.7) | async-done | bytes 393248 | tf_op jit(solution)/shard_map/all_to_all | solution.py:43
  218.8 1.6 fusion.6
  220.5 7.5 %all-to-all-start.8 = ((bf16[32,8,128]{2,1,0:T(8,128)(2,1)}), bf16[32,8,128]{2,1,0:T(8,128)(2,1)S(1)}, u32[]{:S(2)}, u32[]{:S(2)}) async-start(bf16[32,8,128]{2,1,0:T(8,128)(2,1)} %fusion.6), calls=%async_computation.8 | async-start | bytes 131072 | tf_op jit(solution)/shard_map/all_to_all | solution.py:43
  228.0 1.9 convolution_convert_fusion.2
  229.9 7.0 %all-to-all-done.8 = bf16[32,8,128]{2,1,0:T(8,128)(2,1)S(1)} async-done(((bf16[32,8,128]{2,1,0:T(8,128)(2,1)}), bf16[32,8,128]{2,1,0:T(8,128)(2,1)S(1)}, u32[]{:S(2)}, u32[]{:S(2)}) %all-to-all-start.8) | async-done | bytes 65568 | tf_op jit(solution)/shard_map/all_to_all | solution.py:43
  236.9 2.5 %collective-permute-start.17 = (bf16[8,2048]{1,0:T(8,128)(2,1)S(1)}, bf16[8,2048]{1,0:T(8,128)(2,1)S(1)}, u32[]{:S(2)}, u32[]{:S(2)}) collective-permute-start(bf16[8,2048]{1,0:T(8,128)(2,1)S(1)} %bitcast.283), channel_id=1, source_target_pairs={{0,4},{4,0},{1,5},{5,1},{2,6},{6,2},{3,7},{7,3},{8,12},{12,8},{9,1... | collective-permute-start | bytes 98312 | tf_op jit(solution)/shard_map/ppermute | solution.py:39
  239.4 0.9 collective-permute-done.17
  240.2 0.6 fusion.147
  240.9 0.6 fusion.142
  (223 shorter events, 21.0 us)
Async XLA Ops:
  0.6 30.2 %copy-start.6 = (bf16[1,224,4096]{2,1,0:T(8,128)(2,1)S(1)}, bf16[1,224,4096]{2,1,0:T(8,128)(2,1)}, u32[]{:S(2)}) copy-start(bf16[1,224,4096]{2,1,0:T(8,128)(2,1)} %param.9) | copy-start | bytes 5505028
  2.3 20.0 %all-to-all-start = ((bf16[8,8,2048]{2,1,0:T(8,128)(2,1)}), bf16[8,8,2048]{2,1,0:T(8,128)(2,1)S(1)}, u32[]{:S(2)}, u32[]{:S(2)}) async-start(bf16[8,8,2048]{2,1,0:T(8,128)(2,1)} %broadcast_in_dim.215), calls=%async_computation | async-start | bytes 524288 | tf_op jit(solution)/shard_map/all_to_all | solution.py:64
  13.3 17.7 %copy-start.21 = (pred[48]{0:T(512)(128)(4,1)}, pred[48]{0:T(512)(128)(4,1)S(1)}, u32[]{:S(2)}) copy-start(pred[48]{0:T(512)(128)(4,1)S(1)} %get-tuple-element.98) | copy-start | bytes 148
  13.4 17.7 %copy-start.27 = (pred[48]{0:T(512)(128)(4,1)}, pred[48]{0:T(512)(128)(4,1)S(1)}, u32[]{:S(2)}) copy-start(pred[48]{0:T(512)(128)(4,1)S(1)} %get-tuple-element.97) | copy-start | bytes 148
  22.3 8.8 %copy-start.7 = (bf16[1,224,4096]{2,1,0:T(8,128)(2,1)S(1)}, bf16[1,224,4096]{2,1,0:T(8,128)(2,1)}, u32[]{:S(2)}) copy-start(bf16[1,224,4096]{2,1,0:T(8,128)(2,1)} %param.11) | copy-start | bytes 5505028
  22.3 8.8 %copy-start.8 = (bf16[1,224,4096]{2,1,0:T(8,128)(2,1)S(1)}, bf16[1,224,4096]{2,1,0:T(8,128)(2,1)}, u32[]{:S(2)}) copy-start(bf16[1,224,4096]{2,1,0:T(8,128)(2,1)} %param.10) | copy-start | bytes 5505028
  22.5 10.1 %collective-permute-start = (bf16[48,2048]{1,0:T(8,128)(2,1)S(1)}, bf16[48,2048]{1,0:T(8,128)(2,1)S(1)}, u32[]{:S(2)}, u32[]{:S(2)}) collective-permute-start(bf16[48,2048]{1,0:T(8,128)(2,1)S(1)} %convolution_convert_fusion.3), channel_id=1, source_target_pairs={{0,16},{8,24},{16,0},{24,8},{1,17},{9,25},{17,1},{25,9},{2,18},{10... | collective-permute-start | bytes 589832 | tf_op jit(solution)/shard_map/ppermute | solution.py:69
  25.5 8.8 %collective-permute-start.1 = (bf16[48,2048]{1,0:T(8,128)(2,1)S(1)}, bf16[48,2048]{1,0:T(8,128)(2,1)S(1)}, u32[]{:S(2)}, u32[]{:S(2)}) collective-permute-start(bf16[48,2048]{1,0:T(8,128)(2,1)S(1)} %convolution_convert_fusion.3), channel_id=1, source_target_pairs={{0,8},{8,16},{16,24},{24,0},{1,9},{9,17},{17,25},{25,1},{2,10},{10... | collective-permute-start | bytes 589832 | tf_op jit(solution)/shard_map/ppermute | solution.py:69
  25.9 10.1 %collective-permute-start.2 = (bf16[48,2048]{1,0:T(8,128)(2,1)S(1)}, bf16[48,2048]{1,0:T(8,128)(2,1)S(1)}, u32[]{:S(2)}, u32[]{:S(2)}) collective-permute-start(bf16[48,2048]{1,0:T(8,128)(2,1)S(1)} %convolution_convert_fusion.3), channel_id=1, source_target_pairs={{0,24},{8,0},{16,8},{24,16},{1,25},{9,1},{17,9},{25,17},{2,26},{10... | collective-permute-start | bytes 589832 | tf_op jit(solution)/shard_map/ppermute | solution.py:69
  28.2 8.4 %collective-permute-start.3 = (bf16[48,2048]{1,0:T(8,128)(2,1)S(1)}, bf16[48,2048]{1,0:T(8,128)(2,1)S(1)}, u32[]{:S(2)}, u32[]{:S(2)}) collective-permute-start(bf16[48,2048]{1,0:T(8,128)(2,1)S(1)} %convolution_convert_fusion.3), channel_id=1, source_target_pairs={{0,4},{4,0},{1,5},{5,1},{2,6},{6,2},{3,7},{7,3},{8,12},{12,8},{9,1... | collective-permute-start | bytes 589832 | tf_op jit(solution)/shard_map/ppermute | solution.py:39
  31.9 8.5 %copy-start.9 = (bf16[256,2048]{1,0:T(8,128)(2,1)}, bf16[256,2048]{1,0:T(8,128)(2,1)S(1)}, u32[]{:S(2)}) copy-start(bf16[256,2048]{1,0:T(8,128)(2,1)S(1)} %pad.37) | copy-start | bytes 3145732
  32.5 10.1 %copy-start = (bf16[512,2048]{1,0:T(8,128)(2,1)}, bf16[512,2048]{1,0:T(8,128)(2,1)S(1)}, u32[]{:S(2)}) copy-start(bf16[512,2048]{1,0:T(8,128)(2,1)S(1)} %fusion.4) | copy-start | bytes 6291460
  32.5 4.0 %collective-permute-start.4 = (bf16[48,2048]{1,0:T(8,128)(2,1)S(1)}, bf16[48,2048]{1,0:T(8,128)(2,1)S(1)}, u32[]{:S(2)}, u32[]{:S(2)}) collective-permute-start(bf16[48,2048]{1,0:T(8,128)(2,1)S(1)} %collective-permute-done), channel_id=1, source_target_pairs={{0,4},{4,0},{1,5},{5,1},{2,6},{6,2},{3,7},{7,3},{8,12},{12,8},{9,1... | collective-permute-start | bytes 589832 | tf_op jit(solution)/shard_map/ppermute | solution.py:39
  34.3 2.8 %collective-permute-start.5 = (bf16[48,2048]{1,0:T(8,128)(2,1)S(1)}, bf16[48,2048]{1,0:T(8,128)(2,1)S(1)}, u32[]{:S(2)}, u32[]{:S(2)}) collective-permute-start(bf16[48,2048]{1,0:T(8,128)(2,1)S(1)} %collective-permute-done.1), channel_id=1, source_target_pairs={{0,4},{4,0},{1,5},{5,1},{2,6},{6,2},{3,7},{7,3},{8,12},{12,8},{9,1... | collective-permute-start | bytes 589832 | tf_op jit(solution)/shard_map/ppermute | solution.py:39
  36.0 1.4 collective-permute-start.6
  38.0 2.4 copy-start.4
  38.7 1.6 copy-start.25
  40.4 1.7 copy-start.13
  40.4 1.7 copy-start.22
  42.2 1.8 collective-permute-start.7
  45.2 20.6 %all-to-all-start.1 = ((bf16[32,48,128]{2,1,0:T(8,128)(2,1)}), bf16[32,48,128]{2,1,0:T(8,128)(2,1)S(1)}, u32[]{:S(2)}, u32[]{:S(2)}) async-start(bf16[32,48,128]{2,1,0:T(8,128)(2,1)} %bitcast.248), calls=%async_computation.1 | async-start | bytes 786432 | tf_op jit(solution)/shard_map/all_to_all | solution.py:43
  66.8 0.7 collective-permute-start.8
  68.4 24.5 %copy-start.10 = (bf16[256,2048]{1,0:T(8,128)(2,1)S(1)}, bf16[256,2048]{1,0:T(8,128)(2,1)}, u32[]{:S(2)}) copy-start(bf16[256,2048]{1,0:T(8,128)(2,1)} %copy-done.9) | copy-start | bytes 3145732
  68.4 24.5 %copy-start.14 = (f32[96,512]{1,0:T(8,128)S(1)}, f32[96,512]{1,0:T(8,128)}, u32[]{:S(2)}) copy-start(f32[96,512]{1,0:T(8,128)} %copy-done.13) | copy-start | bytes 589828
  68.4 24.5 %copy-start.35 = (f32[96,256]{1,0:T(8,128)S(1)}, f32[96,256]{1,0:T(8,128)}, u32[]{:S(2)}) copy-start(f32[96,256]{1,0:T(8,128)} %get-tuple-element.62) | copy-start | bytes 294916
  86.8 5.9 %collective-permute-start.9 = (bf16[32,48,128]{2,1,0:T(8,128)(2,1)S(1)}, bf16[32,48,128]{2,1,0:T(8,128)(2,1)S(1)}, u32[]{:S(2)}, u32[]{:S(2)}) collective-permute-start(bf16[32,48,128]{2,1,0:T(8,128)(2,1)S(1)} %all_to_all.45), channel_id=1, source_target_pairs={{0,4},{4,0},{1,5},{5,1},{2,6},{6,2},{3,7},{7,3},{8,12},{12,8},{9,1... | collective-permute-start | bytes 1179656 | tf_op jit(solution)/shard_map/ppermute | solution.py:39
  92.9 1.1 copy-start.23
  93.4 1.6 copy-start.1
  94.0 1.8 collective-permute-start.10
  95.9 17.1 %copy-start.29 = (pred[48]{0:T(512)(128)(4,1)S(1)}, pred[48]{0:T(512)(128)(4,1)}, u32[]{:S(2)}) copy-start(pred[48]{0:T(512)(128)(4,1)} %iota_compare_fusion.6) | copy-start | bytes 148
  95.9 17.1 %copy-start.31 = (f32[128]{0:T(128)S(1)}, f32[128]{0:T(128)}, u32[]{:S(2)}) copy-start(f32[128]{0:T(128)} %fusion.164) | copy-start | bytes 1540
  95.9 17.1 %copy-start.33 = (f32[48]{0:T(128)S(1)}, f32[48]{0:T(128)}, u32[]{:S(2)}) copy-start(f32[48]{0:T(128)} %dynamic-slice.14) | copy-start | bytes 580
  113.8 0.7 collective-permute-start.11
  114.5 24.5 %copy-start.11 = (bf16[256,2048]{1,0:T(8,128)(2,1)S(1)}, bf16[256,2048]{1,0:T(8,128)(2,1)}, u32[]{:S(2)}) copy-start(bf16[256,2048]{1,0:T(8,128)(2,1)} %copy-done.9) | copy-start | bytes 3145732
  132.9 5.9 %collective-permute-start.12 = (bf16[32,48,128]{2,1,0:T(8,128)(2,1)S(1)}, bf16[32,48,128]{2,1,0:T(8,128)(2,1)S(1)}, u32[]{:S(2)}, u32[]{:S(2)}) collective-permute-start(bf16[32,48,128]{2,1,0:T(8,128)(2,1)S(1)} %all_to_all.47), channel_id=1, source_target_pairs={{0,4},{4,0},{1,5},{5,1},{2,6},{6,2},{3,7},{7,3},{8,12},{12,8},{9,1... | collective-permute-start | bytes 1179656 | tf_op jit(solution)/shard_map/ppermute | solution.py:39
  139.5 1.6 copy-start.2
  140.1 1.8 collective-permute-start.13
  159.8 10.2 %collective-permute-start.14 = (bf16[48,128]{1,0:T(8,128)(2,1)S(1)}, bf16[48,128]{1,0:T(8,128)(2,1)S(1)}, u32[]{:S(2)}, u32[]{:S(2)}) collective-permute-start(bf16[48,128]{1,0:T(8,128)(2,1)S(1)} %fusion.135), channel_id=1, source_target_pairs={{1,0},{5,4},{9,8},{13,12},{17,16},{21,20},{25,24},{29,28},{33,32},... | collective-permute-start | bytes 36872 | tf_op jit(solution)/shard_map/ppermute | solution.py:230
  170.0 0.6 copy-start.19
  188.5 6.4 %collective-permute-start.15 = (bf16[32,48,128]{2,1,0:T(8,128)(2,1)S(1)}, bf16[32,48,128]{2,1,0:T(8,128)(2,1)}, u32[]{:S(2)}, u32[]{:S(2)}) collective-permute-start(bf16[32,48,128]{2,1,0:T(8,128)(2,1)S(1)} %all_to_all.49), channel_id=1, source_target_pairs={{0,4},{4,0},{1,5},{5,1},{2,6},{6,2},{3,7},{7,3},{8,12},{12,8},{9,1... | collective-permute-start | bytes 1179656 | tf_op jit(solution)/shard_map/ppermute | solution.py:39
  193.4 2.6 %copy-start.12 = (bf16[256,2048]{1,0:T(8,128)(2,1)S(1)}, bf16[256,2048]{1,0:T(8,128)(2,1)}, u32[]{:S(2)}) copy-start(bf16[256,2048]{1,0:T(8,128)(2,1)} %copy-done.9) | copy-start | bytes 3145732
  193.4 2.6 %copy-start.15 = (f32[96,512]{1,0:T(8,128)S(1)}, f32[96,512]{1,0:T(8,128)}, u32[]{:S(2)}) copy-start(f32[96,512]{1,0:T(8,128)} %copy-done.13) | copy-start | bytes 589828
  193.4 2.6 %copy-start.36 = (f32[96,256]{1,0:T(8,128)S(1)}, f32[96,256]{1,0:T(8,128)}, u32[]{:S(2)}) copy-start(f32[96,256]{1,0:T(8,128)} %get-tuple-element.62) | copy-start | bytes 294916
  196.0 1.6 copy-start.3
  196.0 2.0 copy-start.5
  196.0 2.0 copy-start.26
  198.0 0.7 copy-start.24
  198.0 0.7 copy-start.28
  198.9 1.8 collective-permute-start.16
  201.9 16.8 %all-to-all-start.7 = ((bf16[32,48,128]{2,1,0:T(8,128)(2,1)}), bf16[32,48,128]{2,1,0:T(8,128)(2,1)S(1)}, u32[]{:S(2)}, u32[]{:S(2)}) async-start(bf16[32,48,128]{2,1,0:T(8,128)(2,1)} %bitcast.54), calls=%async_computation.7 | async-start | bytes 786432 | tf_op jit(solution)/shard_map/all_to_all | solution.py:43
  208.1 2.2 copy-start.16
  208.1 2.2 copy-start.17
  210.2 8.6 %copy-start.18 = (bf16[256,48]{1,0:T(8,128)(2,1)S(1)}, bf16[256,48]{1,0:T(8,128)(2,1)}, u32[]{:S(2)}) copy-start(bf16[256,48]{1,0:T(8,128)(2,1)} %fusion.100) | copy-start | bytes 73732
  210.2 8.6 %copy-start.20 = (bf16[48,128]{1,0:T(8,128)(2,1)S(1)}, bf16[48,128]{1,0:T(8,128)(2,1)}, u32[]{:S(2)}) copy-start(bf16[48,128]{1,0:T(8,128)(2,1)} %copy-done.19) | copy-start | bytes 36868
  210.2 8.6 %copy-start.30 = (pred[48]{0:T(512)(128)(4,1)S(1)}, pred[48]{0:T(512)(128)(4,1)}, u32[]{:S(2)}) copy-start(pred[48]{0:T(512)(128)(4,1)} %iota_compare_fusion.6) | copy-start | bytes 148
  210.2 8.6 %copy-start.32 = (f32[128]{0:T(128)S(1)}, f32[128]{0:T(128)}, u32[]{:S(2)}) copy-start(f32[128]{0:T(128)} %fusion.164) | copy-start | bytes 1540
  210.3 8.6 %copy-start.34 = (f32[48]{0:T(128)S(1)}, f32[48]{0:T(128)}, u32[]{:S(2)}) copy-start(f32[48]{0:T(128)} %dynamic-slice.14) | copy-start | bytes 580
  220.5 16.4 %all-to-all-start.8 = ((bf16[32,8,128]{2,1,0:T(8,128)(2,1)}), bf16[32,8,128]{2,1,0:T(8,128)(2,1)S(1)}, u32[]{:S(2)}, u32[]{:S(2)}) async-start(bf16[32,8,128]{2,1,0:T(8,128)(2,1)} %fusion.6), calls=%async_computation.8 | async-start | bytes 131072 | tf_op jit(solution)/shard_map/all_to_all | solution.py:43
  236.9 3.3 %collective-permute-start.17 = (bf16[8,2048]{1,0:T(8,128)(2,1)S(1)}, bf16[8,2048]{1,0:T(8,128)(2,1)S(1)}, u32[]{:S(2)}, u32[]{:S(2)}) collective-permute-start(bf16[8,2048]{1,0:T(8,128)(2,1)S(1)} %bitcast.283), channel_id=1, source_target_pairs={{0,4},{4,0},{1,5},{5,1},{2,6},{6,2},{3,7},{7,3},{8,12},{12,8},{9,1... | collective-permute-start | bytes 98312 | tf_op jit(solution)/shard_map/ppermute | solution.py:39

commit v7 on v6

--- a/solution.py
+++ b/solution.py
@@ -6,7 +6,7 @@
 
 NZ, NY, NC, NS = 8, 4, 2, 4
 DP = ("z", "y", "core")
-PLANE = ("y", "z")
+PLANE = ("z", "y")
 LIVE = 85
 PACK = 12
 GROUP = 48
@@ -88,7 +88,7 @@
             packing(counts, y, core),
             selection(counts, y, core, core),
             selection(counts, y, 1 - core, core),
-            wanted_rows(counts, y // 2),
+            wanted_rows(counts, lax.axis_index("z") // 4),
         )
     )
     mine, other, weights = spread_rows(own, weights, pack)
@@ -100,7 +100,7 @@
     shape = (NZ * NY * 8, GROUP)
     index, row = (lax.broadcasted_iota(jnp.int32, shape, d) for d in range(2))
     place, piece = index // 8, index % 8
-    slot = (place % NZ) * NY * NC + (place // NZ) * NC + piece // 2
+    slot = place * NC + piece // 2
     micro = piece % 2
     limit = jnp.where(micro == 0, counts[0], counts[1])
     hit = (piece < 4) & (row_of(micro, slot) == part * GROUP + row) & (slot < limit)
@@ -116,7 +116,7 @@
     lanes = half // BLOCKS
     z, y, core = lax.axis_index("z"), lax.axis_index("y"), lax.axis_index("core")
     section = lax.axis_index("section")
-    part, block = y // 2, (y % 2) * NZ + z
+    part, block = z // 4, (z % 4) * NY + y
 
     def halves(x):
         return (

time: 243 us -> 241 us (level)
  starting transfers between devices: 62.1 us -> 56.5 us
  waiting for transfers between devices: 36.6 us -> 40.8 us
    all_to_all x3, waiting for transfers between devices: 20.2 us -> 24.4 us  [exchange(): return lax.all_to_all(x, PLANE, 0, 0, tiled=True)]
    all_to_all x3, starting transfers between devices: 21.2 us -> 17.7 us  [exchange(): return lax.all_to_all(x, PLANE, 0, 0, tiled=True)]
  transfers between devices with their start and end apart: 22 -> 22, of which waited for: 15 -> 15; matrix products, arithmetic and copies ran while one was open for 11% -> 12% of each run, Pallas kernels for 0% -> 0%
where the time goes in v7:
time: 241 us; the launch traced here: 240 us
  blocking collectives  87.3 us (36%)
  starting transfers between devices  56.5 us (23%)
  waiting for transfers between devices  40.8 us (17%)
  matrix products  18.9 us (8%)
  local copies, waits for them, and re-layouts  18.1 us (8%)
  other arithmetic  15.5 us (6%)
  between operations  2.53 us (1%)
    all_to_all x5, blocking collectives, exchange(): return lax.all_to_all(x, PLANE, 0, 0, tiled=True)  87.3 us
    all_to_all x3, waiting for transfers between devices, exchange(): return lax.all_to_all(x, PLANE, 0, 0, tiled=True)  24.4 us
    ppermute x12, starting transfers between devices, swap_core(): return lax.ppermute(x, 'core', [(0, 1), (1, 0)])  21.5 us
    all_to_all x3, starting transfers between devices, exchange(): return lax.all_to_all(x, PLANE, 0, 0, tiled=True)  17.7 us
    all_to_all x1, starting transfers between devices, spread_rows(): lax.all_to_all(jnp.broadcast_to(own[None], (NZ, count, half)), 'z', 0, 0,...  9 us
    ppermute x3, waiting for transfers between devices, on_device(): moved = lax.ppermute(grad_tile, 'section', [(NS - 1 - step, NS - 2 - step)])  8.87 us
    dot_general x12, matrix products, dot_nn(): lax.dot_general(a, b, (((1,), (0,)), ((), ())), preferred_element_type=F32)  6.93 us
    ppermute x12, waiting for transfers between devices, swap_core(): return lax.ppermute(x, 'core', [(0, 1), (1, 0)])  6.88 us
  transfers between devices with their start and end apart: 22, of which 15 were waited for; matrix products, arithmetic and copies ran while one was open for 12% of the time, Pallas kernels for 0%

profile of v7, /device:TPU:1, one launch (start us, length us, event | category | flops | bytes accessed | tf_op | source)
XLA Modules:
  0.0 239.6 jit_solution(2394188189350247180)
XLA Ops:
  0.6 0.9 pad_maximum_fusion.15
  1.6 0.7 broadcast_in_dim.215
  2.3 9.0 %all-to-all-start = ((bf16[8,8,2048]{2,1,0:T(8,128)(2,1)}), bf16[8,8,2048]{2,1,0:T(8,128)(2,1)S(1)}, u32[]{:S(2)}, u32[]{:S(2)}) async-start(bf16[8,8,2048]{2,1,0:T(8,128)(2,1)} %broadcast_in_dim.215), calls=%async_computation | async-start | bytes 524288 | tf_op jit(solution)/shard_map/all_to_all | solution.py:64
  11.3 1.3 fusion.185
  13.5 1.3 compare_select_fusion.2
  17.1 1.8 fusion.79
  19.1 2.4 fusion.93
  21.4 0.7 constant_dynamic-slice_fusion.4
  22.4 3.0 %collective-permute-start = (bf16[48,2048]{1,0:T(8,128)(2,1)S(1)}, bf16[48,2048]{1,0:T(8,128)(2,1)S(1)}, u32[]{:S(2)}, u32[]{:S(2)}) collective-permute-start(bf16[48,2048]{1,0:T(8,128)(2,1)S(1)} %convolution_convert_fusion.3), channel_id=1, source_target_pairs={{0,16},{8,24},{16,0},{24,8},{1,17},{9,25},{17,1},{25,9},{2,18},{10... | collective-permute-start | bytes 589832 | tf_op jit(solution)/shard_map/ppermute | solution.py:69
  25.8 2.3 collective-permute-start.2
  28.0 2.8 %collective-permute-start.3 = (bf16[48,2048]{1,0:T(8,128)(2,1)S(1)}, bf16[48,2048]{1,0:T(8,128)(2,1)S(1)}, u32[]{:S(2)}, u32[]{:S(2)}) collective-permute-start(bf16[48,2048]{1,0:T(8,128)(2,1)S(1)} %convolution_convert_fusion.3), channel_id=1, source_target_pairs={{0,4},{4,0},{1,5},{5,1},{2,6},{6,2},{3,7},{7,3},{8,12},{12,8},{9,1... | collective-permute-start | bytes 589832 | tf_op jit(solution)/shard_map/ppermute | solution.py:39
  32.5 0.9 collective-permute-start.4
  33.5 0.7 collective-permute-done.1
  34.1 1.8 collective-permute-start.5
  35.9 0.6 fusion.17
  37.3 0.6 add_convert_fusion
  38.7 0.8 fusion.181
  39.5 0.8 convolution_add_fusion
  40.3 1.2 add_reduce_fusion.3
  43.0 1.0 collective-permute-done.7
  44.3 0.8 copy.12
  45.1 8.7 %all-to-all-start.1 = ((bf16[32,48,128]{2,1,0:T(8,128)(2,1)}), bf16[32,48,128]{2,1,0:T(8,128)(2,1)S(1)}, u32[]{:S(2)}, u32[]{:S(2)}) async-start(bf16[32,48,128]{2,1,0:T(8,128)(2,1)} %bitcast.248), calls=%async_computation.1 | async-start | bytes 786432 | tf_op jit(solution)/shard_map/all_to_all | solution.py:43
  54.4 1.2 fusion.157
  55.6 1.3 dynamic-slice.14
  56.8 2.1 fusion.184
  58.9 8.8 %all-to-all-done.1 = bf16[32,48,128]{2,1,0:T(8,128)(2,1)S(1)} async-done(((bf16[32,48,128]{2,1,0:T(8,128)(2,1)}), bf16[32,48,128]{2,1,0:T(8,128)(2,1)S(1)}, u32[]{:S(2)}, u32[]{:S(2)}) %all-to-all-start.1) | async-done | bytes 393248 | tf_op jit(solution)/shard_map/all_to_all | solution.py:43
  67.9 0.9 fusion.120
  68.8 0.7 collective-permute-start.8
  69.4 0.8 bitcast_select_fusion
  70.4 17.7 %all_to_all.45 = bf16[32,48,128]{2,1,0:T(8,128)(2,1)S(1)} all-to-all(bf16[32,48,128]{2,1,0:T(8,128)(2,1)S(1)} %broadcast_in_dim.219), channel_id=1, replica_groups=mesh['z'=8,'y'=4,'core'=2,'section'=4] {'z','y'}, dimensions={0} | all-to-all | bytes 786432 | tf_op jit(solution)/shard_map/all_to_all | solution.py:43
  88.1 3.5 %collective-permute-start.9 = (bf16[32,48,128]{2,1,0:T(8,128)(2,1)S(1)}, bf16[32,48,128]{2,1,0:T(8,128)(2,1)S(1)}, u32[]{:S(2)}, u32[]{:S(2)}) collective-permute-start(bf16[32,48,128]{2,1,0:T(8,128)(2,1)S(1)} %all_to_all.45), channel_id=1, source_target_pairs={{0,4},{4,0},{1,5},{5,1},{2,6},{6,2},{3,7},{7,3},{8,12},{12,8},{9,1... | collective-permute-start | bytes 1179656 | tf_op jit(solution)/shard_map/ppermute | solution.py:39
  92.2 0.8 collective-permute-done.9
  93.1 0.6 add_reduce_fusion.2
  96.5 17.6 %all_to_all.46 = bf16[32,48,128]{2,1,0:T(8,128)(2,1)S(1)} all-to-all(bf16[32,48,128]{2,1,0:T(8,128)(2,1)S(1)} %bitcast.256), channel_id=1, replica_groups=mesh['z'=8,'y'=4,'core'=2,'section'=4] {'z','y'}, dimensions={0} | all-to-all | bytes 786432 | tf_op jit(solution)/shard_map/all_to_all | solution.py:43
  114.3 0.8 fusion.124
  115.1 0.7 collective-permute-start.11
  115.9 17.7 %all_to_all.47 = bf16[32,48,128]{2,1,0:T(8,128)(2,1)S(1)} all-to-all(bf16[32,48,128]{2,1,0:T(8,128)(2,1)S(1)} %broadcast_in_dim.221), channel_id=1, replica_groups=mesh['z'=8,'y'=4,'core'=2,'section'=4] {'z','y'}, dimensions={0} | all-to-all | bytes 786432 | tf_op jit(solution)/shard_map/all_to_all | solution.py:43
  133.6 3.5 %collective-permute-start.12 = (bf16[32,48,128]{2,1,0:T(8,128)(2,1)S(1)}, bf16[32,48,128]{2,1,0:T(8,128)(2,1)S(1)}, u32[]{:S(2)}, u32[]{:S(2)}) collective-permute-start(bf16[32,48,128]{2,1,0:T(8,128)(2,1)S(1)} %all_to_all.47), channel_id=1, source_target_pairs={{0,4},{4,0},{1,5},{5,1},{2,6},{6,2},{3,7},{7,3},{8,12},{12,8},{9,1... | collective-permute-start | bytes 1179656 | tf_op jit(solution)/shard_map/ppermute | solution.py:39
  137.7 0.8 collective-permute-done.12
  142.0 17.6 %all_to_all.48 = bf16[32,48,128]{2,1,0:T(8,128)(2,1)S(1)} all-to-all(bf16[32,48,128]{2,1,0:T(8,128)(2,1)S(1)} %bitcast.258), channel_id=1, replica_groups=mesh['z'=8,'y'=4,'core'=2,'section'=4] {'z','y'}, dimensions={0} | all-to-all | bytes 786432 | tf_op jit(solution)/shard_map/all_to_all | solution.py:43
  159.7 0.8 fusion.128
  160.6 1.3 collective-permute-start.14
  161.9 8.9 %collective-permute-done.14 = bf16[48,128]{1,0:T(8,128)(2,1)S(1)} collective-permute-done((bf16[48,128]{1,0:T(8,128)(2,1)S(1)}, bf16[48,128]{1,0:T(8,128)(2,1)S(1)}, u32[]{:S(2)}, u32[]{:S(2)}) %collective-permute-start.14) | collective-permute-done | bytes 12320 | tf_op jit(solution)/shard_map/ppermute | solution.py:230
  170.8 0.6 copy-done.19
  171.4 16.7 %all_to_all.49 = bf16[32,48,128]{2,1,0:T(8,128)(2,1)S(1)} all-to-all(bf16[32,48,128]{2,1,0:T(8,128)(2,1)S(1)} %broadcast_in_dim.223), channel_id=1, replica_groups=mesh['z'=8,'y'=4,'core'=2,'section'=4] {'z','y'}, dimensions={0} | all-to-all | bytes 786432 | tf_op jit(solution)/shard_map/all_to_all | solution.py:43
  188.1 4.3 %collective-permute-start.15 = (bf16[32,48,128]{2,1,0:T(8,128)(2,1)S(1)}, bf16[32,48,128]{2,1,0:T(8,128)(2,1)}, u32[]{:S(2)}, u32[]{:S(2)}) collective-permute-start(bf16[32,48,128]{2,1,0:T(8,128)(2,1)S(1)} %all_to_all.49), channel_id=1, source_target_pairs={{0,4},{4,0},{1,5},{5,1},{2,6},{6,2},{3,7},{7,3},{8,12},{12,8},{9,1... | collective-permute-start | bytes 1179656 | tf_op jit(solution)/shard_map/ppermute | solution.py:39
  193.0 0.9 collective-permute-done.15
  193.9 1.1 copy.20
  197.1 0.7 fusion.14
  198.7 1.0 collective-permute-done.16
  200.1 0.8 copy.21
  200.9 4.0 %all-to-all-start.7 = ((bf16[32,48,128]{2,1,0:T(8,128)(2,1)}), bf16[32,48,128]{2,1,0:T(8,128)(2,1)S(1)}, u32[]{:S(2)}, u32[]{:S(2)}) async-start(bf16[32,48,128]{2,1,0:T(8,128)(2,1)} %bitcast.54), calls=%async_computation.7 | async-start | bytes 786432 | tf_op jit(solution)/shard_map/all_to_all | solution.py:43
  205.0 1.1 broadcast_select_fusion.1
  206.5 1.9 convolution_convert_fusion.1
  208.4 1.9 convolution_convert_fusion
  210.3 8.5 %all-to-all-done.7 = bf16[32,48,128]{2,1,0:T(8,128)(2,1)S(1)} async-done(((bf16[32,48,128]{2,1,0:T(8,128)(2,1)}), bf16[32,48,128]{2,1,0:T(8,128)(2,1)S(1)}, u32[]{:S(2)}, u32[]{:S(2)}) %all-to-all-start.7) | async-done | bytes 393248 | tf_op jit(solution)/shard_map/all_to_all | solution.py:43
  219.1 1.6 fusion.6
  220.7 5.0 %all-to-all-start.8 = ((bf16[32,8,128]{2,1,0:T(8,128)(2,1)}), bf16[32,8,128]{2,1,0:T(8,128)(2,1)S(1)}, u32[]{:S(2)}, u32[]{:S(2)}) async-start(bf16[32,8,128]{2,1,0:T(8,128)(2,1)} %fusion.6), calls=%async_computation.8 | async-start | bytes 131072 | tf_op jit(solution)/shard_map/all_to_all | solution.py:43
  225.7 1.9 convolution_convert_fusion.2
  227.5 7.0 %all-to-all-done.8 = bf16[32,8,128]{2,1,0:T(8,128)(2,1)S(1)} async-done(((bf16[32,8,128]{2,1,0:T(8,128)(2,1)}), bf16[32,8,128]{2,1,0:T(8,128)(2,1)S(1)}, u32[]{:S(2)}, u32[]{:S(2)}) %all-to-all-start.8) | async-done | bytes 65568 | tf_op jit(solution)/shard_map/all_to_all | solution.py:43
  234.6 2.8 %collective-permute-start.17 = (bf16[8,2048]{1,0:T(8,128)(2,1)S(1)}, bf16[8,2048]{1,0:T(8,128)(2,1)S(1)}, u32[]{:S(2)}, u32[]{:S(2)}) collective-permute-start(bf16[8,2048]{1,0:T(8,128)(2,1)S(1)} %bitcast.283), channel_id=1, source_target_pairs={{0,4},{4,0},{1,5},{5,1},{2,6},{6,2},{3,7},{7,3},{8,12},{12,8},{9,1... | collective-permute-start | bytes 98312 | tf_op jit(solution)/shard_map/ppermute | solution.py:39
  237.4 0.9 collective-permute-done.17
  238.3 0.6 fusion.140
  238.9 0.6 fusion.135
  (223 shorter events, 21.0 us)
Async XLA Ops:
  0.6 30.2 %copy-start.6 = (bf16[1,224,4096]{2,1,0:T(8,128)(2,1)S(1)}, bf16[1,224,4096]{2,1,0:T(8,128)(2,1)}, u32[]{:S(2)}) copy-start(bf16[1,224,4096]{2,1,0:T(8,128)(2,1)} %param.9) | copy-start | bytes 5505028
  2.3 19.9 %all-to-all-start = ((bf16[8,8,2048]{2,1,0:T(8,128)(2,1)}), bf16[8,8,2048]{2,1,0:T(8,128)(2,1)S(1)}, u32[]{:S(2)}, u32[]{:S(2)}) async-start(bf16[8,8,2048]{2,1,0:T(8,128)(2,1)} %broadcast_in_dim.215), calls=%async_computation | async-start | bytes 524288 | tf_op jit(solution)/shard_map/all_to_all | solution.py:64
  13.4 17.7 %copy-start.21 = (pred[48]{0:T(512)(128)(4,1)}, pred[48]{0:T(512)(128)(4,1)S(1)}, u32[]{:S(2)}) copy-start(pred[48]{0:T(512)(128)(4,1)S(1)} %get-tuple-element.98) | copy-start | bytes 148
  13.4 17.7 %copy-start.27 = (pred[48]{0:T(512)(128)(4,1)}, pred[48]{0:T(512)(128)(4,1)S(1)}, u32[]{:S(2)}) copy-start(pred[48]{0:T(512)(128)(4,1)S(1)} %get-tuple-element.97) | copy-start | bytes 148
  22.2 8.9 %copy-start.7 = (bf16[1,224,4096]{2,1,0:T(8,128)(2,1)S(1)}, bf16[1,224,4096]{2,1,0:T(8,128)(2,1)}, u32[]{:S(2)}) copy-start(bf16[1,224,4096]{2,1,0:T(8,128)(2,1)} %param.11) | copy-start | bytes 5505028
  22.2 8.9 %copy-start.8 = (bf16[1,224,4096]{2,1,0:T(8,128)(2,1)S(1)}, bf16[1,224,4096]{2,1,0:T(8,128)(2,1)}, u32[]{:S(2)}) copy-start(bf16[1,224,4096]{2,1,0:T(8,128)(2,1)} %param.10) | copy-start | bytes 5505028
  22.4 10.2 %collective-permute-start = (bf16[48,2048]{1,0:T(8,128)(2,1)S(1)}, bf16[48,2048]{1,0:T(8,128)(2,1)S(1)}, u32[]{:S(2)}, u32[]{:S(2)}) collective-permute-start(bf16[48,2048]{1,0:T(8,128)(2,1)S(1)} %convolution_convert_fusion.3), channel_id=1, source_target_pairs={{0,16},{8,24},{16,0},{24,8},{1,17},{9,25},{17,1},{25,9},{2,18},{10... | collective-permute-start | bytes 589832 | tf_op jit(solution)/shard_map/ppermute | solution.py:69
  25.4 8.8 %collective-permute-start.1 = (bf16[48,2048]{1,0:T(8,128)(2,1)S(1)}, bf16[48,2048]{1,0:T(8,128)(2,1)S(1)}, u32[]{:S(2)}, u32[]{:S(2)}) collective-permute-start(bf16[48,2048]{1,0:T(8,128)(2,1)S(1)} %convolution_convert_fusion.3), channel_id=1, source_target_pairs={{0,8},{8,16},{16,24},{24,0},{1,9},{9,17},{17,25},{25,1},{2,10},{10... | collective-permute-start | bytes 589832 | tf_op jit(solution)/shard_map/ppermute | solution.py:69
  25.8 10.1 %collective-permute-start.2 = (bf16[48,2048]{1,0:T(8,128)(2,1)S(1)}, bf16[48,2048]{1,0:T(8,128)(2,1)S(1)}, u32[]{:S(2)}, u32[]{:S(2)}) collective-permute-start(bf16[48,2048]{1,0:T(8,128)(2,1)S(1)} %convolution_convert_fusion.3), channel_id=1, source_target_pairs={{0,24},{8,0},{16,8},{24,16},{1,25},{9,1},{17,9},{25,17},{2,26},{10... | collective-permute-start | bytes 589832 | tf_op jit(solution)/shard_map/ppermute | solution.py:69
  28.0 8.4 %collective-permute-start.3 = (bf16[48,2048]{1,0:T(8,128)(2,1)S(1)}, bf16[48,2048]{1,0:T(8,128)(2,1)S(1)}, u32[]{:S(2)}, u32[]{:S(2)}) collective-permute-start(bf16[48,2048]{1,0:T(8,128)(2,1)S(1)} %convolution_convert_fusion.3), channel_id=1, source_target_pairs={{0,4},{4,0},{1,5},{5,1},{2,6},{6,2},{3,7},{7,3},{8,12},{12,8},{9,1... | collective-permute-start | bytes 589832 | tf_op jit(solution)/shard_map/ppermute | solution.py:39
  31.9 8.4 %copy-start.9 = (bf16[256,2048]{1,0:T(8,128)(2,1)}, bf16[256,2048]{1,0:T(8,128)(2,1)S(1)}, u32[]{:S(2)}) copy-start(bf16[256,2048]{1,0:T(8,128)(2,1)S(1)} %pad.37) | copy-start | bytes 3145732
  32.5 10.0 %copy-start = (bf16[512,2048]{1,0:T(8,128)(2,1)}, bf16[512,2048]{1,0:T(8,128)(2,1)S(1)}, u32[]{:S(2)}) copy-start(bf16[512,2048]{1,0:T(8,128)(2,1)S(1)} %fusion.4) | copy-start | bytes 6291460
  32.5 3.9 %collective-permute-start.4 = (bf16[48,2048]{1,0:T(8,128)(2,1)S(1)}, bf16[48,2048]{1,0:T(8,128)(2,1)S(1)}, u32[]{:S(2)}, u32[]{:S(2)}) collective-permute-start(bf16[48,2048]{1,0:T(8,128)(2,1)S(1)} %collective-permute-done), channel_id=1, source_target_pairs={{0,4},{4,0},{1,5},{5,1},{2,6},{6,2},{3,7},{7,3},{8,12},{12,8},{9,1... | collective-permute-start | bytes 589832 | tf_op jit(solution)/shard_map/ppermute | solution.py:39
  34.1 2.8 %collective-permute-start.5 = (bf16[48,2048]{1,0:T(8,128)(2,1)S(1)}, bf16[48,2048]{1,0:T(8,128)(2,1)S(1)}, u32[]{:S(2)}, u32[]{:S(2)}) collective-permute-start(bf16[48,2048]{1,0:T(8,128)(2,1)S(1)} %collective-permute-done.1), channel_id=1, source_target_pairs={{0,4},{4,0},{1,5},{5,1},{2,6},{6,2},{3,7},{7,3},{8,12},{12,8},{9,1... | collective-permute-start | bytes 589832 | tf_op jit(solution)/shard_map/ppermute | solution.py:39
  35.9 1.4 collective-permute-start.6
  37.9 2.4 copy-start.4
  38.7 1.6 copy-start.25
  40.3 1.7 copy-start.13
  40.3 1.7 copy-start.22
  42.2 1.8 collective-permute-start.7
  45.1 22.6 %all-to-all-start.1 = ((bf16[32,48,128]{2,1,0:T(8,128)(2,1)}), bf16[32,48,128]{2,1,0:T(8,128)(2,1)S(1)}, u32[]{:S(2)}, u32[]{:S(2)}) async-start(bf16[32,48,128]{2,1,0:T(8,128)(2,1)} %bitcast.248), calls=%async_computation.1 | async-start | bytes 786432 | tf_op jit(solution)/shard_map/all_to_all | solution.py:43
  68.8 0.7 collective-permute-start.8
  70.3 22.8 %copy-start.10 = (bf16[256,2048]{1,0:T(8,128)(2,1)S(1)}, bf16[256,2048]{1,0:T(8,128)(2,1)}, u32[]{:S(2)}) copy-start(bf16[256,2048]{1,0:T(8,128)(2,1)} %copy-done.9) | copy-start | bytes 3145732
  70.3 22.8 %copy-start.14 = (f32[96,512]{1,0:T(8,128)S(1)}, f32[96,512]{1,0:T(8,128)}, u32[]{:S(2)}) copy-start(f32[96,512]{1,0:T(8,128)} %copy-done.13) | copy-start | bytes 589828
  70.3 22.8 %copy-start.35 = (f32[96,256]{1,0:T(8,128)S(1)}, f32[96,256]{1,0:T(8,128)}, u32[]{:S(2)}) copy-start(f32[96,256]{1,0:T(8,128)} %get-tuple-element.62) | copy-start | bytes 294916
  88.1 4.9 %collective-permute-start.9 = (bf16[32,48,128]{2,1,0:T(8,128)(2,1)S(1)}, bf16[32,48,128]{2,1,0:T(8,128)(2,1)S(1)}, u32[]{:S(2)}, u32[]{:S(2)}) collective-permute-start(bf16[32,48,128]{2,1,0:T(8,128)(2,1)S(1)} %all_to_all.45), channel_id=1, source_target_pairs={{0,4},{4,0},{1,5},{5,1},{2,6},{6,2},{3,7},{7,3},{8,12},{12,8},{9,1... | collective-permute-start | bytes 1179656 | tf_op jit(solution)/shard_map/ppermute | solution.py:39
  93.1 1.1 copy-start.23
  93.7 1.6 copy-start.1
  94.3 1.8 collective-permute-start.10
  96.1 18.1 %copy-start.29 = (pred[48]{0:T(512)(128)(4,1)S(1)}, pred[48]{0:T(512)(128)(4,1)}, u32[]{:S(2)}) copy-start(pred[48]{0:T(512)(128)(4,1)} %iota_compare_fusion.6) | copy-start | bytes 148
  96.1 18.1 %copy-start.31 = (f32[128]{0:T(128)S(1)}, f32[128]{0:T(128)}, u32[]{:S(2)}) copy-start(f32[128]{0:T(128)} %fusion.157) | copy-start | bytes 1540
  96.1 18.1 %copy-start.33 = (f32[48]{0:T(128)S(1)}, f32[48]{0:T(128)}, u32[]{:S(2)}) copy-start(f32[48]{0:T(128)} %dynamic-slice.14) | copy-start | bytes 580
  115.1 0.7 collective-permute-start.11
  115.8 22.8 %copy-start.11 = (bf16[256,2048]{1,0:T(8,128)(2,1)S(1)}, bf16[256,2048]{1,0:T(8,128)(2,1)}, u32[]{:S(2)}) copy-start(bf16[256,2048]{1,0:T(8,128)(2,1)} %copy-done.9) | copy-start | bytes 3145732
  133.6 4.9 %collective-permute-start.12 = (bf16[32,48,128]{2,1,0:T(8,128)(2,1)S(1)}, bf16[32,48,128]{2,1,0:T(8,128)(2,1)S(1)}, u32[]{:S(2)}, u32[]{:S(2)}) collective-permute-start(bf16[32,48,128]{2,1,0:T(8,128)(2,1)S(1)} %all_to_all.47), channel_id=1, source_target_pairs={{0,4},{4,0},{1,5},{5,1},{2,6},{6,2},{3,7},{7,3},{8,12},{12,8},{9,1... | collective-permute-start | bytes 1179656 | tf_op jit(solution)/shard_map/ppermute | solution.py:39
  139.2 1.6 copy-start.2
  139.8 1.8 collective-permute-start.13
  160.6 10.2 %collective-permute-start.14 = (bf16[48,128]{1,0:T(8,128)(2,1)S(1)}, bf16[48,128]{1,0:T(8,128)(2,1)S(1)}, u32[]{:S(2)}, u32[]{:S(2)}) collective-permute-start(bf16[48,128]{1,0:T(8,128)(2,1)S(1)} %fusion.128), channel_id=1, source_target_pairs={{1,0},{5,4},{9,8},{13,12},{17,16},{21,20},{25,24},{29,28},{33,32},... | collective-permute-start | bytes 36872 | tf_op jit(solution)/shard_map/ppermute | solution.py:230
  170.8 0.6 copy-start.19
  188.1 5.8 %collective-permute-start.15 = (bf16[32,48,128]{2,1,0:T(8,128)(2,1)S(1)}, bf16[32,48,128]{2,1,0:T(8,128)(2,1)}, u32[]{:S(2)}, u32[]{:S(2)}) collective-permute-start(bf16[32,48,128]{2,1,0:T(8,128)(2,1)S(1)} %all_to_all.49), channel_id=1, source_target_pairs={{0,4},{4,0},{1,5},{5,1},{2,6},{6,2},{3,7},{7,3},{8,12},{12,8},{9,1... | collective-permute-start | bytes 1179656 | tf_op jit(solution)/shard_map/ppermute | solution.py:39
  192.4 2.6 %copy-start.12 = (bf16[256,2048]{1,0:T(8,128)(2,1)S(1)}, bf16[256,2048]{1,0:T(8,128)(2,1)}, u32[]{:S(2)}) copy-start(bf16[256,2048]{1,0:T(8,128)(2,1)} %copy-done.9) | copy-start | bytes 3145732
  192.4 2.6 %copy-start.15 = (f32[96,512]{1,0:T(8,128)S(1)}, f32[96,512]{1,0:T(8,128)}, u32[]{:S(2)}) copy-start(f32[96,512]{1,0:T(8,128)} %copy-done.13) | copy-start | bytes 589828
  192.4 2.6 %copy-start.36 = (f32[96,256]{1,0:T(8,128)S(1)}, f32[96,256]{1,0:T(8,128)}, u32[]{:S(2)}) copy-start(f32[96,256]{1,0:T(8,128)} %get-tuple-element.62) | copy-start | bytes 294916
  195.0 1.6 copy-start.3
  195.1 2.0 copy-start.5
  195.1 2.0 copy-start.26
  197.1 0.7 copy-start.24
  197.1 0.7 copy-start.28
  198.0 1.8 collective-permute-start.16
  200.9 17.9 %all-to-all-start.7 = ((bf16[32,48,128]{2,1,0:T(8,128)(2,1)}), bf16[32,48,128]{2,1,0:T(8,128)(2,1)S(1)}, u32[]{:S(2)}, u32[]{:S(2)}) async-start(bf16[32,48,128]{2,1,0:T(8,128)(2,1)} %bitcast.54), calls=%async_computation.7 | async-start | bytes 786432 | tf_op jit(solution)/shard_map/all_to_all | solution.py:43
  206.3 2.2 copy-start.16
  206.3 2.2 copy-start.17
  208.4 10.6 %copy-start.18 = (bf16[256,48]{1,0:T(8,128)(2,1)S(1)}, bf16[256,48]{1,0:T(8,128)(2,1)}, u32[]{:S(2)}) copy-start(bf16[256,48]{1,0:T(8,128)(2,1)} %fusion.93) | copy-start | bytes 73732
  208.4 10.6 %copy-start.20 = (bf16[48,128]{1,0:T(8,128)(2,1)S(1)}, bf16[48,128]{1,0:T(8,128)(2,1)}, u32[]{:S(2)}) copy-start(bf16[48,128]{1,0:T(8,128)(2,1)} %copy-done.19) | copy-start | bytes 36868
  208.4 10.6 %copy-start.30 = (pred[48]{0:T(512)(128)(4,1)S(1)}, pred[48]{0:T(512)(128)(4,1)}, u32[]{:S(2)}) copy-start(pred[48]{0:T(512)(128)(4,1)} %iota_compare_fusion.6) | copy-start | bytes 148
  208.4 10.6 %copy-start.32 = (f32[128]{0:T(128)S(1)}, f32[128]{0:T(128)}, u32[]{:S(2)}) copy-start(f32[128]{0:T(128)} %fusion.157) | copy-start | bytes 1540
  208.4 10.6 %copy-start.34 = (f32[48]{0:T(128)S(1)}, f32[48]{0:T(128)}, u32[]{:S(2)}) copy-start(f32[48]{0:T(128)} %dynamic-slice.14) | copy-start | bytes 580
  220.7 13.9 %all-to-all-start.8 = ((bf16[32,8,128]{2,1,0:T(8,128)(2,1)}), bf16[32,8,128]{2,1,0:T(8,128)(2,1)S(1)}, u32[]{:S(2)}, u32[]{:S(2)}) async-start(bf16[32,8,128]{2,1,0:T(8,128)(2,1)} %fusion.6), calls=%async_computation.8 | async-start | bytes 131072 | tf_op jit(solution)/shard_map/all_to_all | solution.py:43
  234.6 3.7 %collective-permute-start.17 = (bf16[8,2048]{1,0:T(8,128)(2,1)S(1)}, bf16[8,2048]{1,0:T(8,128)(2,1)S(1)}, u32[]{:S(2)}, u32[]{:S(2)}) collective-permute-start(bf16[8,2048]{1,0:T(8,128)(2,1)S(1)} %bitcast.283), channel_id=1, source_target_pairs={{0,4},{4,0},{1,5},{5,1},{2,6},{6,2},{3,7},{7,3},{8,12},{12,8},{9,1... | collective-permute-start | bytes 98312 | tf_op jit(solution)/shard_map/ppermute | solution.py:39
